TPU v7x, 32 devices: a whole 2x2x4 slice. The times are simulated.
32 devices in a mesh: block: 4 (over y, x), tok: 8 (over z, core).
Axes of the slice: x: 2, y: 2, z: 4, core: 2. Of those that a mesh axis runs over, the one named last changes fastest.
Arguments:
- queries: float32 [4096, 256], P(('block', 'tok')), may hold values from -6 to 6
- keys: float32 [4096, 256], P(('block', 'tok')), may hold values from -6 to 6
- values: float32 [4096, 256], P(('block', 'tok')), may hold values from -6 to 6
- rates: float32 [4096], P(('block', 'tok')), may hold values from 0.0001 to 0.001
- states: float32 [4, 3, 256, 256], P('block', None, 'tok'), may hold values from -0.375 to 0.375
- out_cot: float32 [4096, 256], P(('block', 'tok')), may hold values from -6 to 6
- final_cot: float32 [3, 256, 256], P(None, 'tok'), may hold values from -6 to 6
Outputs:
- d_queries: float32 [4096, 256], P(('block', 'tok'))
- d_keys: float32 [4096, 256], P(('block', 'tok'))
- d_values: float32 [4096, 256], P(('block', 'tok'))
- d_rates: float32 [4096], P(('block', 'tok'))
- d_states: float32 [4, 3, 256, 256], P('block', None, 'tok')
All inputs are finite; a program needn't handle non-finite values.
Results may differ from a plain program's by a relative error of at most 0.00029.
Values sent between devices are 32-bit elements; how exact they have to be, the bound alone decides.
No kernel may reach another device: no remote copies, remote signals or barrier semaphores. Data moves between devices by JAX's collectives and lax.ppermute only.
A program may use at most 64 MiB of HBM per device.

v0:
```python
import functools

import jax
import jax.numpy as jnp
from jax import lax
from jax.experimental import pallas as pl
from jax.experimental.pallas import tpu as pltpu
from jax.sharding import PartitionSpec as P


EPS = 1e-06
HIGH = lax.Precision.HIGHEST


def mm(left, right):
    return lax.dot_general(left, right, (((1,), (0,)), ((), ())), precision=HIGH, preferred_element_type=jnp.float32)


def mm_nt(left, right):
    return lax.dot_general(left, right, (((1,), (1,)), ((), ())), precision=HIGH, preferred_element_type=jnp.float32)


def mm_tn(left, right):
    return lax.dot_general(left, right, (((0,), (0,)), ((), ())), precision=HIGH, preferred_element_type=jnp.float32)


def silu_parts(first):
    sig = 1.0 / (1.0 + jnp.exp(-first))
    slope = sig * (1.0 - sig)
    value = first * sig
    d_one = sig + first * slope
    d_two = slope * (2.0 + first * (1.0 - 2.0 * sig))
    return value, d_one, d_two


def direct(size):
    return size % 2 == 0 and size <= 16


def chip_shift(array, by):
    size = lax.axis_size("tok")
    return lax.ppermute(array, "tok", [(j, (j + 2 * by) % size) for j in range(size)])


def core_swap(array):
    size = lax.axis_size("tok")
    return lax.ppermute(array, "tok", [(j, j ^ 1) for j in range(size)])


def gather_pieces(array):
    size = lax.axis_size("tok")
    if not direct(size):
        return lax.all_gather(array, "tok")
    mine = jnp.stack([array] + [chip_shift(array, by) for by in range(1, size // 2)])
    return jnp.concatenate([mine, core_swap(mine)])


def spread_sum(pieces):
    size = lax.axis_size("tok")
    if not direct(size):
        return lax.psum_scatter(pieces, "tok")
    half = size // 2
    mine = pieces[:half] + core_swap(pieces[half:])
    total = mine[0]
    for by in range(1, half):
        total = total + chip_shift(mine[by], -by)
    return total


def sum_all(array):
    size = lax.axis_size("tok")
    if not direct(size):
        return jnp.sum(lax.all_gather(array, "tok"), axis=0)
    array = array + core_swap(array)
    total = array
    for by in range(1, size // 2):
        total = total + chip_shift(array, by)
    return total


def rows_to_hidden(rows):
    size = lax.axis_size("tok")
    count, depth, width = rows.shape
    parts = rows.reshape(count, depth, size, width // size).transpose(2, 0, 3, 1)
    parts = lax.all_to_all(parts, "tok", 0, 0)
    return parts.transpose(1, 2, 0, 3).reshape(count, width // size, depth * size)


def hidden_to_rows(slices):
    size = lax.axis_size("tok")
    count, depth, width = slices.shape
    parts = slices.reshape(count, depth, size, width // size).transpose(2, 0, 1, 3)
    parts = lax.all_to_all(parts, "tok", 0, 0)
    return parts.transpose(1, 3, 0, 2).reshape(count, width // size, depth * size)


def to_block(array, source, target, by=0):
    size = lax.axis_size("tok")
    pairs = [(source * size + j, target * size + (j + by) % size) for j in range(size)]
    return lax.ppermute(array, ("block", "tok"), pairs)


def up_one(array):
    groups = lax.axis_size("block")
    return lax.ppermute(array, "block", [(i, i + 1) for i in range(groups - 1)])


def slice_forward(weights, keys, scaled):
    first, gate = mm_nt(weights[0], keys), mm_nt(weights[1], keys)
    value, d_one, d_two = silu_parts(first)
    d_mixed = mm_nt(weights[2], scaled)
    mixed = value * gate
    d_gate = d_mixed * value
    d_first = d_mixed * gate * d_one
    grads = jnp.stack([mm(d_first, keys), mm(d_gate, keys), mm(mixed, scaled)])
    return grads, (gate, value, d_one, d_two, d_mixed)


def slice_adjoint(cot, kept, keys, scaled):
    gate, value, d_one, d_two, d_mixed = kept
    t_first, t_gate, p_mixed = mm_nt(cot[0], keys), mm_nt(cot[1], keys), mm_nt(cot[2], scaled)
    t_mixed = d_one * t_first * gate + value * t_gate
    c_gate = p_mixed * value + d_mixed * d_one * t_first
    c_first = p_mixed * gate * d_one + d_mixed * (d_two * t_first * gate + d_one * t_gate)
    return jnp.stack([mm(c_first, keys), mm(c_gate, keys), mm(t_mixed, scaled)])


def query_adjoint(weights, queries, out_cot):
    first, gate = mm_nt(queries, weights[0]), mm_nt(queries, weights[1])
    value, d_one, _ = silu_parts(first)
    d_mixed = mm_nt(out_cot, weights[2])
    d_gate = d_mixed * value
    d_first = d_mixed * gate * d_one
    d_queries = mm(d_first, weights[0]) + mm(d_gate, weights[1])
    d_weights = jnp.stack([mm_tn(d_first, queries), mm_tn(d_gate, queries), mm_tn(value * gate, out_cot)])
    return d_queries, d_weights


def token_adjoint(weights, cot, keys, scaled):
    first, gate = mm_nt(keys, weights[0]), mm_nt(keys, weights[1])
    value, d_one, d_two = silu_parts(first)
    d_mixed = mm_nt(scaled, weights[2])
    mixed = value * gate
    d_gate = d_mixed * value
    d_first = d_mixed * gate * d_one
    t_first, t_gate, p_mixed = mm_nt(keys, cot[0]), mm_nt(keys, cot[1]), mm_nt(scaled, cot[2])
    t_mixed = d_one * t_first * gate + value * t_gate
    c_gate = p_mixed * value + d_mixed * d_one * t_first
    c_first = p_mixed * gate * d_one + d_mixed * (d_two * t_first * gate + d_one * t_gate)
    d_keys = mm(c_first, weights[0]) + mm(c_gate, weights[1]) + mm(d_first, cot[0]) + mm(d_gate, cot[1])
    t_out = mm(t_mixed, weights[2]) + mm(mixed, cot[2])
    return d_keys, t_out


def over_hidden(array):
    return jnp.sum(array[:2], axis=1)


def per_device_general(queries, keys, values, rates, states, out_cot, final_cot):
    groups, size = lax.axis_size("block"), lax.axis_size("tok")
    position = lax.axis_index("block")
    own_rows = states[0]
    scaled = -rates[:, None] * values
    both = gather_pieces(jnp.stack([keys, scaled]))
    width = keys.shape[1]
    all_keys = both[:, 0].reshape(-1, width)
    all_scaled = both[:, 1].reshape(-1, width)
    split = rows_to_hidden(jnp.concatenate([own_rows[:2], final_cot[:2]]))
    own = jnp.concatenate([split[:2], own_rows[2:]])
    last = jnp.concatenate([split[2:], final_cot[2:]])
    grads, kept = slice_forward(own, all_keys, all_scaled)
    shifted = own - grads
    earlier = up_one(shifted[:2])
    sums = sum_all(jnp.concatenate([over_hidden(own * own), over_hidden(shifted * shifted), over_hidden(last * shifted)]))
    row_norm = [jnp.sqrt(sums[0:2, None, :] + EPS), jnp.sqrt(jnp.sum(own[2:] ** 2, axis=-1, keepdims=True) + EPS)]
    new_norm = [jnp.sqrt(sums[2:4, None, :] + EPS), jnp.sqrt(jnp.sum(shifted[2:] ** 2, axis=-1, keepdims=True) + EPS)]

    pieces = gather_pieces(own)
    whole = pieces.transpose(1, 0, 2, 3).reshape(3, -1, width)
    d_queries, d_weights = query_adjoint(whole, queries, out_cot)
    apply_state = spread_sum(d_weights.reshape(3, size, -1, width).transpose(1, 0, 2, 3))

    is_last = position == groups - 1
    incoming = jnp.where(is_last, last, 0.0)
    inner = jnp.where(is_last, sums[4:6], 0.0)
    for section in range(groups):
        inners = [inner[:, None, :], jnp.sum(incoming[2:] * shifted[2:], axis=-1, keepdims=True)]
        cots, straights = [], []
        for part, dot, old, new in zip((slice(0, 2), slice(2, 3)), inners, row_norm, new_norm):
            d_shifted = old / new * incoming[part] - old * dot / (new * new * new) * shifted[part]
            cots.append(-d_shifted)
            straights.append(d_shifted + dot / new * own[part] / old)
        cot = jnp.concatenate(cots)
        straight = jnp.concatenate(straights)
        rows_now = slice_adjoint(cot, kept, all_keys, all_scaled) + apply_state + straight
        if section + 1 < groups:
            source = groups - 1 - section
            partial = over_hidden(rows_now[:2] * earlier)
            incoming = incoming + to_block(rows_now, source, source - 1)
            if direct(size):
                for by in range(size):
                    inner = inner + to_block(partial, source, source - 1, by)
            else:
                inner = inner + to_block(sum_all(partial), source, source - 1)
    cot_pieces = gather_pieces(cot)
    whole_cot = cot_pieces.transpose(1, 0, 2, 3).reshape(3, -1, width)
    d_keys, t_out = token_adjoint(whole, whole_cot, keys, scaled)
    d_values = -rates[:, None] * t_out
    d_rates = -jnp.sum(values * t_out, axis=-1)
    d_rows = jnp.concatenate([hidden_to_rows(rows_now[:2]), rows_now[2:]])
    return (d_queries, d_keys, d_values, d_rates, d_rows[None])


def halves(array):
    upper = array.astype(jnp.bfloat16)
    return upper, (array - upper.astype(jnp.float32)).astype(jnp.bfloat16)


def product(left, right, contract):
    def one(a, b):
        return lax.dot_general(a, b, (((1,), (contract,)), ((), ())), preferred_element_type=jnp.float32)

    return one(left[0], right[0]) + (one(left[0], right[1]) + one(left[1], right[0]))


def nn(left, right):
    return product(left, right, 0)


def nt(left, right):
    return product(left, right, 1)


def kernel_call(body, outs, *operands, scratch=(), raw=False, spill=False, limit=24 * 1024 * 1024):
    space = pltpu.MemorySpace.HBM if raw else pltpu.VMEM
    return pl.pallas_call(
        body,
        in_specs=[pl.BlockSpec(memory_space=space) for _ in operands],
        out_specs=[pl.BlockSpec(memory_space=pltpu.VMEM) for _ in outs],
        out_shape=[(jax.ShapeDtypeStruct if spill else pltpu.VMEM)(shape, dtype) for shape, dtype in outs],
        scratch_shapes=list(scratch),
        compiler_params=pltpu.CompilerParams(vmem_limit_bytes=limit),
    )(*operands)


def my_chip():
    return lax.div(lax.axis_index("tok"), 2)


def my_core():
    return lax.rem(lax.axis_index("tok"), 2)


def in_chain():
    return (my_chip() == LOW) | (my_chip() == HIGH_CHIP)


def f32(*shape):
    return shape, jnp.float32


def bf16(*shape):
    return shape, jnp.bfloat16


def column(row, width):
    block = jnp.broadcast_to(row, (128, row.shape[1])).T
    return jnp.concatenate([block] * (width // 128), axis=1)


CHIPS = 4
LOW, HIGH_CHIP = 1, 2
CHUNK = 256
PACK_LIMIT = 61 * 1024 * 1024


def rows_at(start, count):
    return pl.ds(pl.multiple_of(start, count), count)


def pack_body(*refs):
    count = 7
    sources, outs = refs[:count], refs[count : count + CHIPS + 1]
    buffers, sems = refs[count + CHIPS + 1 : -1], refs[-1]
    copies = [pltpu.make_async_copy(a, b, sems.at[i]) for i, (a, b) in enumerate(zip(sources, buffers))]
    for copy in copies:
        copy.start()
    for copy in copies:
        copy.wait()
    keys, values, rates, rows, final, queries, cot = buffers
    packs, ahead = outs[:CHIPS], outs[CHIPS]
    tokens = keys.shape[0]
    depth = rows.shape[1]
    scaled = -column(rates[...], values.shape[1]) * values[...]
    sides = []
    for side in range(2):
        parts = []
        for core in range(2):
            lanes = []
            for source in (rows, final):
                for m in range(2):
                    for i in range(2):
                        start = (4 * side + 2 * i + core) * depth
                        lanes.append(source[m, :, start : start + depth])
            parts.append(jnp.concatenate(lanes, axis=1))
        sides.append(jnp.concatenate(parts))
    for by, pack in enumerate(packs):
        pack[:tokens] = keys[...]
        pack[tokens : 2 * tokens] = scaled
        low = jnp.bitwise_xor(my_chip(), by) == LOW
        pack[2 * tokens : 2 * tokens + 2 * depth] = jnp.where(low, sides[0], sides[1])
        if by < 2:
            pack[2 * tokens + 2 * depth : 2 * tokens + 3 * depth] = rows[2]
            pack[2 * tokens + 3 * depth :] = final[2]
    ahead[:tokens] = queries[...]
    ahead[tokens:] = cot[...]


def unpack(packs, mates, own, last, table):
    depth = own.shape[1] // 2
    base = packs[0].shape[0] - 4 * depth
    span = own.shape[1]
    chip, core = my_chip(), my_core()
    for by in range(CHIPS):
        source = jnp.bitwise_xor(chip, by)
        mine = rows_at(base + core * depth, depth)
        table[rows_at((2 * source + core) * depth, depth), :] = packs[by][mine, :]
        table[rows_at((2 * source + 1 - core) * depth, depth), :] = mates[by][mine, :]
    turned = table[...].T
    keep = jnp.where(lax.axis_index("block") == lax.axis_size("block") - 1, 1.0, 0.0)
    own[0], own[1] = turned[:span], turned[span : 2 * span]
    last[0], last[1] = turned[2 * span : 3 * span] * keep, turned[3 * span :] * keep
    low = chip == LOW
    for place, out, scale in ((2 * depth, own, 1.0), (3 * depth, last, keep)):
        cut = slice(base + place, base + place + depth)
        out[2, :depth] = jnp.where(low, packs[1][cut, :], packs[0][cut, :]) * scale
        out[2, depth:] = jnp.where(low, packs[0][cut, :], packs[1][cut, :]) * scale


def forward_body(*refs):
    packs, mates = refs[:CHIPS], refs[CHIPS : 2 * CHIPS]
    own, last, key_high, key_low, scaled_high, scaled_low, kept, shifted, sums, table = refs[2 * CHIPS :]
    pieces = packs + mates
    depth = key_high.shape[0] // len(pieces)
    span = own.shape[1]

    @pl.when(~in_chain())
    def _():
        for out in (own, shifted, sums):
            out[...] = jnp.zeros(out.shape, jnp.float32)

    @pl.when(in_chain())
    def _():
        unpack(packs, mates, own, last, table)
        for index, piece in enumerate(pieces):
            cut = slice(index * depth, (index + 1) * depth)
            key_high[cut, :], key_low[cut, :] = halves(piece[:depth, :])
            scaled_high[cut, :], scaled_low[cut, :] = halves(piece[depth : 2 * depth, :])
        pair = halves(jnp.concatenate([own[0], own[1]]))
        second = halves(own[2])
        grad_pair, grad_second = 0.0, 0.0
        for start in range(0, key_high.shape[0], CHUNK):
            cut = slice(start, start + CHUNK)
            key_cut = key_high[cut, :], key_low[cut, :]
            scaled_cut = scaled_high[cut, :], scaled_low[cut, :]
            both = nt(pair, key_cut)
            d_mixed = nt(second, scaled_cut)
            first, gate = both[:span], both[span:]
            value, d_one, d_two = silu_parts(first)
            for place, array in enumerate((gate, value, d_one, d_two, d_mixed)):
                kept[place, :, cut] = array
            d_pair = jnp.concatenate([d_mixed * gate * d_one, d_mixed * value])
            grad_pair += nn(halves(d_pair), key_cut)
            grad_second += nn(halves(value * gate), scaled_cut)
        moved = own[0] - grad_pair[:span], own[1] - grad_pair[span:], own[2] - grad_second
        rows = []
        for left, right in ((own, own), (moved, moved), (last, moved)):
            rows += [jnp.sum(left[m] * right[m], axis=0, keepdims=True) for m in range(2)]
        sums[...] = jnp.concatenate(rows + [jnp.zeros((2, own.shape[2]), jnp.float32)])
        for m in range(3):
            shifted[m] = moved[m]


def apply_body(source, own, raw, earlier, *refs):
    pieces, (applied, payload, partial) = refs[:-3], refs[-3:]
    span = own.shape[1]
    depth = pieces[0].shape[0] // 2
    active = (lax.axis_index("block") == source) & in_chain()

    @pl.when(~active)
    def _():
        payload[...] = jnp.zeros(payload.shape, jnp.float32)
        partial[...] = jnp.zeros(partial.shape, jnp.float32)

    @pl.when(in_chain())
    def _():
        pair = halves(jnp.concatenate([own[0], own[1]]))
        second = halves(own[2])
        out_pair, out_second = 0.0, 0.0
        for index in range(0, len(pieces), 2):
            one, two = pieces[index], pieces[index + 1]
            query = halves(jnp.concatenate([one[:depth, :], two[:depth, :]]))
            cot = halves(jnp.concatenate([one[depth:, :], two[depth:, :]]))
            both = nt(pair, query)
            d_mixed = nt(second, cot)
            first, gate = both[:span], both[span:]
            value, d_one, _ = silu_parts(first)
            out_pair += nn(halves(jnp.concatenate([d_mixed * gate * d_one, d_mixed * value])), query)
            out_second += nn(halves(value * gate), cot)
        applied[: 2 * span] = out_pair
        applied[2 * span :] = out_second

    @pl.when(active)
    def _():
        rows = [raw[m] + applied[m * span : (m + 1) * span, :] for m in range(3)]
        finish(rows, earlier, payload, partial)


def finish(rows, earlier, payload, partial):
    sums = [jnp.sum(rows[m] * earlier[m], axis=0, keepdims=True) for m in range(2)]
    partial[...] = jnp.concatenate(sums + [jnp.zeros((6, rows[0].shape[1]), jnp.float32)])
    for m in range(3):
        payload[m] = rows[m]


def state_terms(own, shifted, last, sums, inners, arrived):
    total = sums[0][...] + sums[1][...] + (sums[2][...] + sums[3][...])
    inner = total[4:6]
    for array in inners:
        inner = inner + array[0:2]
    cots, straights = [], []
    for m in range(3):
        incoming = last[m]
        for array in arrived:
            incoming = incoming + array[m]
        if m < 2:
            dot, old, new = inner[m : m + 1], jnp.sqrt(total[m : m + 1] + EPS), jnp.sqrt(total[m + 2 : m + 3] + EPS)
        else:
            dot = jnp.sum(incoming * shifted[m], axis=-1, keepdims=True)
            old = jnp.sqrt(jnp.sum(own[m] * own[m], axis=-1, keepdims=True) + EPS)
            new = jnp.sqrt(jnp.sum(shifted[m] * shifted[m], axis=-1, keepdims=True) + EPS)
        d_shifted = old / new * incoming - old * dot / (new * new * new) * shifted[m]
        cots.append(-d_shifted)
        straights.append(d_shifted + dot / new * own[m] / old)
    return cots, straights


def section_rows(count, refs):
    own, shifted, last = refs[:3]
    sums, inners, arrived = refs[3:7], refs[7 : 7 + 4 * count], refs[7 + 4 * count : 7 + 5 * count]
    key_high, key_low, scaled_high, scaled_low, kept = refs[7 + 5 * count : 12 + 5 * count]
    span = own.shape[1]
    cots, straights = state_terms(own, shifted, last, sums, inners, arrived)
    pair = halves(jnp.concatenate(cots[:2]))
    second = halves(cots[2])
    d_pair, d_second = 0.0, 0.0
    for start in range(0, key_high.shape[0], CHUNK):
        cut = slice(start, start + CHUNK)
        key_cut = key_high[cut, :], key_low[cut, :]
        scaled_cut = scaled_high[cut, :], scaled_low[cut, :]
        gate, value, d_one, d_two, d_mixed = [kept[place, :, cut] for place in range(5)]
        both = nt(pair, key_cut)
        p_mixed = nt(second, scaled_cut)
        t_first, t_gate = both[:span], both[span:]
        lift = d_one * t_first
        t_mixed = lift * gate + value * t_gate
        c_gate = p_mixed * value + d_mixed * lift
        c_first = p_mixed * gate * d_one + d_mixed * (d_two * t_first * gate + d_one * t_gate)
        d_pair += nn(halves(jnp.concatenate([c_first, c_gate])), key_cut)
        d_second += nn(halves(t_mixed), scaled_cut)
    return [d_pair[:span] + straights[0], d_pair[span:] + straights[1], d_second + straights[2]]


def first_body(source, *refs):
    raw = refs[-1]

    @pl.when((lax.axis_index("block") == source) & in_chain())
    def _():
        rows = section_rows(0, refs)
        for m in range(3):
            raw[m] = rows[m]


def section_body(source, *refs):
    applied, earlier, payload, partial = refs[-4:]
    active = (lax.axis_index("block") == source) & in_chain()

    @pl.when(~active)
    def _():
        payload[...] = jnp.zeros(payload.shape, jnp.float32)
        partial[...] = jnp.zeros(partial.shape, jnp.float32)

    @pl.when(active)
    def _():
        span = payload.shape[1]
        rows = section_rows(1, refs)
        finish([row + applied[m * span : (m + 1) * span, :] for m, row in enumerate(rows)], earlier, payload, partial)


def terms_body(count, *refs):
    cot = refs[-1]
    span = refs[0].shape[1]

    @pl.when(~in_chain())
    def _():
        cot[...] = jnp.zeros(cot.shape, jnp.float32)

    @pl.when(in_chain())
    def _():
        cots, _ = state_terms(*refs[:3], refs[3:7], refs[7 : 7 + 4 * count], refs[7 + 4 * count : 7 + 5 * count])
        for m in range(3):
            cot[m * span : (m + 1) * span, :] = cots[m]


def final_body(count, *refs):
    applied, outs, table = refs[-6], refs[-5:-1], refs[-1]
    span = refs[0].shape[1]
    depth = span // 2
    chip = my_chip()

    @pl.when(~in_chain())
    def _():
        for out in outs:
            out[...] = jnp.zeros(out.shape, jnp.float32)

    @pl.when(in_chain())
    def _():
        rows = [row + applied[m * span : (m + 1) * span, :] for m, row in enumerate(section_rows(count, refs))]
        table[...] = jnp.concatenate(rows[:2]).T
        low = chip == LOW
        upper, lower = rows[2][:depth], rows[2][depth:]
        picks = jnp.where(low, lower, upper), jnp.where(low, upper, lower), upper, upper
        for by, (out, pick) in enumerate(zip(outs, picks)):
            start = rows_at(jnp.bitwise_xor(chip, by) * 2 * depth, 2 * depth)
            out[:, :128] = table[start, :]
            out[:depth, 128:] = pick[:, :128]
            out[depth:, 128:] = pick[:, 128:]


def joined(refs):
    return [[refs[i], refs[i + 1]] for i in range(0, 8, 2)]


def taken(pair, cut):
    return pair[0][cut, :] + pair[1][cut, :]


def load_halves(pieces, part, span):
    return halves(jnp.concatenate([taken(pair, slice(part * span, (part + 1) * span)) for pair in pieces]))


def query_body(queries, out_cot, *refs):
    pieces, d_queries = joined(refs[:8]), refs[8]
    span = queries.shape[1] // len(pieces)
    one, three, two = [load_halves(pieces, part, span) for part in range(3)]
    query, cot = halves(queries[...]), halves(out_cot[...])
    first, gate = nt(query, one), nt(query, three)
    value, d_one, _ = silu_parts(first)
    d_mixed = nt(cot, two)
    d_gate = d_mixed * value
    d_first = d_mixed * gate * d_one
    d_queries[...] = nn(halves(d_first), one) + nn(halves(d_gate), three)


def token_body(keys, values, rates, *refs):
    weights, cots = joined(refs[:8]), joined(refs[8:16])
    d_keys, d_values, d_rates, d_rows = refs[24:]
    width = keys.shape[1]
    span = width // len(weights)
    one, three, two = [load_halves(weights, part, span) for part in range(3)]
    c_one, c_three, c_two = [load_halves(cots, part, span) for part in range(3)]
    ends = [taken(pair, slice(None)) for pair in joined(refs[16:24])]
    rate = column(rates[...], width)
    key, scaled = halves(keys[...]), halves(-rate * values[...])
    first, gate = nt(key, one), nt(key, three)
    value, d_one, d_two = silu_parts(first)
    d_mixed = nt(scaled, two)
    t_first, t_gate, p_mixed = nt(key, c_one), nt(key, c_three), nt(scaled, c_two)
    mixed = value * gate
    d_gate = d_mixed * value
    d_first = d_mixed * gate * d_one
    lift = d_one * t_first
    t_mixed = lift * gate + value * t_gate
    c_gate = p_mixed * value + d_mixed * lift
    c_first = p_mixed * gate * d_one + d_mixed * (d_two * t_first * gate + d_one * t_gate)
    d_keys[...] = nn(halves(c_first), one) + nn(halves(c_gate), three) + nn(halves(d_first), c_one) + nn(halves(d_gate), c_three)
    t_out = nn(halves(t_mixed), two) + nn(halves(mixed), c_two)
    d_values[...] = -rate * t_out
    d_rates[...] = -jnp.sum((values[...] * t_out).T, axis=0, keepdims=True)
    depth = d_rows.shape[1]
    low_side, upper_core = my_chip() <= LOW, my_core() == 0
    sides = []
    for near, far in ((ends[0], ends[1]), (ends[2], ends[3])):
        pair = jnp.where(low_side, near, far), jnp.where(low_side, far, near)
        sides.append([jnp.where(upper_core, piece[:depth], piece[depth:]) for piece in pair])
    by_core = [[jnp.where(upper_core, a, b) for a, b in zip(*sides)], [jnp.where(upper_core, b, a) for a, b in zip(*sides)]]
    for m in range(2):
        parts = []
        for side in range(2):
            for i in range(2):
                for core in range(2):
                    start = (2 * m + i) * depth
                    parts.append(by_core[core][side][:, start : start + depth])
        d_rows[m] = jnp.concatenate(parts, axis=1)
    d_rows[2] = jnp.concatenate([ends[0][:depth, 128:], ends[0][depth:, 128:]], axis=1)


def by_xor(array, by, chips):
    return lax.ppermute(array, "tok", [(2 * a + core, 2 * (a ^ by) + core) for a in chips for core in range(2)])


def both_cores(pieces):
    swapped = [core_swap(pieces[0])]
    return pieces + swapped + [core_swap(piece) for piece in pieces[1:]]


def hops(arrays, near, far, across):
    first = by_xor(arrays[1], 1, near)
    second = by_xor(arrays[2], 2, far)
    third = by_xor(arrays[3], 3, across)
    return first, second, third


ALL, MIDDLE, OUTER = tuple(range(CHIPS)), (LOW, HIGH_CHIP), (0, CHIPS - 1)


def to_chain(arrays):
    return both_cores([arrays[0], *hops(arrays, ALL, OUTER, MIDDLE)])


def from_chain(arrays, whole):
    near, far, across = hops(arrays, ALL, ALL if whole else MIDDLE, ALL if whole else MIDDLE)
    return both_cores([arrays[0], near, across, far])


def to_earlier(array):
    groups = lax.axis_size("block")
    return lax.ppermute(array, "block", [(i, (i - 1) % groups) for i in range(groups)])


def chain_to_block(array, source, target, by):
    size = lax.axis_size("tok")
    places = [(chip, core) for chip in (LOW, HIGH_CHIP) for core in range(2)]
    return lax.ppermute(
        array,
        ("block", "tok"),
        [(source * size + 2 * chip + core, target * size + 2 * (chip ^ by) + core) for chip, core in places],
    )


def to_later(array):
    groups = lax.axis_size("block")
    return lax.ppermute(array, "block", [(i, (i + 1) % groups) for i in range(groups)])


def per_device(queries, keys, values, rates, states, out_cot, final_cot):
    groups, size = lax.axis_size("block"), lax.axis_size("tok")
    depth, width = keys.shape
    own_rows = states[0]
    rows = own_rows.shape[1]
    if not (size == 2 * CHIPS and 4 * rows == 128 and depth == 128 and width == 8 * rows):
        return per_device_general(queries, keys, values, rates, states, out_cot, final_cot)
    span, tokens = 2 * rows, depth * size
    rates_row = rates.reshape(1, depth)
    state, square, wide = f32(3, span, width), f32(depth, width), f32(3 * span, width)
    sources = (keys, values, rates_row, own_rows, final_cot, queries, out_cot)
    longer, shorter = f32(2 * depth + 4 * rows, width), f32(2 * depth + 2 * rows, width)
    *packs, ahead = kernel_call(
        pack_body,
        [longer, longer, shorter, shorter, f32(2 * depth, width)],
        *sources,
        scratch=[pltpu.VMEM(array.shape, array.dtype) for array in sources] + [pltpu.SemaphoreType.DMA((len(sources),))],
        raw=True,
        limit=PACK_LIMIT,
    )
    pieces = to_chain(packs)
    ahead_pieces = to_chain([ahead] * CHIPS)
    half = bf16(tokens, width)
    own, last, *halved, kept, shifted, sums = kernel_call(
        forward_body,
        [state, state, half, half, half, half, f32(5, span, tokens), state, f32(8, width)],
        *pieces,
        scratch=[pltpu.VMEM((width, 4 * span), jnp.float32)],
    )
    across = by_xor(sums, 3, ALL)
    all_sums = [sums, core_swap(sums), across, core_swap(across)]
    earlier = to_later(shifted)
    weights = from_chain([own.reshape(3 * span, width)] * CHIPS, False)

    inners, arrived = [], []
    common = [own, shifted, last, *all_sums]
    sent = [state, f32(8, width)]
    (raw,) = kernel_call(functools.partial(first_body, groups - 1), [state], *common, *halved, kept)
    for section in range(groups - 1):
        source = groups - 1 - section
        if section == 0:
            body = functools.partial(apply_body, source)
            applied, payload, partial = kernel_call(body, [wide] + sent, own, raw, earlier, *ahead_pieces)
        else:
            body = functools.partial(section_body, source)
            payload, partial = kernel_call(
                body, sent, *common, *inners[-4:], *arrived[-1:], *halved, kept, applied, earlier
            )
        cross = chain_to_block(partial, source, source - 1, 3)
        straight = to_earlier(partial)
        arrived.append(to_earlier(payload))
        inners += [straight, cross, core_swap(straight), core_swap(cross)]
    received = [*common, *inners, *arrived]
    (cot,) = kernel_call(functools.partial(terms_body, groups - 1), [wide], *received)
    cots = from_chain([cot] * CHIPS, False)
    ends = kernel_call(
        functools.partial(final_body, groups - 1),
        [f32(2 * rows, width)] * CHIPS,
        *received,
        *halved,
        kept,
        applied,
        scratch=[pltpu.VMEM((width, 128), jnp.float32)],
    )
    end_pieces = from_chain(ends, True)
    (d_queries,) = kernel_call(query_body, [square], queries, out_cot, *weights, spill=True)
    d_keys, d_values, d_rates, d_rows = kernel_call(
        token_body,
        [square, square, f32(1, depth), f32(3, rows, width)],
        keys,
        values,
        rates_row,
        *weights,
        *cots,
        *end_pieces,
        spill=True,
    )
    return (d_queries, d_keys, d_values, d_rates.reshape(depth), d_rows[None])


def solution(mesh):
    return jax.shard_map(
        per_device,
        mesh=mesh,
        in_specs=(
            P(("block", "tok"), None),
            P(("block", "tok"), None),
            P(("block", "tok"), None),
            P(("block", "tok")),
            P("block", None, "tok", None),
            P(("block", "tok"), None),
            P(None, "tok", None),
        ),
        out_specs=(
            P(("block", "tok"), None),
            P(("block", "tok"), None),
            P(("block", "tok"), None),
            P(("block", "tok")),
            P("block", None, "tok", None),
        ),
        check_vma=False,
    )
```

profile of v0, /device:TPU:0, one launch (start us, length us, event | category | flops | bytes accessed | tf_op | source)
XLA Modules:
  0.0 131.4 jit_solution(6962987018621253797)
XLA Ops:
  0.6 1.5 %shard_map.110 = (f32[384,256]{1,0:T(8,128)S(1)}, f32[384,256]{1,0:T(8,128)S(1)}, f32[320,256]{1,0:T(8,128)S(1)}, f32[320,256]{1,0:T(8,128)S(1)}, f32[256,256]{1,0:T(8,128)S(1)}) custom-call(f32[128,256]{1,0:T(8,128)} %keys.1, f32[128,256]{1,0:T(8,128)} %values.1, f32[1,128]{1,0:T(1,128)} %bitcast.11, f32[3,32,256]{2,1,0:T(8,128)} %bitcast.13, ...), custom_call_target="tpu_custom_call" | custom-call | tf_op jit(solution)/shard_map/pallas_call | solution.py:236
  2.1 3.1 %collective-permute-start = (f32[384,256]{1,0:T(8,128)S(1)}, f32[384,256]{1,0:T(8,128)S(1)}, u32[]{:S(2)}, u32[]{:S(2)}) collective-permute-start(f32[384,256]{1,0:T(8,128)S(1)} %get-tuple-element.35), channel_id=1, source_target_pairs={{0,2},{1,3},{2,0},{3,1},{4,6},{5,7},{6,4},{7,5},{8,10},{9,11},{10,... | collective-permute-start | bytes 1179656 | tf_op jit(solution)/shard_map/ppermute | solution.py:609
  5.3 4.9 %collective-permute-start.1 = (f32[320,256]{1,0:T(8,128)S(1)}, f32[320,256]{1,0:T(8,128)S(1)}, u32[]{:S(2)}, u32[]{:S(2)}) collective-permute-start(f32[320,256]{1,0:T(8,128)S(1)} %get-tuple-element.36), channel_id=1, source_target_pairs={{0,4},{1,5},{6,2},{7,3},{8,12},{9,13},{14,10},{15,11},{16,20},{17,... | collective-permute-start | bytes 983048 | tf_op jit(solution)/shard_map/ppermute | solution.py:609
  10.9 3.0 %collective-permute-start.19 = (f32[256,256]{1,0:T(8,128)S(1)}, f32[256,256]{1,0:T(8,128)S(1)}, u32[]{:S(2)}, u32[]{:S(2)}) collective-permute-start(f32[256,256]{1,0:T(8,128)S(1)} %get-tuple-element.47.refs_0_), channel_id=1, source_target_pairs={{0,4},{1,5},{6,2},{7,3},{8,12},{9,13},{14,10},{15,11},{16,20},{17,... | collective-permute-start | bytes 786440 | tf_op jit(solution)/shard_map/ppermute | solution.py:609
  13.9 6.5 %collective-permute-done.18.refs_1_ = f32[256,256]{1,0:T(8,128)S(1)} collective-permute-done((f32[256,256]{1,0:T(8,128)S(1)}, f32[256,256]{1,0:T(8,128)S(1)}, u32[]{:S(2)}, u32[]{:S(2)}) %collective-permute-start.18) | collective-permute-done | bytes 262176 | tf_op jit(solution)/shard_map/ppermute | solution.py:609
  20.9 6.5 %collective-permute-done.1.refs_2_ = f32[320,256]{1,0:T(8,128)S(1)} collective-permute-done((f32[320,256]{1,0:T(8,128)S(1)}, f32[320,256]{1,0:T(8,128)S(1)}, u32[]{:S(2)}, u32[]{:S(2)}) %collective-permute-start.1) | collective-permute-done | bytes 327712 | tf_op jit(solution)/shard_map/ppermute | solution.py:609
  27.9 4.0 %collective-permute-done.19.refs_2_ = f32[256,256]{1,0:T(8,128)S(1)} collective-permute-done((f32[256,256]{1,0:T(8,128)S(1)}, f32[256,256]{1,0:T(8,128)S(1)}, u32[]{:S(2)}, u32[]{:S(2)}) %collective-permute-start.19) | collective-permute-done | bytes 262176 | tf_op jit(solution)/shard_map/ppermute | solution.py:609
  33.7 2.5 %collective-permute-start.15 = (f32[8,256]{1,0:T(8,128)S(1)}, f32[8,256]{1,0:T(8,128)S(1)}, u32[]{:S(2)}, u32[]{:S(2)}) collective-permute-start(f32[8,256]{1,0:T(8,128)S(1)} %get-tuple-element.41.refs_3_), channel_id=1, source_target_pairs={{0,6},{1,7},{2,4},{3,5},{4,2},{5,3},{6,0},{7,1},{8,14},{9,15},{10,... | collective-permute-start | bytes 24584 | tf_op jit(solution)/shard_map/ppermute | solution.py:609
  36.2 3.1 %collective-permute-done.15.refs_5_ = f32[8,256]{1,0:T(8,128)S(1)} collective-permute-done((f32[8,256]{1,0:T(8,128)S(1)}, f32[8,256]{1,0:T(8,128)S(1)}, u32[]{:S(2)}, u32[]{:S(2)}) %collective-permute-start.15) | collective-permute-done | bytes 8224 | tf_op jit(solution)/shard_map/ppermute | solution.py:609
  39.3 1.2 collective-permute-done.14.refs_4_
  41.7 1.5 %collective-permute-start.17 = (f32[3,64,256]{2,1,0:T(8,128)S(1)}, f32[3,64,256]{2,1,0:T(8,128)S(1)}, u32[]{:S(2)}, u32[]{:S(2)}) collective-permute-start(f32[3,64,256]{2,1,0:T(8,128)S(1)} %get-tuple-element.39.refs_1_), channel_id=1, source_target_pairs={{0,8},{8,16},{16,24},{24,0},{1,9},{9,17},{17,25},{25,1},{2,10},{10... | collective-permute-start | bytes 589832 | tf_op jit(solution)/shard_map/ppermute | solution.py:653
  43.2 6.4 %collective-permute-done.17.earlier.refs_18_ = f32[3,64,256]{2,1,0:T(8,128)S(1)} collective-permute-done((f32[3,64,256]{2,1,0:T(8,128)S(1)}, f32[3,64,256]{2,1,0:T(8,128)S(1)}, u32[]{:S(2)}, u32[]{:S(2)}) %collective-permute-start.17) | collective-permute-done | bytes 196640 | tf_op jit(solution)/shard_map/ppermute | solution.py:653
  49.6 1.6 %collective-permute-start.29 = (f32[3,64,256]{2,1,0:T(8,128)S(1)}, f32[3,64,256]{2,1,0:T(8,128)S(1)}, u32[]{:S(2)}, u32[]{:S(2)}) collective-permute-start(f32[3,64,256]{2,1,0:T(8,128)S(1)} %get-tuple-element.49), channel_id=1, source_target_pairs={{0,24},{8,0},{16,8},{24,16},{1,25},{9,1},{17,9},{25,17},{2,26},{10... | collective-permute-start | bytes 589832 | tf_op jit(solution)/shard_map/ppermute | solution.py:638
  51.2 1.4 %collective-permute-start.25 = (f32[8,256]{1,0:T(8,128)S(1)}, f32[8,256]{1,0:T(8,128)S(1)}, u32[]{:S(2)}, u32[]{:S(2)}) collective-permute-start(f32[8,256]{1,0:T(8,128)S(1)} %get-tuple-element.48), channel_id=1, source_target_pairs={{0,24},{8,0},{16,8},{24,16},{1,25},{9,1},{17,9},{25,17},{2,26},{10... | collective-permute-start | bytes 24584 | tf_op jit(solution)/shard_map/ppermute | solution.py:638
  53.3 2.7 %collective-permute-done.25.refs_7_ = f32[8,256]{1,0:T(8,128)S(1)} collective-permute-done((f32[8,256]{1,0:T(8,128)S(1)}, f32[8,256]{1,0:T(8,128)S(1)}, u32[]{:S(2)}, u32[]{:S(2)}) %collective-permute-start.25) | collective-permute-done | bytes 8224 | tf_op jit(solution)/shard_map/ppermute | solution.py:638
  57.3 2.5 %collective-permute-start.34 = (f32[3,64,256]{2,1,0:T(8,128)S(1)}, f32[3,64,256]{2,1,0:T(8,128)S(1)}, u32[]{:S(2)}, u32[]{:S(2)}) collective-permute-start(f32[3,64,256]{2,1,0:T(8,128)S(1)} %get-tuple-element.52), channel_id=1, source_target_pairs={{0,24},{8,0},{16,8},{24,16},{1,25},{9,1},{17,9},{25,17},{2,26},{10... | collective-permute-start | bytes 589832 | tf_op jit(solution)/shard_map/ppermute | solution.py:638
  59.8 14.3 %collective-permute-start.7 = (f32[192,256]{1,0:T(8,128)S(1)}, f32[192,256]{1,0:T(8,128)S(1)}, u32[]{:S(2)}, u32[]{:S(2)}) collective-permute-start(f32[192,256]{1,0:T(8,128)S(1)} %bitcast.5), channel_id=1, source_target_pairs={{0,2},{1,3},{2,0},{3,1},{4,6},{5,7},{6,4},{7,5},{8,10},{9,11},{10,... | collective-permute-start | bytes 589832 | tf_op jit(solution)/shard_map/ppermute | solution.py:609
  74.7 1.3 collective-permute-start.9
  76.0 4.6 %collective-permute-start.30 = (f32[8,256]{1,0:T(8,128)S(1)}, f32[8,256]{1,0:T(8,128)S(1)}, u32[]{:S(2)}, u32[]{:S(2)}) collective-permute-start(f32[8,256]{1,0:T(8,128)S(1)} %get-tuple-element.51), channel_id=1, source_target_pairs={{0,24},{8,0},{16,8},{24,16},{1,25},{9,1},{17,9},{25,17},{2,26},{10... | collective-permute-start | bytes 24584 | tf_op jit(solution)/shard_map/ppermute | solution.py:638
  80.6 1.4 %collective-permute-done.30.refs_7_.refs_11_ = f32[8,256]{1,0:T(8,128)S(1)} collective-permute-done((f32[8,256]{1,0:T(8,128)S(1)}, f32[8,256]{1,0:T(8,128)S(1)}, u32[]{:S(2)}, u32[]{:S(2)}) %collective-permute-start.30) | collective-permute-done | bytes 8224 | tf_op jit(solution)/shard_map/ppermute | solution.py:638
  82.7 1.2 collective-permute-done.32.refs_9_.refs_13_
  85.1 3.2 %collective-permute-start.39 = (f32[3,64,256]{2,1,0:T(8,128)S(1)}, f32[3,64,256]{2,1,0:T(8,128)S(1)}, u32[]{:S(2)}, u32[]{:S(2)}) collective-permute-start(f32[3,64,256]{2,1,0:T(8,128)S(1)} %get-tuple-element.54), channel_id=1, source_target_pairs={{0,24},{8,0},{16,8},{24,16},{1,25},{9,1},{17,9},{25,17},{2,26},{10... | collective-permute-start | bytes 589832 | tf_op jit(solution)/shard_map/ppermute | solution.py:638
  89.6 3.4 %collective-permute-done.35.refs_15_ = f32[8,256]{1,0:T(8,128)S(1)} collective-permute-done((f32[8,256]{1,0:T(8,128)S(1)}, f32[8,256]{1,0:T(8,128)S(1)}, u32[]{:S(2)}, u32[]{:S(2)}) %collective-permute-start.35) | collective-permute-done | bytes 8224 | tf_op jit(solution)/shard_map/ppermute | solution.py:638
  94.7 9.5 %collective-permute-start.40 = (f32[192,256]{1,0:T(8,128)S(1)}, f32[192,256]{1,0:T(8,128)S(1)}, u32[]{:S(2)}, u32[]{:S(2)}) collective-permute-start(f32[192,256]{1,0:T(8,128)S(1)} %shard_map.117.refs_8_), channel_id=1, source_target_pairs={{0,2},{1,3},{2,0},{3,1},{4,6},{5,7},{6,4},{7,5},{8,10},{9,11},{10,... | collective-permute-start | bytes 589832 | tf_op jit(solution)/shard_map/ppermute | solution.py:609
  104.9 1.3 collective-permute-start.42
  106.5 5.8 %collective-permute-start.47 = (f32[64,256]{1,0:T(8,128)S(1)}, f32[64,256]{1,0:T(8,128)S(1)}, u32[]{:S(2)}, u32[]{:S(2)}) collective-permute-start(f32[64,256]{1,0:T(8,128)S(1)} %get-tuple-element.56), channel_id=1, source_target_pairs={{0,2},{1,3},{2,0},{3,1},{4,6},{5,7},{6,4},{7,5},{8,10},{9,11},{10,... | collective-permute-start | bytes 196616 | tf_op jit(solution)/shard_map/ppermute | solution.py:609
  112.3 1.4 %collective-permute-start.48 = (f32[64,256]{1,0:T(8,128)S(1)}, f32[64,256]{1,0:T(8,128)S(1)}, u32[]{:S(2)}, u32[]{:S(2)}) collective-permute-start(f32[64,256]{1,0:T(8,128)S(1)} %get-tuple-element.57), channel_id=1, source_target_pairs={{0,6},{1,7},{2,4},{3,5},{4,2},{5,3},{6,0},{7,1},{8,14},{9,15},{10,... | collective-permute-start | bytes 196616 | tf_op jit(solution)/shard_map/ppermute | solution.py:609
  113.7 5.6 %collective-permute-done.47.refs_17_ = f32[64,256]{1,0:T(8,128)S(1)} collective-permute-done((f32[64,256]{1,0:T(8,128)S(1)}, f32[64,256]{1,0:T(8,128)S(1)}, u32[]{:S(2)}, u32[]{:S(2)}) %collective-permute-start.47) | collective-permute-done | bytes 65568 | tf_op jit(solution)/shard_map/ppermute | solution.py:609
  119.4 5.1 %collective-permute-done.49.refs_19_ = f32[64,256]{1,0:T(8,128)S(1)} collective-permute-done((f32[64,256]{1,0:T(8,128)S(1)}, f32[64,256]{1,0:T(8,128)S(1)}, u32[]{:S(2)}, u32[]{:S(2)}) %collective-permute-start.49) | collective-permute-done | bytes 65568 | tf_op jit(solution)/shard_map/ppermute | solution.py:609
  126.3 1.0 collective-permute-done.52.refs_22_
  127.6 1.5 %shard_map.112 = f32[128,256]{1,0:T(8,128)} custom-call(f32[128,256]{1,0:T(8,128)S(1)} %copy-done.2, f32[128,256]{1,0:T(8,128)S(1)} %copy-done.3, f32[192,256]{1,0:T(8,128)S(1)} %bitcast.9, f32[192,256]{1,0:T(8,128)S(1)} %collective-permute-done.7.refs_1_, f32[192,256]{1,0:T(8,128)S(1)} %collective-permute-done.8.refs_2_, ...), custom_call_target="tpu_custom_call" | custom-call | tf_op jit(solution)/shard_map/pallas_call | solution.py:236
  129.1 2.2 %shard_map.119 = (f32[128,256]{1,0:T(8,128)}, f32[128,256]{1,0:T(8,128)}, f32[1,128]{1,0:T(1,128)}, f32[3,32,256]{2,1,0:T(8,128)}) custom-call(f32[128,256]{1,0:T(8,128)S(1)} %copy-done, f32[128,256]{1,0:T(8,128)S(1)} %copy-done.1, f32[1,128]{1,0:T(1,128)S(1)} %bitcast.12, f32[192,256]{1,0:T(8,128)S(1)} %bitcast.10, ...), custom_call_target="tpu_custom_call" | custom-call | tf_op jit(solution)/shard_map/pallas_call | solution.py:236
  (96 shorter events, 15.3 us)
Async XLA Ops:
  2.1 18.2 %collective-permute-start = (f32[384,256]{1,0:T(8,128)S(1)}, f32[384,256]{1,0:T(8,128)S(1)}, u32[]{:S(2)}, u32[]{:S(2)}) collective-permute-start(f32[384,256]{1,0:T(8,128)S(1)} %get-tuple-element.35), channel_id=1, source_target_pairs={{0,2},{1,3},{2,0},{3,1},{4,6},{5,7},{6,4},{7,5},{8,10},{9,11},{10,... | collective-permute-start | bytes 1179656 | tf_op jit(solution)/shard_map/ppermute | solution.py:609
  5.3 15.1 %collective-permute-start.18 = (f32[256,256]{1,0:T(8,128)S(1)}, f32[256,256]{1,0:T(8,128)S(1)}, u32[]{:S(2)}, u32[]{:S(2)}) collective-permute-start(f32[256,256]{1,0:T(8,128)S(1)} %get-tuple-element.47.refs_0_), channel_id=1, source_target_pairs={{0,2},{1,3},{2,0},{3,1},{4,6},{5,7},{6,4},{7,5},{8,10},{9,11},{10,... | collective-permute-start | bytes 786440 | tf_op jit(solution)/shard_map/ppermute | solution.py:609
  5.3 22.1 %collective-permute-start.1 = (f32[320,256]{1,0:T(8,128)S(1)}, f32[320,256]{1,0:T(8,128)S(1)}, u32[]{:S(2)}, u32[]{:S(2)}) collective-permute-start(f32[320,256]{1,0:T(8,128)S(1)} %get-tuple-element.36), channel_id=1, source_target_pairs={{0,4},{1,5},{6,2},{7,3},{8,12},{9,13},{14,10},{15,11},{16,20},{17,... | collective-permute-start | bytes 983048 | tf_op jit(solution)/shard_map/ppermute | solution.py:609
  10.2 17.2 %collective-permute-start.2 = (f32[320,256]{1,0:T(8,128)S(1)}, f32[320,256]{1,0:T(8,128)S(1)}, u32[]{:S(2)}, u32[]{:S(2)}) collective-permute-start(f32[320,256]{1,0:T(8,128)S(1)} %get-tuple-element.37), channel_id=1, source_target_pairs={{2,4},{3,5},{4,2},{5,3},{10,12},{11,13},{12,10},{13,11},{18,20},{1... | collective-permute-start | bytes 983048 | tf_op jit(solution)/shard_map/ppermute | solution.py:609
  10.9 21.0 %collective-permute-start.19 = (f32[256,256]{1,0:T(8,128)S(1)}, f32[256,256]{1,0:T(8,128)S(1)}, u32[]{:S(2)}, u32[]{:S(2)}) collective-permute-start(f32[256,256]{1,0:T(8,128)S(1)} %get-tuple-element.47.refs_0_), channel_id=1, source_target_pairs={{0,4},{1,5},{6,2},{7,3},{8,12},{9,13},{14,10},{15,11},{16,20},{17,... | collective-permute-start | bytes 786440 | tf_op jit(solution)/shard_map/ppermute | solution.py:609
  20.4 12.3 %collective-permute-start.3 = (f32[384,256]{1,0:T(8,128)S(1)}, f32[384,256]{1,0:T(8,128)S(1)}, u32[]{:S(2)}, u32[]{:S(2)}) collective-permute-start(f32[384,256]{1,0:T(8,128)S(1)} %get-tuple-element.34.refs_0_), channel_id=1, source_target_pairs={{0,1},{1,0},{2,3},{3,2},{4,5},{5,4},{6,7},{7,6},{8,9},{9,8},{10,11... | collective-permute-start | bytes 1179656 | tf_op jit(solution)/shard_map/ppermute | solution.py:47
  20.4 13.3 %collective-permute-start.4 = (f32[384,256]{1,0:T(8,128)S(1)}, f32[384,256]{1,0:T(8,128)S(1)}, u32[]{:S(2)}, u32[]{:S(2)}) collective-permute-start(f32[384,256]{1,0:T(8,128)S(1)} %collective-permute-done.refs_1_), channel_id=1, source_target_pairs={{0,1},{1,0},{2,3},{3,2},{4,5},{5,4},{6,7},{7,6},{8,9},{9,8},{10,11... | collective-permute-start | bytes 1179656 | tf_op jit(solution)/shard_map/ppermute | solution.py:47
  27.4 5.8 %collective-permute-start.5 = (f32[320,256]{1,0:T(8,128)S(1)}, f32[320,256]{1,0:T(8,128)S(1)}, u32[]{:S(2)}, u32[]{:S(2)}) collective-permute-start(f32[320,256]{1,0:T(8,128)S(1)} %collective-permute-done.1.refs_2_), channel_id=1, source_target_pairs={{0,1},{1,0},{2,3},{3,2},{4,5},{5,4},{6,7},{7,6},{8,9},{9,8},{10,11... | collective-permute-start | bytes 983048 | tf_op jit(solution)/shard_map/ppermute | solution.py:47
  27.4 5.8 %collective-permute-start.6 = (f32[320,256]{1,0:T(8,128)S(1)}, f32[320,256]{1,0:T(8,128)S(1)}, u32[]{:S(2)}, u32[]{:S(2)}) collective-permute-start(f32[320,256]{1,0:T(8,128)S(1)} %collective-permute-done.2.refs_3_), channel_id=1, source_target_pairs={{0,1},{1,0},{2,3},{3,2},{4,5},{5,4},{6,7},{7,6},{8,9},{9,8},{10,11... | collective-permute-start | bytes 983048 | tf_op jit(solution)/shard_map/ppermute | solution.py:47
  32.6 10.6 %collective-permute-start.21 = (f32[256,256]{1,0:T(8,128)S(1)}, f32[256,256]{1,0:T(8,128)S(1)}, u32[]{:S(2)}, u32[]{:S(2)}) collective-permute-start(f32[256,256]{1,0:T(8,128)S(1)} %get-tuple-element.47.refs_0_), channel_id=1, source_target_pairs={{0,1},{1,0},{2,3},{3,2},{4,5},{5,4},{6,7},{7,6},{8,9},{9,8},{10,11... | collective-permute-start | bytes 786440 | tf_op jit(solution)/shard_map/ppermute | solution.py:47
  32.7 10.5 %collective-permute-start.22 = (f32[256,256]{1,0:T(8,128)S(1)}, f32[256,256]{1,0:T(8,128)S(1)}, u32[]{:S(2)}, u32[]{:S(2)}) collective-permute-start(f32[256,256]{1,0:T(8,128)S(1)} %collective-permute-done.18.refs_1_), channel_id=1, source_target_pairs={{0,1},{1,0},{2,3},{3,2},{4,5},{5,4},{6,7},{7,6},{8,9},{9,8},{10,11... | collective-permute-start | bytes 786440 | tf_op jit(solution)/shard_map/ppermute | solution.py:47
  33.2 10.0 %collective-permute-start.23 = (f32[256,256]{1,0:T(8,128)S(1)}, f32[256,256]{1,0:T(8,128)S(1)}, u32[]{:S(2)}, u32[]{:S(2)}) collective-permute-start(f32[256,256]{1,0:T(8,128)S(1)} %collective-permute-done.19.refs_2_), channel_id=1, source_target_pairs={{0,1},{1,0},{2,3},{3,2},{4,5},{5,4},{6,7},{7,6},{8,9},{9,8},{10,11... | collective-permute-start | bytes 786440 | tf_op jit(solution)/shard_map/ppermute | solution.py:47
  33.2 9.9 %collective-permute-start.24 = (f32[256,256]{1,0:T(8,128)S(1)}, f32[256,256]{1,0:T(8,128)S(1)}, u32[]{:S(2)}, u32[]{:S(2)}) collective-permute-start(f32[256,256]{1,0:T(8,128)S(1)} %collective-permute-done.20.refs_3_), channel_id=1, source_target_pairs={{0,1},{1,0},{2,3},{3,2},{4,5},{5,4},{6,7},{7,6},{8,9},{9,8},{10,11... | collective-permute-start | bytes 786440 | tf_op jit(solution)/shard_map/ppermute | solution.py:47
  33.7 5.6 %collective-permute-start.15 = (f32[8,256]{1,0:T(8,128)S(1)}, f32[8,256]{1,0:T(8,128)S(1)}, u32[]{:S(2)}, u32[]{:S(2)}) collective-permute-start(f32[8,256]{1,0:T(8,128)S(1)} %get-tuple-element.41.refs_3_), channel_id=1, source_target_pairs={{0,6},{1,7},{2,4},{3,5},{4,2},{5,3},{6,0},{7,1},{8,14},{9,15},{10,... | collective-permute-start | bytes 24584 | tf_op jit(solution)/shard_map/ppermute | solution.py:609
  41.7 7.9 %collective-permute-start.17 = (f32[3,64,256]{2,1,0:T(8,128)S(1)}, f32[3,64,256]{2,1,0:T(8,128)S(1)}, u32[]{:S(2)}, u32[]{:S(2)}) collective-permute-start(f32[3,64,256]{2,1,0:T(8,128)S(1)} %get-tuple-element.39.refs_1_), channel_id=1, source_target_pairs={{0,8},{8,16},{16,24},{24,0},{1,9},{9,17},{17,25},{25,1},{2,10},{10... | collective-permute-start | bytes 589832 | tf_op jit(solution)/shard_map/ppermute | solution.py:653
  49.6 7.7 %collective-permute-start.29 = (f32[3,64,256]{2,1,0:T(8,128)S(1)}, f32[3,64,256]{2,1,0:T(8,128)S(1)}, u32[]{:S(2)}, u32[]{:S(2)}) collective-permute-start(f32[3,64,256]{2,1,0:T(8,128)S(1)} %get-tuple-element.49), channel_id=1, source_target_pairs={{0,24},{8,0},{16,8},{24,16},{1,25},{9,1},{17,9},{25,17},{2,26},{10... | collective-permute-start | bytes 589832 | tf_op jit(solution)/shard_map/ppermute | solution.py:638
  57.3 27.8 %collective-permute-start.34 = (f32[3,64,256]{2,1,0:T(8,128)S(1)}, f32[3,64,256]{2,1,0:T(8,128)S(1)}, u32[]{:S(2)}, u32[]{:S(2)}) collective-permute-start(f32[3,64,256]{2,1,0:T(8,128)S(1)} %get-tuple-element.52), channel_id=1, source_target_pairs={{0,24},{8,0},{16,8},{24,16},{1,25},{9,1},{17,9},{25,17},{2,26},{10... | collective-permute-start | bytes 589832 | tf_op jit(solution)/shard_map/ppermute | solution.py:638
  59.8 28.5 %collective-permute-start.7 = (f32[192,256]{1,0:T(8,128)S(1)}, f32[192,256]{1,0:T(8,128)S(1)}, u32[]{:S(2)}, u32[]{:S(2)}) collective-permute-start(f32[192,256]{1,0:T(8,128)S(1)} %bitcast.5), channel_id=1, source_target_pairs={{0,2},{1,3},{2,0},{3,1},{4,6},{5,7},{6,4},{7,5},{8,10},{9,11},{10,... | collective-permute-start | bytes 589832 | tf_op jit(solution)/shard_map/ppermute | solution.py:609
  74.1 14.8 %collective-permute-start.8 = (f32[192,256]{1,0:T(8,128)S(1)}, f32[192,256]{1,0:T(8,128)S(1)}, u32[]{:S(2)}, u32[]{:S(2)}) collective-permute-start(f32[192,256]{1,0:T(8,128)S(1)} %bitcast.6), channel_id=1, source_target_pairs={{2,4},{3,5},{4,2},{5,3},{10,12},{11,13},{12,10},{13,11},{18,20},{1... | collective-permute-start | bytes 589832 | tf_op jit(solution)/shard_map/ppermute | solution.py:609
  74.7 14.2 %collective-permute-start.9 = (f32[192,256]{1,0:T(8,128)S(1)}, f32[192,256]{1,0:T(8,128)S(1)}, u32[]{:S(2)}, u32[]{:S(2)}) collective-permute-start(f32[192,256]{1,0:T(8,128)S(1)} %bitcast.7), channel_id=1, source_target_pairs={{2,6},{3,7},{4,0},{5,1},{10,14},{11,15},{12,8},{13,9},{18,22},{19,... | collective-permute-start | bytes 589832 | tf_op jit(solution)/shard_map/ppermute | solution.py:609
  76.0 5.9 %collective-permute-start.30 = (f32[8,256]{1,0:T(8,128)S(1)}, f32[8,256]{1,0:T(8,128)S(1)}, u32[]{:S(2)}, u32[]{:S(2)}) collective-permute-start(f32[8,256]{1,0:T(8,128)S(1)} %get-tuple-element.51), channel_id=1, source_target_pairs={{0,24},{8,0},{16,8},{24,16},{1,25},{9,1},{17,9},{25,17},{2,26},{10... | collective-permute-start | bytes 24584 | tf_op jit(solution)/shard_map/ppermute | solution.py:638
  85.1 9.6 %collective-permute-start.39 = (f32[3,64,256]{2,1,0:T(8,128)S(1)}, f32[3,64,256]{2,1,0:T(8,128)S(1)}, u32[]{:S(2)}, u32[]{:S(2)}) collective-permute-start(f32[3,64,256]{2,1,0:T(8,128)S(1)} %get-tuple-element.54), channel_id=1, source_target_pairs={{0,24},{8,0},{16,8},{24,16},{1,25},{9,1},{17,9},{25,17},{2,26},{10... | collective-permute-start | bytes 589832 | tf_op jit(solution)/shard_map/ppermute | solution.py:638
  88.3 15.9 %collective-permute-start.10 = (f32[192,256]{1,0:T(8,128)S(1)}, f32[192,256]{1,0:T(8,128)S(1)}, u32[]{:S(2)}, u32[]{:S(2)}) collective-permute-start(f32[192,256]{1,0:T(8,128)S(1)} %bitcast.8), channel_id=1, source_target_pairs={{0,1},{1,0},{2,3},{3,2},{4,5},{5,4},{6,7},{7,6},{8,9},{9,8},{10,11... | collective-permute-start | bytes 589832 | tf_op jit(solution)/shard_map/ppermute | solution.py:47
  88.3 16.6 %collective-permute-start.11 = (f32[192,256]{1,0:T(8,128)S(1)}, f32[192,256]{1,0:T(8,128)S(1)}, u32[]{:S(2)}, u32[]{:S(2)}) collective-permute-start(f32[192,256]{1,0:T(8,128)S(1)} %collective-permute-done.7.refs_1_), channel_id=1, source_target_pairs={{0,1},{1,0},{2,3},{3,2},{4,5},{5,4},{6,7},{7,6},{8,9},{9,8},{10,11... | collective-permute-start | bytes 589832 | tf_op jit(solution)/shard_map/ppermute | solution.py:47
  94.2 12.3 %collective-permute-start.12 = (f32[192,256]{1,0:T(8,128)S(1)}, f32[192,256]{1,0:T(8,128)S(1)}, u32[]{:S(2)}, u32[]{:S(2)}) collective-permute-start(f32[192,256]{1,0:T(8,128)S(1)} %collective-permute-done.8.refs_2_), channel_id=1, source_target_pairs={{0,1},{1,0},{2,3},{3,2},{4,5},{5,4},{6,7},{7,6},{8,9},{9,8},{10,11... | collective-permute-start | bytes 589832 | tf_op jit(solution)/shard_map/ppermute | solution.py:47
  94.3 18.0 %collective-permute-start.13 = (f32[192,256]{1,0:T(8,128)S(1)}, f32[192,256]{1,0:T(8,128)S(1)}, u32[]{:S(2)}, u32[]{:S(2)}) collective-permute-start(f32[192,256]{1,0:T(8,128)S(1)} %collective-permute-done.9.refs_3_), channel_id=1, source_target_pairs={{0,1},{1,0},{2,3},{3,2},{4,5},{5,4},{6,7},{7,6},{8,9},{9,8},{10,11... | collective-permute-start | bytes 589832 | tf_op jit(solution)/shard_map/ppermute | solution.py:47
  94.7 30.3 %collective-permute-start.40 = (f32[192,256]{1,0:T(8,128)S(1)}, f32[192,256]{1,0:T(8,128)S(1)}, u32[]{:S(2)}, u32[]{:S(2)}) collective-permute-start(f32[192,256]{1,0:T(8,128)S(1)} %shard_map.117.refs_8_), channel_id=1, source_target_pairs={{0,2},{1,3},{2,0},{3,1},{4,6},{5,7},{6,4},{7,5},{8,10},{9,11},{10,... | collective-permute-start | bytes 589832 | tf_op jit(solution)/shard_map/ppermute | solution.py:609
  104.2 20.9 %collective-permute-start.41 = (f32[192,256]{1,0:T(8,128)S(1)}, f32[192,256]{1,0:T(8,128)S(1)}, u32[]{:S(2)}, u32[]{:S(2)}) collective-permute-start(f32[192,256]{1,0:T(8,128)S(1)} %shard_map.117.refs_8_), channel_id=1, source_target_pairs={{2,4},{3,5},{4,2},{5,3},{10,12},{11,13},{12,10},{13,11},{18,20},{1... | collective-permute-start | bytes 589832 | tf_op jit(solution)/shard_map/ppermute | solution.py:609
  104.9 20.7 %collective-permute-start.42 = (f32[192,256]{1,0:T(8,128)S(1)}, f32[192,256]{1,0:T(8,128)S(1)}, u32[]{:S(2)}, u32[]{:S(2)}) collective-permute-start(f32[192,256]{1,0:T(8,128)S(1)} %shard_map.117.refs_8_), channel_id=1, source_target_pairs={{2,6},{3,7},{4,0},{5,1},{10,14},{11,15},{12,8},{13,9},{18,22},{19,... | collective-permute-start | bytes 589832 | tf_op jit(solution)/shard_map/ppermute | solution.py:609
  106.5 12.9 %collective-permute-start.47 = (f32[64,256]{1,0:T(8,128)S(1)}, f32[64,256]{1,0:T(8,128)S(1)}, u32[]{:S(2)}, u32[]{:S(2)}) collective-permute-start(f32[64,256]{1,0:T(8,128)S(1)} %get-tuple-element.56), channel_id=1, source_target_pairs={{0,2},{1,3},{2,0},{3,1},{4,6},{5,7},{6,4},{7,5},{8,10},{9,11},{10,... | collective-permute-start | bytes 196616 | tf_op jit(solution)/shard_map/ppermute | solution.py:609
  112.3 7.0 %collective-permute-start.48 = (f32[64,256]{1,0:T(8,128)S(1)}, f32[64,256]{1,0:T(8,128)S(1)}, u32[]{:S(2)}, u32[]{:S(2)}) collective-permute-start(f32[64,256]{1,0:T(8,128)S(1)} %get-tuple-element.57), channel_id=1, source_target_pairs={{0,6},{1,7},{2,4},{3,5},{4,2},{5,3},{6,0},{7,1},{8,14},{9,15},{10,... | collective-permute-start | bytes 196616 | tf_op jit(solution)/shard_map/ppermute | solution.py:609
  119.4 5.2 %collective-permute-start.49 = (f32[64,256]{1,0:T(8,128)S(1)}, f32[64,256]{1,0:T(8,128)S(1)}, u32[]{:S(2)}, u32[]{:S(2)}) collective-permute-start(f32[64,256]{1,0:T(8,128)S(1)} %get-tuple-element.58), channel_id=1, source_target_pairs={{0,4},{1,5},{2,6},{3,7},{4,0},{5,1},{6,2},{7,3},{8,12},{9,13},{10,... | collective-permute-start | bytes 196616 | tf_op jit(solution)/shard_map/ppermute | solution.py:609
  (27 other events, 187.0 us)
where the time goes:
time: 132 us; the launch traced here: 131 us
  starting transfers between devices  72.8 us (55%)
  waiting for transfers between devices  52 us (39%)
  Pallas kernels  5.6 us (4%)
    ppermute x16, starting transfers between devices, by_xor(): lax.ppermute(array, 'tok', [(2 * a + core, 2 * (a ^ by) + core) for a in...  49.8 us
    ppermute x16, waiting for transfers between devices, by_xor(): lax.ppermute(array, 'tok', [(2 * a + core, 2 * (a ^ by) + core) for a in...  30.9 us
    ppermute x6, starting transfers between devices, to_earlier(): lax.ppermute(array, 'block', [(i, (i - 1) % groups) for i in range(groups)])  13.4 us
    ppermute x6, waiting for transfers between devices, to_earlier(): lax.ppermute(array, 'block', [(i, (i - 1) % groups) for i in range(groups)])  7.43 us
    ppermute x28, waiting for transfers between devices, core_swap(): return lax.ppermute(array, 'tok', [(j, j ^ 1) for j in range(size)])  7.33 us
    ppermute x1, waiting for transfers between devices, to_later(): lax.ppermute(array, 'block', [(i, (i + 1) % groups) for i in range(groups)])  6.36 us
    ppermute x28, starting transfers between devices, core_swap(): return lax.ppermute(array, 'tok', [(j, j ^ 1) for j in range(size)])  6.1 us
    pallas_call x10, Pallas kernels, kernel_call(): pl.pallas_call(body, in_specs=[pl.BlockSpec(memory_space=space) for _ in...  5.6 us
  transfers between devices with their start and end apart: 54, of which 19 were waited for; matrix products, arithmetic and copies ran while one was open for 0% of the time, Pallas kernels for 1%

commit v1 on v0

--- a/solution.py
+++ b/solution.py
@@ -529,10 +529,10 @@
         table[...] = jnp.concatenate(rows[:2]).T
         low = chip == LOW
         upper, lower = rows[2][:depth], rows[2][depth:]
-        picks = jnp.where(low, lower, upper), jnp.where(low, upper, lower), upper, upper
-        for by, (out, pick) in enumerate(zip(outs, picks)):
-            start = rows_at(jnp.bitwise_xor(chip, by) * 2 * depth, 2 * depth)
-            out[:, :128] = table[start, :]
+        picks = jnp.where(low, lower, upper), jnp.where(low, upper, lower)
+        for by, out in enumerate(outs):
+            out[:, :128] = table[rows_at(jnp.bitwise_xor(chip, by) * 2 * depth, 2 * depth), :]
+        for out, pick in zip(outs, picks):
             out[:depth, 128:] = pick[:, :128]
             out[depth:, 128:] = pick[:, 128:]
 
@@ -591,7 +591,7 @@
     low_side, upper_core = my_chip() <= LOW, my_core() == 0
     sides = []
     for near, far in ((ends[0], ends[1]), (ends[2], ends[3])):
-        pair = jnp.where(low_side, near, far), jnp.where(low_side, far, near)
+        pair = jnp.where(low_side, near[:, :128], far), jnp.where(low_side, far, near[:, :128])
         sides.append([jnp.where(upper_core, piece[:depth], piece[depth:]) for piece in pair])
     by_core = [[jnp.where(upper_core, a, b) for a, b in zip(*sides)], [jnp.where(upper_core, b, a) for a, b in zip(*sides)]]
     for m in range(2):
@@ -609,9 +609,19 @@
     return lax.ppermute(array, "tok", [(2 * a + core, 2 * (a ^ by) + core) for a in chips for core in range(2)])
 
 
+def exchanged(array):
+    size = lax.axis_size("tok")
+    gathered = [array]
+    for bits in (2 * (LOW ^ HIGH_CHIP), 2 * (LOW ^ HIGH_CHIP) + 1, 1):
+        gathered.append(lax.ppermute(array, "tok", [(j, j ^ bits) for j in range(size)]))
+    return gathered
+
+
 def both_cores(pieces):
     swapped = [core_swap(pieces[0])]
-    return pieces + swapped + [core_swap(piece) for piece in pieces[1:]]
+    for piece in pieces[1:]:
+        swapped.append(core_swap(piece))
+    return pieces + swapped
 
 
 def hops(arrays, near, far, across):
@@ -636,16 +646,6 @@
 def to_earlier(array):
     groups = lax.axis_size("block")
     return lax.ppermute(array, "block", [(i, (i - 1) % groups) for i in range(groups)])
-
-
-def chain_to_block(array, source, target, by):
-    size = lax.axis_size("tok")
-    places = [(chip, core) for chip in (LOW, HIGH_CHIP) for core in range(2)]
-    return lax.ppermute(
-        array,
-        ("block", "tok"),
-        [(source * size + 2 * chip + core, target * size + 2 * (chip ^ by) + core) for chip, core in places],
-    )
 
 
 def to_later(array):
@@ -682,8 +682,7 @@
         *pieces,
         scratch=[pltpu.VMEM((width, 4 * span), jnp.float32)],
     )
-    across = by_xor(sums, 3, ALL)
-    all_sums = [sums, core_swap(sums), across, core_swap(across)]
+    all_sums = exchanged(sums)
     earlier = to_later(shifted)
     weights = from_chain([own.reshape(3 * span, width)] * CHIPS, False)
 
@@ -701,16 +700,15 @@
             payload, partial = kernel_call(
                 body, sent, *common, *inners[-4:], *arrived[-1:], *halved, kept, applied, earlier
             )
-        cross = chain_to_block(partial, source, source - 1, 3)
         straight = to_earlier(partial)
         arrived.append(to_earlier(payload))
-        inners += [straight, cross, core_swap(straight), core_swap(cross)]
+        inners += exchanged(straight)
     received = [*common, *inners, *arrived]
     (cot,) = kernel_call(functools.partial(terms_body, groups - 1), [wide], *received)
     cots = from_chain([cot] * CHIPS, False)
     ends = kernel_call(
         functools.partial(final_body, groups - 1),
-        [f32(2 * rows, width)] * CHIPS,
+        [f32(2 * rows, width)] * 2 + [f32(2 * rows, 128)] * 2,
         *received,
         *halved,
         kept,

time: 132 us -> 139 us (1.053)
  waiting for transfers between devices: 52 us -> 61.6 us
  starting transfers between devices: 72.8 us -> 69.7 us
    ppermute x3 -> x12, waiting for transfers between devices: 0.01 us -> 25.4 us  [exchanged(): lax.ppermute(array, 'tok', [(j, j ^ bits) for j in range(size)])]
    ppermute x16 -> x15, waiting for transfers between devices: 30.9 us -> 19 us  [by_xor(): lax.ppermute(array, 'tok', [(2 * a + core, 2 * (a ^ by) + core) for a in...]
    ppermute x16 -> x15, starting transfers between devices: 49.8 us -> 39.4 us  [by_xor(): lax.ppermute(array, 'tok', [(2 * a + core, 2 * (a ^ by) + core) for a in...]
    ppermute x3 -> x12, starting transfers between devices: 1.95 us -> 12.3 us  [exchanged(): lax.ppermute(array, 'tok', [(j, j ^ bits) for j in range(size)])]
    ppermute x28 -> x20, waiting for transfers between devices: 7.33 us -> 2.14 us  [core_swap(): return lax.ppermute(array, 'tok', [(j, j ^ 1) for j in range(size)])]
    ppermute x6, starting transfers between devices: 13.4 us -> 11.5 us  [to_earlier(): lax.ppermute(array, 'block', [(i, (i - 1) % groups) for i in range(groups)])]
    ppermute x28 -> x20, starting transfers between devices: 6.1 us -> 5.1 us  [core_swap(): return lax.ppermute(array, 'tok', [(j, j ^ 1) for j in range(size)])]
  transfers between devices with their start and end apart: 54 -> 54, of which waited for: 19 -> 21; matrix products, arithmetic and copies ran while one was open for 0% -> 0% of each run, Pallas kernels for 1% -> 1%
where the time goes in v1:
time: 139 us; the launch traced here: 138 us
  starting transfers between devices  69.7 us (50%)
  waiting for transfers between devices  61.6 us (44%)
  Pallas kernels  5.58 us (4%)
    ppermute x15, starting transfers between devices, by_xor(): lax.ppermute(array, 'tok', [(2 * a + core, 2 * (a ^ by) + core) for a in...  39.4 us
    ppermute x12, waiting for transfers between devices, exchanged(): lax.ppermute(array, 'tok', [(j, j ^ bits) for j in range(size)])  25.4 us
    ppermute x15, waiting for transfers between devices, by_xor(): lax.ppermute(array, 'tok', [(2 * a + core, 2 * (a ^ by) + core) for a in...  19 us
    ppermute x12, starting transfers between devices, exchanged(): lax.ppermute(array, 'tok', [(j, j ^ bits) for j in range(size)])  12.3 us
    ppermute x6, starting transfers between devices, to_earlier(): lax.ppermute(array, 'block', [(i, (i - 1) % groups) for i in range(groups)])  11.5 us
    ppermute x6, waiting for transfers between devices, to_earlier(): lax.ppermute(array, 'block', [(i, (i - 1) % groups) for i in range(groups)])  8.75 us
    ppermute x1, waiting for transfers between devices, to_later(): lax.ppermute(array, 'block', [(i, (i + 1) % groups) for i in range(groups)])  6.36 us
    pallas_call x10, Pallas kernels, kernel_call(): pl.pallas_call(body, in_specs=[pl.BlockSpec(memory_space=space) for _ in...  5.58 us
  transfers between devices with their start and end apart: 54, of which 21 were waited for; matrix products, arithmetic and copies ran while one was open for 0% of the time, Pallas kernels for 1%

profile of v1, /device:TPU:0, one launch (start us, length us, event | category | flops | bytes accessed | tf_op | source)
XLA Modules:
  0.0 137.9 jit_solution(2469828555297989425)
XLA Ops:
  2.1 3.1 %collective-permute-start = (f32[384,256]{1,0:T(8,128)S(1)}, f32[384,256]{1,0:T(8,128)S(1)}, u32[]{:S(2)}, u32[]{:S(2)}) collective-permute-start(f32[384,256]{1,0:T(8,128)S(1)} %get-tuple-element.35), channel_id=1, source_target_pairs={{0,2},{1,3},{2,0},{3,1},{4,6},{5,7},{6,4},{7,5},{8,10},{9,11},{10,... | collective-permute-start | bytes 1179656 | tf_op jit(solution)/shard_map/ppermute | solution.py:609
  5.3 4.9 %collective-permute-start.1 = (f32[320,256]{1,0:T(8,128)S(1)}, f32[320,256]{1,0:T(8,128)S(1)}, u32[]{:S(2)}, u32[]{:S(2)}) collective-permute-start(f32[320,256]{1,0:T(8,128)S(1)} %get-tuple-element.36), channel_id=1, source_target_pairs={{0,4},{1,5},{6,2},{7,3},{8,12},{9,13},{14,10},{15,11},{16,20},{17,... | collective-permute-start | bytes 983048 | tf_op jit(solution)/shard_map/ppermute | solution.py:609
  10.9 3.0 %collective-permute-start.19 = (f32[256,256]{1,0:T(8,128)S(1)}, f32[256,256]{1,0:T(8,128)S(1)}, u32[]{:S(2)}, u32[]{:S(2)}) collective-permute-start(f32[256,256]{1,0:T(8,128)S(1)} %get-tuple-element.47.refs_0_), channel_id=1, source_target_pairs={{0,4},{1,5},{6,2},{7,3},{8,12},{9,13},{14,10},{15,11},{16,20},{17,... | collective-permute-start | bytes 786440 | tf_op jit(solution)/shard_map/ppermute | solution.py:609
  13.9 6.5 %collective-permute-done.18.refs_1_ = f32[256,256]{1,0:T(8,128)S(1)} collective-permute-done((f32[256,256]{1,0:T(8,128)S(1)}, f32[256,256]{1,0:T(8,128)S(1)}, u32[]{:S(2)}, u32[]{:S(2)}) %collective-permute-start.18) | collective-permute-done | bytes 262176 | tf_op jit(solution)/shard_map/ppermute | solution.py:609
  20.9 6.5 %collective-permute-done.1.refs_2_ = f32[320,256]{1,0:T(8,128)S(1)} collective-permute-done((f32[320,256]{1,0:T(8,128)S(1)}, f32[320,256]{1,0:T(8,128)S(1)}, u32[]{:S(2)}, u32[]{:S(2)}) %collective-permute-start.1) | collective-permute-done | bytes 327712 | tf_op jit(solution)/shard_map/ppermute | solution.py:609
  27.9 4.0 %collective-permute-done.19.refs_2_ = f32[256,256]{1,0:T(8,128)S(1)} collective-permute-done((f32[256,256]{1,0:T(8,128)S(1)}, f32[256,256]{1,0:T(8,128)S(1)}, u32[]{:S(2)}, u32[]{:S(2)}) %collective-permute-start.19) | collective-permute-done | bytes 262176 | tf_op jit(solution)/shard_map/ppermute | solution.py:609
  33.7 2.5 %collective-permute-start.14 = (f32[8,256]{1,0:T(8,128)S(1)}, f32[8,256]{1,0:T(8,128)S(1)}, u32[]{:S(2)}, u32[]{:S(2)}) collective-permute-start(f32[8,256]{1,0:T(8,128)S(1)} %get-tuple-element.41.refs_3_), channel_id=1, source_target_pairs={{0,6},{1,7},{2,4},{3,5},{4,2},{5,3},{6,0},{7,1},{8,14},{9,15},{10,... | collective-permute-start | bytes 24584 | tf_op jit(solution)/shard_map/ppermute | solution.py:616
  36.2 3.1 %collective-permute-done.14.refs_4_ = f32[8,256]{1,0:T(8,128)S(1)} collective-permute-done((f32[8,256]{1,0:T(8,128)S(1)}, f32[8,256]{1,0:T(8,128)S(1)}, u32[]{:S(2)}, u32[]{:S(2)}) %collective-permute-start.14) | collective-permute-done | bytes 8224 | tf_op jit(solution)/shard_map/ppermute | solution.py:616
  40.3 3.9 %collective-permute-done.15.refs_5_ = f32[8,256]{1,0:T(8,128)S(1)} collective-permute-done((f32[8,256]{1,0:T(8,128)S(1)}, f32[8,256]{1,0:T(8,128)S(1)}, u32[]{:S(2)}, u32[]{:S(2)}) %collective-permute-start.15) | collective-permute-done | bytes 8224 | tf_op jit(solution)/shard_map/ppermute | solution.py:616
  46.9 6.4 %collective-permute-done.17.earlier.refs_18_ = f32[3,64,256]{2,1,0:T(8,128)S(1)} collective-permute-done((f32[3,64,256]{2,1,0:T(8,128)S(1)}, f32[3,64,256]{2,1,0:T(8,128)S(1)}, u32[]{:S(2)}, u32[]{:S(2)}) %collective-permute-start.17) | collective-permute-done | bytes 196640 | tf_op jit(solution)/shard_map/ppermute | solution.py:653
  53.3 1.6 %collective-permute-start.29 = (f32[3,64,256]{2,1,0:T(8,128)S(1)}, f32[3,64,256]{2,1,0:T(8,128)S(1)}, u32[]{:S(2)}, u32[]{:S(2)}) collective-permute-start(f32[3,64,256]{2,1,0:T(8,128)S(1)} %get-tuple-element.49), channel_id=1, source_target_pairs={{0,24},{8,0},{16,8},{24,16},{1,25},{9,1},{17,9},{25,17},{2,26},{10... | collective-permute-start | bytes 589832 | tf_op jit(solution)/shard_map/ppermute | solution.py:648
  56.3 3.3 %collective-permute-done.25.refs_7_ = f32[8,256]{1,0:T(8,128)S(1)} collective-permute-done((f32[8,256]{1,0:T(8,128)S(1)}, f32[8,256]{1,0:T(8,128)S(1)}, u32[]{:S(2)}, u32[]{:S(2)}) %collective-permute-start.25) | collective-permute-done | bytes 8224 | tf_op jit(solution)/shard_map/ppermute | solution.py:648
  59.6 2.5 %collective-permute-start.26 = (f32[8,256]{1,0:T(8,128)S(1)}, f32[8,256]{1,0:T(8,128)S(1)}, u32[]{:S(2)}, u32[]{:S(2)}) collective-permute-start(f32[8,256]{1,0:T(8,128)S(1)} %collective-permute-done.25.refs_7_), channel_id=1, source_target_pairs={{0,6},{1,7},{2,4},{3,5},{4,2},{5,3},{6,0},{7,1},{8,14},{9,15},{10,... | collective-permute-start | bytes 24584 | tf_op jit(solution)/shard_map/ppermute | solution.py:616
  63.6 1.5 %collective-permute-done.26.refs_8_ = f32[8,256]{1,0:T(8,128)S(1)} collective-permute-done((f32[8,256]{1,0:T(8,128)S(1)}, f32[8,256]{1,0:T(8,128)S(1)}, u32[]{:S(2)}, u32[]{:S(2)}) %collective-permute-start.26) | collective-permute-done | bytes 8224 | tf_op jit(solution)/shard_map/ppermute | solution.py:616
  65.1 1.9 %collective-permute-done.27.refs_9_ = f32[8,256]{1,0:T(8,128)S(1)} collective-permute-done((f32[8,256]{1,0:T(8,128)S(1)}, f32[8,256]{1,0:T(8,128)S(1)}, u32[]{:S(2)}, u32[]{:S(2)}) %collective-permute-start.27) | collective-permute-done | bytes 8224 | tf_op jit(solution)/shard_map/ppermute | solution.py:616
  67.0 2.5 %collective-permute-start.34 = (f32[3,64,256]{2,1,0:T(8,128)S(1)}, f32[3,64,256]{2,1,0:T(8,128)S(1)}, u32[]{:S(2)}, u32[]{:S(2)}) collective-permute-start(f32[3,64,256]{2,1,0:T(8,128)S(1)} %get-tuple-element.52), channel_id=1, source_target_pairs={{0,24},{8,0},{16,8},{24,16},{1,25},{9,1},{17,9},{25,17},{2,26},{10... | collective-permute-start | bytes 589832 | tf_op jit(solution)/shard_map/ppermute | solution.py:648
  69.5 8.9 %collective-permute-start.7 = (f32[192,256]{1,0:T(8,128)S(1)}, f32[192,256]{1,0:T(8,128)S(1)}, u32[]{:S(2)}, u32[]{:S(2)}) collective-permute-start(f32[192,256]{1,0:T(8,128)S(1)} %bitcast.5), channel_id=1, source_target_pairs={{0,2},{1,3},{2,0},{3,1},{4,6},{5,7},{6,4},{7,5},{8,10},{9,11},{10,... | collective-permute-start | bytes 589832 | tf_op jit(solution)/shard_map/ppermute | solution.py:609
  80.4 2.6 %collective-permute-start.30 = (f32[8,256]{1,0:T(8,128)S(1)}, f32[8,256]{1,0:T(8,128)S(1)}, u32[]{:S(2)}, u32[]{:S(2)}) collective-permute-start(f32[8,256]{1,0:T(8,128)S(1)} %get-tuple-element.51), channel_id=1, source_target_pairs={{0,24},{8,0},{16,8},{24,16},{1,25},{9,1},{17,9},{25,17},{2,26},{10... | collective-permute-start | bytes 24584 | tf_op jit(solution)/shard_map/ppermute | solution.py:648
  84.4 2.3 %collective-permute-start.31 = (f32[8,256]{1,0:T(8,128)S(1)}, f32[8,256]{1,0:T(8,128)S(1)}, u32[]{:S(2)}, u32[]{:S(2)}) collective-permute-start(f32[8,256]{1,0:T(8,128)S(1)} %collective-permute-done.30.refs_7_.refs_11_), channel_id=1, source_target_pairs={{0,6},{1,7},{2,4},{3,5},{4,2},{5,3},{6,0},{7,1},{8,14},{9,15},{10,... | collective-permute-start | bytes 24584 | tf_op jit(solution)/shard_map/ppermute | solution.py:616
  86.7 3.2 %collective-permute-done.31.refs_8_.refs_12_ = f32[8,256]{1,0:T(8,128)S(1)} collective-permute-done((f32[8,256]{1,0:T(8,128)S(1)}, f32[8,256]{1,0:T(8,128)S(1)}, u32[]{:S(2)}, u32[]{:S(2)}) %collective-permute-start.31) | collective-permute-done | bytes 8224 | tf_op jit(solution)/shard_map/ppermute | solution.py:616
  89.9 4.9 %collective-permute-done.32.refs_9_.refs_13_ = f32[8,256]{1,0:T(8,128)S(1)} collective-permute-done((f32[8,256]{1,0:T(8,128)S(1)}, f32[8,256]{1,0:T(8,128)S(1)}, u32[]{:S(2)}, u32[]{:S(2)}) %collective-permute-start.32) | collective-permute-done | bytes 8224 | tf_op jit(solution)/shard_map/ppermute | solution.py:616
  96.0 3.2 %collective-permute-start.39 = (f32[3,64,256]{2,1,0:T(8,128)S(1)}, f32[3,64,256]{2,1,0:T(8,128)S(1)}, u32[]{:S(2)}, u32[]{:S(2)}) collective-permute-start(f32[3,64,256]{2,1,0:T(8,128)S(1)} %get-tuple-element.54), channel_id=1, source_target_pairs={{0,24},{8,0},{16,8},{24,16},{1,25},{9,1},{17,9},{25,17},{2,26},{10... | collective-permute-start | bytes 589832 | tf_op jit(solution)/shard_map/ppermute | solution.py:648
  99.8 4.1 %collective-permute-done.35.refs_15_ = f32[8,256]{1,0:T(8,128)S(1)} collective-permute-done((f32[8,256]{1,0:T(8,128)S(1)}, f32[8,256]{1,0:T(8,128)S(1)}, u32[]{:S(2)}, u32[]{:S(2)}) %collective-permute-start.35) | collective-permute-done | bytes 8224 | tf_op jit(solution)/shard_map/ppermute | solution.py:648
  103.9 2.2 %collective-permute-start.36 = (f32[8,256]{1,0:T(8,128)S(1)}, f32[8,256]{1,0:T(8,128)S(1)}, u32[]{:S(2)}, u32[]{:S(2)}) collective-permute-start(f32[8,256]{1,0:T(8,128)S(1)} %collective-permute-done.35.refs_15_), channel_id=1, source_target_pairs={{0,6},{1,7},{2,4},{3,5},{4,2},{5,3},{6,0},{7,1},{8,14},{9,15},{10,... | collective-permute-start | bytes 24584 | tf_op jit(solution)/shard_map/ppermute | solution.py:616
  106.4 3.0 %collective-permute-done.36.refs_16_ = f32[8,256]{1,0:T(8,128)S(1)} collective-permute-done((f32[8,256]{1,0:T(8,128)S(1)}, f32[8,256]{1,0:T(8,128)S(1)}, u32[]{:S(2)}, u32[]{:S(2)}) %collective-permute-start.36) | collective-permute-done | bytes 8224 | tf_op jit(solution)/shard_map/ppermute | solution.py:616
  109.4 1.6 %collective-permute-done.37.refs_17_ = f32[8,256]{1,0:T(8,128)S(1)} collective-permute-done((f32[8,256]{1,0:T(8,128)S(1)}, f32[8,256]{1,0:T(8,128)S(1)}, u32[]{:S(2)}, u32[]{:S(2)}) %collective-permute-start.37) | collective-permute-done | bytes 8224 | tf_op jit(solution)/shard_map/ppermute | solution.py:616
  114.1 1.7 %collective-permute-start.48 = (f32[64,128]{1,0:T(8,128)S(1)}, f32[64,128]{1,0:T(8,128)S(1)}, u32[]{:S(2)}, u32[]{:S(2)}) collective-permute-start(f32[64,128]{1,0:T(8,128)S(1)} %get-tuple-element.57), channel_id=1, source_target_pairs={{0,6},{1,7},{2,4},{3,5},{4,2},{5,3},{6,0},{7,1},{8,14},{9,15},{10,... | collective-permute-start | bytes 98312 | tf_op jit(solution)/shard_map/ppermute | solution.py:609
  115.8 5.7 %collective-permute-start.47 = (f32[64,256]{1,0:T(8,128)S(1)}, f32[64,256]{1,0:T(8,128)S(1)}, u32[]{:S(2)}, u32[]{:S(2)}) collective-permute-start(f32[64,256]{1,0:T(8,128)S(1)} %get-tuple-element.56), channel_id=1, source_target_pairs={{0,2},{1,3},{2,0},{3,1},{4,6},{5,7},{6,4},{7,5},{8,10},{9,11},{10,... | collective-permute-start | bytes 196616 | tf_op jit(solution)/shard_map/ppermute | solution.py:609
  121.4 6.6 %collective-permute-start.49 = (f32[64,128]{1,0:T(8,128)S(1)}, f32[64,128]{1,0:T(8,128)S(1)}, u32[]{:S(2)}, u32[]{:S(2)}) collective-permute-start(f32[64,128]{1,0:T(8,128)S(1)} %get-tuple-element.58), channel_id=1, source_target_pairs={{0,4},{1,5},{2,6},{3,7},{4,0},{5,1},{6,2},{7,3},{8,12},{9,13},{10,... | collective-permute-start | bytes 98312 | tf_op jit(solution)/shard_map/ppermute | solution.py:609
  128.0 2.0 %collective-permute-done.49.refs_19_ = f32[64,128]{1,0:T(8,128)S(1)} collective-permute-done((f32[64,128]{1,0:T(8,128)S(1)}, f32[64,128]{1,0:T(8,128)S(1)}, u32[]{:S(2)}, u32[]{:S(2)}) %collective-permute-start.49) | collective-permute-done | bytes 32800 | tf_op jit(solution)/shard_map/ppermute | solution.py:609
  134.1 1.5 %shard_map.112 = f32[128,256]{1,0:T(8,128)} custom-call(f32[128,256]{1,0:T(8,128)S(1)} %copy-done.2, f32[128,256]{1,0:T(8,128)S(1)} %copy-done.3, f32[192,256]{1,0:T(8,128)S(1)} %bitcast.9, f32[192,256]{1,0:T(8,128)S(1)} %collective-permute-done.7.refs_1_, f32[192,256]{1,0:T(8,128)S(1)} %collective-permute-done.8.refs_2_, ...), custom_call_target="tpu_custom_call" | custom-call | tf_op jit(solution)/shard_map/pallas_call | solution.py:236
  135.7 2.2 %shard_map.119 = (f32[128,256]{1,0:T(8,128)}, f32[128,256]{1,0:T(8,128)}, f32[1,128]{1,0:T(1,128)}, f32[3,32,256]{2,1,0:T(8,128)}) custom-call(f32[128,256]{1,0:T(8,128)S(1)} %copy-done, f32[128,256]{1,0:T(8,128)S(1)} %copy-done.1, f32[1,128]{1,0:T(1,128)S(1)} %bitcast.12, f32[192,256]{1,0:T(8,128)S(1)} %bitcast.10, ...), custom_call_target="tpu_custom_call" | custom-call | tf_op jit(solution)/shard_map/pallas_call | solution.py:236
  (96 shorter events, 24.2 us)
Async XLA Ops:
  2.1 18.2 %collective-permute-start = (f32[384,256]{1,0:T(8,128)S(1)}, f32[384,256]{1,0:T(8,128)S(1)}, u32[]{:S(2)}, u32[]{:S(2)}) collective-permute-start(f32[384,256]{1,0:T(8,128)S(1)} %get-tuple-element.35), channel_id=1, source_target_pairs={{0,2},{1,3},{2,0},{3,1},{4,6},{5,7},{6,4},{7,5},{8,10},{9,11},{10,... | collective-permute-start | bytes 1179656 | tf_op jit(solution)/shard_map/ppermute | solution.py:609
  5.3 15.1 %collective-permute-start.18 = (f32[256,256]{1,0:T(8,128)S(1)}, f32[256,256]{1,0:T(8,128)S(1)}, u32[]{:S(2)}, u32[]{:S(2)}) collective-permute-start(f32[256,256]{1,0:T(8,128)S(1)} %get-tuple-element.47.refs_0_), channel_id=1, source_target_pairs={{0,2},{1,3},{2,0},{3,1},{4,6},{5,7},{6,4},{7,5},{8,10},{9,11},{10,... | collective-permute-start | bytes 786440 | tf_op jit(solution)/shard_map/ppermute | solution.py:609
  5.3 22.1 %collective-permute-start.1 = (f32[320,256]{1,0:T(8,128)S(1)}, f32[320,256]{1,0:T(8,128)S(1)}, u32[]{:S(2)}, u32[]{:S(2)}) collective-permute-start(f32[320,256]{1,0:T(8,128)S(1)} %get-tuple-element.36), channel_id=1, source_target_pairs={{0,4},{1,5},{6,2},{7,3},{8,12},{9,13},{14,10},{15,11},{16,20},{17,... | collective-permute-start | bytes 983048 | tf_op jit(solution)/shard_map/ppermute | solution.py:609
  10.2 17.2 %collective-permute-start.2 = (f32[320,256]{1,0:T(8,128)S(1)}, f32[320,256]{1,0:T(8,128)S(1)}, u32[]{:S(2)}, u32[]{:S(2)}) collective-permute-start(f32[320,256]{1,0:T(8,128)S(1)} %get-tuple-element.37), channel_id=1, source_target_pairs={{2,4},{3,5},{4,2},{5,3},{10,12},{11,13},{12,10},{13,11},{18,20},{1... | collective-permute-start | bytes 983048 | tf_op jit(solution)/shard_map/ppermute | solution.py:609
  10.9 21.0 %collective-permute-start.19 = (f32[256,256]{1,0:T(8,128)S(1)}, f32[256,256]{1,0:T(8,128)S(1)}, u32[]{:S(2)}, u32[]{:S(2)}) collective-permute-start(f32[256,256]{1,0:T(8,128)S(1)} %get-tuple-element.47.refs_0_), channel_id=1, source_target_pairs={{0,4},{1,5},{6,2},{7,3},{8,12},{9,13},{14,10},{15,11},{16,20},{17,... | collective-permute-start | bytes 786440 | tf_op jit(solution)/shard_map/ppermute | solution.py:609
  20.4 12.3 %collective-permute-start.3 = (f32[384,256]{1,0:T(8,128)S(1)}, f32[384,256]{1,0:T(8,128)S(1)}, u32[]{:S(2)}, u32[]{:S(2)}) collective-permute-start(f32[384,256]{1,0:T(8,128)S(1)} %get-tuple-element.34.refs_0_), channel_id=1, source_target_pairs={{0,1},{1,0},{2,3},{3,2},{4,5},{5,4},{6,7},{7,6},{8,9},{9,8},{10,11... | collective-permute-start | bytes 1179656 | tf_op jit(solution)/shard_map/ppermute | solution.py:47
  20.4 13.3 %collective-permute-start.4 = (f32[384,256]{1,0:T(8,128)S(1)}, f32[384,256]{1,0:T(8,128)S(1)}, u32[]{:S(2)}, u32[]{:S(2)}) collective-permute-start(f32[384,256]{1,0:T(8,128)S(1)} %collective-permute-done.refs_1_), channel_id=1, source_target_pairs={{0,1},{1,0},{2,3},{3,2},{4,5},{5,4},{6,7},{7,6},{8,9},{9,8},{10,11... | collective-permute-start | bytes 1179656 | tf_op jit(solution)/shard_map/ppermute | solution.py:47
  27.4 5.8 %collective-permute-start.5 = (f32[320,256]{1,0:T(8,128)S(1)}, f32[320,256]{1,0:T(8,128)S(1)}, u32[]{:S(2)}, u32[]{:S(2)}) collective-permute-start(f32[320,256]{1,0:T(8,128)S(1)} %collective-permute-done.1.refs_2_), channel_id=1, source_target_pairs={{0,1},{1,0},{2,3},{3,2},{4,5},{5,4},{6,7},{7,6},{8,9},{9,8},{10,11... | collective-permute-start | bytes 983048 | tf_op jit(solution)/shard_map/ppermute | solution.py:47
  27.4 5.8 %collective-permute-start.6 = (f32[320,256]{1,0:T(8,128)S(1)}, f32[320,256]{1,0:T(8,128)S(1)}, u32[]{:S(2)}, u32[]{:S(2)}) collective-permute-start(f32[320,256]{1,0:T(8,128)S(1)} %collective-permute-done.2.refs_3_), channel_id=1, source_target_pairs={{0,1},{1,0},{2,3},{3,2},{4,5},{5,4},{6,7},{7,6},{8,9},{9,8},{10,11... | collective-permute-start | bytes 983048 | tf_op jit(solution)/shard_map/ppermute | solution.py:47
  32.6 14.3 %collective-permute-start.21 = (f32[256,256]{1,0:T(8,128)S(1)}, f32[256,256]{1,0:T(8,128)S(1)}, u32[]{:S(2)}, u32[]{:S(2)}) collective-permute-start(f32[256,256]{1,0:T(8,128)S(1)} %get-tuple-element.47.refs_0_), channel_id=1, source_target_pairs={{0,1},{1,0},{2,3},{3,2},{4,5},{5,4},{6,7},{7,6},{8,9},{9,8},{10,11... | collective-permute-start | bytes 786440 | tf_op jit(solution)/shard_map/ppermute | solution.py:47
  32.7 14.2 %collective-permute-start.22 = (f32[256,256]{1,0:T(8,128)S(1)}, f32[256,256]{1,0:T(8,128)S(1)}, u32[]{:S(2)}, u32[]{:S(2)}) collective-permute-start(f32[256,256]{1,0:T(8,128)S(1)} %collective-permute-done.18.refs_1_), channel_id=1, source_target_pairs={{0,1},{1,0},{2,3},{3,2},{4,5},{5,4},{6,7},{7,6},{8,9},{9,8},{10,11... | collective-permute-start | bytes 786440 | tf_op jit(solution)/shard_map/ppermute | solution.py:47
  33.2 13.7 %collective-permute-start.23 = (f32[256,256]{1,0:T(8,128)S(1)}, f32[256,256]{1,0:T(8,128)S(1)}, u32[]{:S(2)}, u32[]{:S(2)}) collective-permute-start(f32[256,256]{1,0:T(8,128)S(1)} %collective-permute-done.19.refs_2_), channel_id=1, source_target_pairs={{0,1},{1,0},{2,3},{3,2},{4,5},{5,4},{6,7},{7,6},{8,9},{9,8},{10,11... | collective-permute-start | bytes 786440 | tf_op jit(solution)/shard_map/ppermute | solution.py:47
  33.2 13.7 %collective-permute-start.24 = (f32[256,256]{1,0:T(8,128)S(1)}, f32[256,256]{1,0:T(8,128)S(1)}, u32[]{:S(2)}, u32[]{:S(2)}) collective-permute-start(f32[256,256]{1,0:T(8,128)S(1)} %collective-permute-done.20.refs_3_), channel_id=1, source_target_pairs={{0,1},{1,0},{2,3},{3,2},{4,5},{5,4},{6,7},{7,6},{8,9},{9,8},{10,11... | collective-permute-start | bytes 786440 | tf_op jit(solution)/shard_map/ppermute | solution.py:47
  33.7 5.6 %collective-permute-start.14 = (f32[8,256]{1,0:T(8,128)S(1)}, f32[8,256]{1,0:T(8,128)S(1)}, u32[]{:S(2)}, u32[]{:S(2)}) collective-permute-start(f32[8,256]{1,0:T(8,128)S(1)} %get-tuple-element.41.refs_3_), channel_id=1, source_target_pairs={{0,6},{1,7},{2,4},{3,5},{4,2},{5,3},{6,0},{7,1},{8,14},{9,15},{10,... | collective-permute-start | bytes 24584 | tf_op jit(solution)/shard_map/ppermute | solution.py:616
  45.4 7.9 %collective-permute-start.17 = (f32[3,64,256]{2,1,0:T(8,128)S(1)}, f32[3,64,256]{2,1,0:T(8,128)S(1)}, u32[]{:S(2)}, u32[]{:S(2)}) collective-permute-start(f32[3,64,256]{2,1,0:T(8,128)S(1)} %get-tuple-element.39.refs_1_), channel_id=1, source_target_pairs={{0,8},{8,16},{16,24},{24,0},{1,9},{9,17},{17,25},{25,1},{2,10},{10... | collective-permute-start | bytes 589832 | tf_op jit(solution)/shard_map/ppermute | solution.py:653
  53.3 13.7 %collective-permute-start.29 = (f32[3,64,256]{2,1,0:T(8,128)S(1)}, f32[3,64,256]{2,1,0:T(8,128)S(1)}, u32[]{:S(2)}, u32[]{:S(2)}) collective-permute-start(f32[3,64,256]{2,1,0:T(8,128)S(1)} %get-tuple-element.49), channel_id=1, source_target_pairs={{0,24},{8,0},{16,8},{24,16},{1,25},{9,1},{17,9},{25,17},{2,26},{10... | collective-permute-start | bytes 589832 | tf_op jit(solution)/shard_map/ppermute | solution.py:648
  67.0 29.0 %collective-permute-start.34 = (f32[3,64,256]{2,1,0:T(8,128)S(1)}, f32[3,64,256]{2,1,0:T(8,128)S(1)}, u32[]{:S(2)}, u32[]{:S(2)}) collective-permute-start(f32[3,64,256]{2,1,0:T(8,128)S(1)} %get-tuple-element.52), channel_id=1, source_target_pairs={{0,24},{8,0},{16,8},{24,16},{1,25},{9,1},{17,9},{25,17},{2,26},{10... | collective-permute-start | bytes 589832 | tf_op jit(solution)/shard_map/ppermute | solution.py:648
  69.5 29.8 %collective-permute-start.7 = (f32[192,256]{1,0:T(8,128)S(1)}, f32[192,256]{1,0:T(8,128)S(1)}, u32[]{:S(2)}, u32[]{:S(2)}) collective-permute-start(f32[192,256]{1,0:T(8,128)S(1)} %bitcast.5), channel_id=1, source_target_pairs={{0,2},{1,3},{2,0},{3,1},{4,6},{5,7},{6,4},{7,5},{8,10},{9,11},{10,... | collective-permute-start | bytes 589832 | tf_op jit(solution)/shard_map/ppermute | solution.py:609
  78.4 21.3 %collective-permute-start.8 = (f32[192,256]{1,0:T(8,128)S(1)}, f32[192,256]{1,0:T(8,128)S(1)}, u32[]{:S(2)}, u32[]{:S(2)}) collective-permute-start(f32[192,256]{1,0:T(8,128)S(1)} %bitcast.6), channel_id=1, source_target_pairs={{2,4},{3,5},{4,2},{5,3},{10,12},{11,13},{12,10},{13,11},{18,20},{1... | collective-permute-start | bytes 589832 | tf_op jit(solution)/shard_map/ppermute | solution.py:609
  79.1 27.0 %collective-permute-start.9 = (f32[192,256]{1,0:T(8,128)S(1)}, f32[192,256]{1,0:T(8,128)S(1)}, u32[]{:S(2)}, u32[]{:S(2)}) collective-permute-start(f32[192,256]{1,0:T(8,128)S(1)} %bitcast.7), channel_id=1, source_target_pairs={{2,6},{3,7},{4,0},{5,1},{10,14},{11,15},{12,8},{13,9},{18,22},{19,... | collective-permute-start | bytes 589832 | tf_op jit(solution)/shard_map/ppermute | solution.py:609
  84.4 5.5 %collective-permute-start.31 = (f32[8,256]{1,0:T(8,128)S(1)}, f32[8,256]{1,0:T(8,128)S(1)}, u32[]{:S(2)}, u32[]{:S(2)}) collective-permute-start(f32[8,256]{1,0:T(8,128)S(1)} %collective-permute-done.30.refs_7_.refs_11_), channel_id=1, source_target_pairs={{0,6},{1,7},{2,4},{3,5},{4,2},{5,3},{6,0},{7,1},{8,14},{9,15},{10,... | collective-permute-start | bytes 24584 | tf_op jit(solution)/shard_map/ppermute | solution.py:616
  96.0 15.5 %collective-permute-start.39 = (f32[3,64,256]{2,1,0:T(8,128)S(1)}, f32[3,64,256]{2,1,0:T(8,128)S(1)}, u32[]{:S(2)}, u32[]{:S(2)}) collective-permute-start(f32[3,64,256]{2,1,0:T(8,128)S(1)} %get-tuple-element.54), channel_id=1, source_target_pairs={{0,24},{8,0},{16,8},{24,16},{1,25},{9,1},{17,9},{25,17},{2,26},{10... | collective-permute-start | bytes 589832 | tf_op jit(solution)/shard_map/ppermute | solution.py:648
  99.2 12.4 %collective-permute-start.10 = (f32[192,256]{1,0:T(8,128)S(1)}, f32[192,256]{1,0:T(8,128)S(1)}, u32[]{:S(2)}, u32[]{:S(2)}) collective-permute-start(f32[192,256]{1,0:T(8,128)S(1)} %bitcast.8), channel_id=1, source_target_pairs={{0,1},{1,0},{2,3},{3,2},{4,5},{5,4},{6,7},{7,6},{8,9},{9,8},{10,11... | collective-permute-start | bytes 589832 | tf_op jit(solution)/shard_map/ppermute | solution.py:47
  99.2 13.2 %collective-permute-start.11 = (f32[192,256]{1,0:T(8,128)S(1)}, f32[192,256]{1,0:T(8,128)S(1)}, u32[]{:S(2)}, u32[]{:S(2)}) collective-permute-start(f32[192,256]{1,0:T(8,128)S(1)} %collective-permute-done.7.refs_1_), channel_id=1, source_target_pairs={{0,1},{1,0},{2,3},{3,2},{4,5},{5,4},{6,7},{7,6},{8,9},{9,8},{10,11... | collective-permute-start | bytes 589832 | tf_op jit(solution)/shard_map/ppermute | solution.py:47
  103.9 5.4 %collective-permute-start.36 = (f32[8,256]{1,0:T(8,128)S(1)}, f32[8,256]{1,0:T(8,128)S(1)}, u32[]{:S(2)}, u32[]{:S(2)}) collective-permute-start(f32[8,256]{1,0:T(8,128)S(1)} %collective-permute-done.35.refs_15_), channel_id=1, source_target_pairs={{0,6},{1,7},{2,4},{3,5},{4,2},{5,3},{6,0},{7,1},{8,14},{9,15},{10,... | collective-permute-start | bytes 24584 | tf_op jit(solution)/shard_map/ppermute | solution.py:616
  111.6 18.9 %collective-permute-start.40 = (f32[192,256]{1,0:T(8,128)S(1)}, f32[192,256]{1,0:T(8,128)S(1)}, u32[]{:S(2)}, u32[]{:S(2)}) collective-permute-start(f32[192,256]{1,0:T(8,128)S(1)} %shard_map.117.refs_8_), channel_id=1, source_target_pairs={{0,2},{1,3},{2,0},{3,1},{4,6},{5,7},{6,4},{7,5},{8,10},{9,11},{10,... | collective-permute-start | bytes 589832 | tf_op jit(solution)/shard_map/ppermute | solution.py:609
  111.7 18.9 %collective-permute-start.41 = (f32[192,256]{1,0:T(8,128)S(1)}, f32[192,256]{1,0:T(8,128)S(1)}, u32[]{:S(2)}, u32[]{:S(2)}) collective-permute-start(f32[192,256]{1,0:T(8,128)S(1)} %shard_map.117.refs_8_), channel_id=1, source_target_pairs={{2,4},{3,5},{4,2},{5,3},{10,12},{11,13},{12,10},{13,11},{18,20},{1... | collective-permute-start | bytes 589832 | tf_op jit(solution)/shard_map/ppermute | solution.py:609
  112.5 18.6 %collective-permute-start.42 = (f32[192,256]{1,0:T(8,128)S(1)}, f32[192,256]{1,0:T(8,128)S(1)}, u32[]{:S(2)}, u32[]{:S(2)}) collective-permute-start(f32[192,256]{1,0:T(8,128)S(1)} %shard_map.117.refs_8_), channel_id=1, source_target_pairs={{2,6},{3,7},{4,0},{5,1},{10,14},{11,15},{12,8},{13,9},{18,22},{19,... | collective-permute-start | bytes 589832 | tf_op jit(solution)/shard_map/ppermute | solution.py:609
  114.1 7.4 %collective-permute-start.48 = (f32[64,128]{1,0:T(8,128)S(1)}, f32[64,128]{1,0:T(8,128)S(1)}, u32[]{:S(2)}, u32[]{:S(2)}) collective-permute-start(f32[64,128]{1,0:T(8,128)S(1)} %get-tuple-element.57), channel_id=1, source_target_pairs={{0,6},{1,7},{2,4},{3,5},{4,2},{5,3},{6,0},{7,1},{8,14},{9,15},{10,... | collective-permute-start | bytes 98312 | tf_op jit(solution)/shard_map/ppermute | solution.py:609
  115.8 14.2 %collective-permute-start.47 = (f32[64,256]{1,0:T(8,128)S(1)}, f32[64,256]{1,0:T(8,128)S(1)}, u32[]{:S(2)}, u32[]{:S(2)}) collective-permute-start(f32[64,256]{1,0:T(8,128)S(1)} %get-tuple-element.56), channel_id=1, source_target_pairs={{0,2},{1,3},{2,0},{3,1},{4,6},{5,7},{6,4},{7,5},{8,10},{9,11},{10,... | collective-permute-start | bytes 196616 | tf_op jit(solution)/shard_map/ppermute | solution.py:609
  121.4 8.6 %collective-permute-start.49 = (f32[64,128]{1,0:T(8,128)S(1)}, f32[64,128]{1,0:T(8,128)S(1)}, u32[]{:S(2)}, u32[]{:S(2)}) collective-permute-start(f32[64,128]{1,0:T(8,128)S(1)} %get-tuple-element.58), channel_id=1, source_target_pairs={{0,4},{1,5},{2,6},{3,7},{4,0},{5,1},{6,2},{7,3},{8,12},{9,13},{10,... | collective-permute-start | bytes 98312 | tf_op jit(solution)/shard_map/ppermute | solution.py:609
  130.0 5.6 %collective-permute-start.43 = (f32[192,256]{1,0:T(8,128)S(1)}, f32[192,256]{1,0:T(8,128)S(1)}, u32[]{:S(2)}, u32[]{:S(2)}) collective-permute-start(f32[192,256]{1,0:T(8,128)S(1)} %shard_map.117.refs_8_), channel_id=1, source_target_pairs={{0,1},{1,0},{2,3},{3,2},{4,5},{5,4},{6,7},{7,6},{8,9},{9,8},{10,11... | collective-permute-start | bytes 589832 | tf_op jit(solution)/shard_map/ppermute | solution.py:47
  (27 other events, 185.7 us)

commit v2 on v1

--- a/solution.py
+++ b/solution.py
@@ -468,7 +468,7 @@
         c_first = p_mixed * gate * d_one + d_mixed * (d_two * t_first * gate + d_one * t_gate)
         d_pair += nn(halves(jnp.concatenate([c_first, c_gate])), key_cut)
         d_second += nn(halves(t_mixed), scaled_cut)
-    return [d_pair[:span] + straights[0], d_pair[span:] + straights[1], d_second + straights[2]]
+    return cots, [d_pair[:span] + straights[0], d_pair[span:] + straights[1], d_second + straights[2]]
 
 
 def first_body(source, *refs):
@@ -476,7 +476,7 @@
 
     @pl.when((lax.axis_index("block") == source) & in_chain())
     def _():
-        rows = section_rows(0, refs)
+        _, rows = section_rows(0, refs)
         for m in range(3):
             raw[m] = rows[m]
 
@@ -493,23 +493,8 @@
     @pl.when(active)
     def _():
         span = payload.shape[1]
-        rows = section_rows(1, refs)
+        _, rows = section_rows(1, refs)
         finish([row + applied[m * span : (m + 1) * span, :] for m, row in enumerate(rows)], earlier, payload, partial)
-
-
-def terms_body(count, *refs):
-    cot = refs[-1]
-    span = refs[0].shape[1]
-
-    @pl.when(~in_chain())
-    def _():
-        cot[...] = jnp.zeros(cot.shape, jnp.float32)
-
-    @pl.when(in_chain())
-    def _():
-        cots, _ = state_terms(*refs[:3], refs[3:7], refs[7 : 7 + 4 * count], refs[7 + 4 * count : 7 + 5 * count])
-        for m in range(3):
-            cot[m * span : (m + 1) * span, :] = cots[m]
 
 
 def final_body(count, *refs):
@@ -525,16 +510,21 @@
 
     @pl.when(in_chain())
     def _():
-        rows = [row + applied[m * span : (m + 1) * span, :] for m, row in enumerate(section_rows(count, refs))]
+        cots, rows = section_rows(count, refs)
+        for out in outs:
+            for m in range(3):
+                out[m * span : (m + 1) * span, :] = cots[m]
+        rows = [row + applied[m * span : (m + 1) * span, :] for m, row in enumerate(rows)]
         table[...] = jnp.concatenate(rows[:2]).T
+        for by, out in enumerate(outs):
+            start = jnp.bitwise_xor(chip, by) * 2 * depth
+            for core in range(2):
+                lanes = slice(core * 128, (core + 1) * 128)
+                out[3 * span : 3 * span + depth, lanes] = table[rows_at(start + core * depth, depth), :]
         low = chip == LOW
         upper, lower = rows[2][:depth], rows[2][depth:]
-        picks = jnp.where(low, lower, upper), jnp.where(low, upper, lower)
-        for by, out in enumerate(outs):
-            out[:, :128] = table[rows_at(jnp.bitwise_xor(chip, by) * 2 * depth, 2 * depth), :]
-        for out, pick in zip(outs, picks):
-            out[:depth, 128:] = pick[:, :128]
-            out[depth:, 128:] = pick[:, 128:]
+        outs[0][3 * span + depth :] = jnp.where(low, lower, upper)
+        outs[1][3 * span + depth :] = jnp.where(low, upper, lower)
 
 
 def joined(refs):
@@ -564,12 +554,11 @@
 
 def token_body(keys, values, rates, *refs):
     weights, cots = joined(refs[:8]), joined(refs[8:16])
-    d_keys, d_values, d_rates, d_rows = refs[24:]
+    d_keys, d_values, d_rates, d_rows = refs[16:]
     width = keys.shape[1]
     span = width // len(weights)
     one, three, two = [load_halves(weights, part, span) for part in range(3)]
     c_one, c_three, c_two = [load_halves(cots, part, span) for part in range(3)]
-    ends = [taken(pair, slice(None)) for pair in joined(refs[16:24])]
     rate = column(rates[...], width)
     key, scaled = halves(keys[...]), halves(-rate * values[...])
     first, gate = nt(key, one), nt(key, three)
@@ -589,10 +578,12 @@
     d_rates[...] = -jnp.sum((values[...] * t_out).T, axis=0, keepdims=True)
     depth = d_rows.shape[1]
     low_side, upper_core = my_chip() <= LOW, my_core() == 0
+    block = slice(3 * span, 3 * span + depth)
     sides = []
-    for near, far in ((ends[0], ends[1]), (ends[2], ends[3])):
-        pair = jnp.where(low_side, near[:, :128], far), jnp.where(low_side, far, near[:, :128])
-        sides.append([jnp.where(upper_core, piece[:depth], piece[depth:]) for piece in pair])
+    for near, far in (cots[:2], cots[2:]):
+        near, far = taken(near, block), taken(far, block)
+        near, far = [jnp.where(upper_core, piece[:, :128], piece[:, 128:]) for piece in (near, far)]
+        sides.append([jnp.where(low_side, near, far), jnp.where(low_side, far, near)])
     by_core = [[jnp.where(upper_core, a, b) for a, b in zip(*sides)], [jnp.where(upper_core, b, a) for a, b in zip(*sides)]]
     for m in range(2):
         parts = []
@@ -602,7 +593,7 @@
                     start = (2 * m + i) * depth
                     parts.append(by_core[core][side][:, start : start + depth])
         d_rows[m] = jnp.concatenate(parts, axis=1)
-    d_rows[2] = jnp.concatenate([ends[0][:depth, 128:], ends[0][depth:, 128:]], axis=1)
+    d_rows[2] = taken(cots[0], slice(3 * span + depth, None))
 
 
 def by_xor(array, by, chips):
@@ -638,9 +629,16 @@
     return both_cores([arrays[0], *hops(arrays, ALL, OUTER, MIDDLE)])
 
 
-def from_chain(arrays, whole):
-    near, far, across = hops(arrays, ALL, ALL if whole else MIDDLE, ALL if whole else MIDDLE)
+def from_chain(arrays):
+    near, far, across = hops(arrays, ALL, MIDDLE, MIDDLE)
     return both_cores([arrays[0], near, across, far])
+
+
+def from_chain_relayed(array):
+    near = by_xor(array, 1, ALL)
+    across = by_xor(array, 3, MIDDLE)
+    far = by_xor(across, 1, ALL)
+    return both_cores([array, near, across, far])
 
 
 def to_earlier(array):
@@ -684,7 +682,7 @@
     )
     all_sums = exchanged(sums)
     earlier = to_later(shifted)
-    weights = from_chain([own.reshape(3 * span, width)] * CHIPS, False)
+    weights = from_chain_relayed(own.reshape(3 * span, width))
 
     inners, arrived = [], []
     common = [own, shifted, last, *all_sums]
@@ -704,18 +702,17 @@
         arrived.append(to_earlier(payload))
         inners += exchanged(straight)
     received = [*common, *inners, *arrived]
-    (cot,) = kernel_call(functools.partial(terms_body, groups - 1), [wide], *received)
-    cots = from_chain([cot] * CHIPS, False)
+    long, short = f32(4 * span, width), f32(3 * span + rows, width)
     ends = kernel_call(
         functools.partial(final_body, groups - 1),
-        [f32(2 * rows, width)] * 2 + [f32(2 * rows, 128)] * 2,
+        [long, long, short, short],
         *received,
         *halved,
         kept,
         applied,
         scratch=[pltpu.VMEM((width, 128), jnp.float32)],
     )
-    end_pieces = from_chain(ends, True)
+    cots = from_chain(ends)
     (d_queries,) = kernel_call(query_body, [square], queries, out_cot, *weights, spill=True)
     d_keys, d_values, d_rates, d_rows = kernel_call(
         token_body,
@@ -725,7 +722,6 @@
         rates_row,
         *weights,
         *cots,
-        *end_pieces,
         spill=True,
     )
     return (d_queries, d_keys, d_values, d_rates.reshape(depth), d_rows[None])

time: 139 us -> 131 us (0.942)
  starting transfers between devices: 69.7 us -> 53.9 us
  waiting for transfers between devices: 61.6 us -> 71.1 us
    ppermute x15 -> x12, starting transfers between devices: 39.4 us -> 24.9 us  [by_xor(): lax.ppermute(array, 'tok', [(2 * a + core, 2 * (a ^ by) + core) for a in...]
    ppermute x15 -> x12, waiting for transfers between devices: 19 us -> 29.9 us  [by_xor(): lax.ppermute(array, 'tok', [(2 * a + core, 2 * (a ^ by) + core) for a in...]
    ppermute x6, starting transfers between devices: 11.5 us -> 9.19 us  [to_earlier(): lax.ppermute(array, 'block', [(i, (i - 1) % groups) for i in range(groups)])]
    ppermute x12, starting transfers between devices: 12.3 us -> 14.4 us  [exchanged(): lax.ppermute(array, 'tok', [(j, j ^ bits) for j in range(size)])]
    ppermute x12, waiting for transfers between devices: 25.4 us -> 23.5 us  [exchanged(): lax.ppermute(array, 'tok', [(j, j ^ bits) for j in range(size)])]
    ppermute x20 -> x16, starting transfers between devices: 5.1 us -> 3.92 us  [core_swap(): return lax.ppermute(array, 'tok', [(j, j ^ 1) for j in range(size)])]
    pallas_call x10 -> x9, Pallas kernels: 5.58 us -> 5.34 us  [kernel_call(): pl.pallas_call(body, in_specs=[pl.BlockSpec(memory_space=space) for _ in...]
  transfers between devices with their start and end apart: 54 -> 47, of which waited for: 21 -> 20; matrix products, arithmetic and copies ran while one was open for 0% -> 0% of each run, Pallas kernels for 1% -> 1%
where the time goes in v2:
time: 131 us
  waiting for transfers between devices  71.1 us (54%)
  starting transfers between devices  53.9 us (41%)
  Pallas kernels  5.34 us (4%)
    ppermute x12, waiting for transfers between devices, by_xor(): lax.ppermute(array, 'tok', [(2 * a + core, 2 * (a ^ by) + core) for a in...  29.9 us
    ppermute x12, starting transfers between devices, by_xor(): lax.ppermute(array, 'tok', [(2 * a + core, 2 * (a ^ by) + core) for a in...  24.9 us
    ppermute x12, waiting for transfers between devices, exchanged(): lax.ppermute(array, 'tok', [(j, j ^ bits) for j in range(size)])  23.5 us
    ppermute x12, starting transfers between devices, exchanged(): lax.ppermute(array, 'tok', [(j, j ^ bits) for j in range(size)])  14.4 us
    ppermute x6, waiting for transfers between devices, to_earlier(): lax.ppermute(array, 'block', [(i, (i - 1) % groups) for i in range(groups)])  9.91 us
    ppermute x6, starting transfers between devices, to_earlier(): lax.ppermute(array, 'block', [(i, (i - 1) % groups) for i in range(groups)])  9.19 us
    ppermute x1, waiting for transfers between devices, to_later(): lax.ppermute(array, 'block', [(i, (i + 1) % groups) for i in range(groups)])  6.36 us
    pallas_call x9, Pallas kernels, kernel_call(): pl.pallas_call(body, in_specs=[pl.BlockSpec(memory_space=space) for _ in...  5.34 us
  transfers between devices with their start and end apart: 47, of which 20 were waited for; matrix products, arithmetic and copies ran while one was open for 0% of the time, Pallas kernels for 1%

profile of v2, /device:TPU:0, one launch (start us, length us, event | category | flops | bytes accessed | tf_op | source)
XLA Modules:
  0.0 131.2 jit_solution(163433297802524554)
XLA Ops:
  0.6 1.5 %shard_map.110 = (f32[384,256]{1,0:T(8,128)S(1)}, f32[384,256]{1,0:T(8,128)S(1)}, f32[320,256]{1,0:T(8,128)S(1)}, f32[320,256]{1,0:T(8,128)S(1)}, f32[256,256]{1,0:T(8,128)S(1)}) custom-call(f32[128,256]{1,0:T(8,128)} %keys.1, f32[128,256]{1,0:T(8,128)} %values.1, f32[1,128]{1,0:T(1,128)} %bitcast.10, f32[3,32,256]{2,1,0:T(8,128)} %bitcast.12, ...), custom_call_target="tpu_custom_call" | custom-call | tf_op jit(solution)/shard_map/pallas_call | solution.py:236
  2.1 3.1 %collective-permute-start = (f32[384,256]{1,0:T(8,128)S(1)}, f32[384,256]{1,0:T(8,128)S(1)}, u32[]{:S(2)}, u32[]{:S(2)}) collective-permute-start(f32[384,256]{1,0:T(8,128)S(1)} %get-tuple-element.35), channel_id=1, source_target_pairs={{0,2},{1,3},{2,0},{3,1},{4,6},{5,7},{6,4},{7,5},{8,10},{9,11},{10,... | collective-permute-start | bytes 1179656 | tf_op jit(solution)/shard_map/ppermute | solution.py:600
  5.3 4.9 %collective-permute-start.1 = (f32[320,256]{1,0:T(8,128)S(1)}, f32[320,256]{1,0:T(8,128)S(1)}, u32[]{:S(2)}, u32[]{:S(2)}) collective-permute-start(f32[320,256]{1,0:T(8,128)S(1)} %get-tuple-element.36), channel_id=1, source_target_pairs={{0,4},{1,5},{6,2},{7,3},{8,12},{9,13},{14,10},{15,11},{16,20},{17,... | collective-permute-start | bytes 983048 | tf_op jit(solution)/shard_map/ppermute | solution.py:600
  10.9 3.0 %collective-permute-start.19 = (f32[256,256]{1,0:T(8,128)S(1)}, f32[256,256]{1,0:T(8,128)S(1)}, u32[]{:S(2)}, u32[]{:S(2)}) collective-permute-start(f32[256,256]{1,0:T(8,128)S(1)} %get-tuple-element.47.refs_0_), channel_id=1, source_target_pairs={{0,4},{1,5},{6,2},{7,3},{8,12},{9,13},{14,10},{15,11},{16,20},{17,... | collective-permute-start | bytes 786440 | tf_op jit(solution)/shard_map/ppermute | solution.py:600
  13.9 6.5 %collective-permute-done.18.refs_1_ = f32[256,256]{1,0:T(8,128)S(1)} collective-permute-done((f32[256,256]{1,0:T(8,128)S(1)}, f32[256,256]{1,0:T(8,128)S(1)}, u32[]{:S(2)}, u32[]{:S(2)}) %collective-permute-start.18) | collective-permute-done | bytes 262176 | tf_op jit(solution)/shard_map/ppermute | solution.py:600
  20.9 6.5 %collective-permute-done.1.refs_2_ = f32[320,256]{1,0:T(8,128)S(1)} collective-permute-done((f32[320,256]{1,0:T(8,128)S(1)}, f32[320,256]{1,0:T(8,128)S(1)}, u32[]{:S(2)}, u32[]{:S(2)}) %collective-permute-start.1) | collective-permute-done | bytes 327712 | tf_op jit(solution)/shard_map/ppermute | solution.py:600
  27.9 4.0 %collective-permute-done.19.refs_2_ = f32[256,256]{1,0:T(8,128)S(1)} collective-permute-done((f32[256,256]{1,0:T(8,128)S(1)}, f32[256,256]{1,0:T(8,128)S(1)}, u32[]{:S(2)}, u32[]{:S(2)}) %collective-permute-start.19) | collective-permute-done | bytes 262176 | tf_op jit(solution)/shard_map/ppermute | solution.py:600
  33.7 2.5 %collective-permute-start.14 = (f32[8,256]{1,0:T(8,128)S(1)}, f32[8,256]{1,0:T(8,128)S(1)}, u32[]{:S(2)}, u32[]{:S(2)}) collective-permute-start(f32[8,256]{1,0:T(8,128)S(1)} %get-tuple-element.41.refs_3_), channel_id=1, source_target_pairs={{0,6},{1,7},{2,4},{3,5},{4,2},{5,3},{6,0},{7,1},{8,14},{9,15},{10,... | collective-permute-start | bytes 24584 | tf_op jit(solution)/shard_map/ppermute | solution.py:607
  36.2 3.1 %collective-permute-done.14.refs_4_ = f32[8,256]{1,0:T(8,128)S(1)} collective-permute-done((f32[8,256]{1,0:T(8,128)S(1)}, f32[8,256]{1,0:T(8,128)S(1)}, u32[]{:S(2)}, u32[]{:S(2)}) %collective-permute-start.14) | collective-permute-done | bytes 8224 | tf_op jit(solution)/shard_map/ppermute | solution.py:607
  40.3 3.9 %collective-permute-done.15.refs_5_ = f32[8,256]{1,0:T(8,128)S(1)} collective-permute-done((f32[8,256]{1,0:T(8,128)S(1)}, f32[8,256]{1,0:T(8,128)S(1)}, u32[]{:S(2)}, u32[]{:S(2)}) %collective-permute-start.15) | collective-permute-done | bytes 8224 | tf_op jit(solution)/shard_map/ppermute | solution.py:607
  45.4 1.5 %collective-permute-start.17 = (f32[3,64,256]{2,1,0:T(8,128)S(1)}, f32[3,64,256]{2,1,0:T(8,128)S(1)}, u32[]{:S(2)}, u32[]{:S(2)}) collective-permute-start(f32[3,64,256]{2,1,0:T(8,128)S(1)} %get-tuple-element.39.refs_1_), channel_id=1, source_target_pairs={{0,8},{8,16},{16,24},{24,0},{1,9},{9,17},{17,25},{25,1},{2,10},{10... | collective-permute-start | bytes 589832 | tf_op jit(solution)/shard_map/ppermute | solution.py:651
  46.9 6.4 %collective-permute-done.17.earlier.refs_18_ = f32[3,64,256]{2,1,0:T(8,128)S(1)} collective-permute-done((f32[3,64,256]{2,1,0:T(8,128)S(1)}, f32[3,64,256]{2,1,0:T(8,128)S(1)}, u32[]{:S(2)}, u32[]{:S(2)}) %collective-permute-start.17) | collective-permute-done | bytes 196640 | tf_op jit(solution)/shard_map/ppermute | solution.py:651
  53.3 1.6 %collective-permute-start.29 = (f32[3,64,256]{2,1,0:T(8,128)S(1)}, f32[3,64,256]{2,1,0:T(8,128)S(1)}, u32[]{:S(2)}, u32[]{:S(2)}) collective-permute-start(f32[3,64,256]{2,1,0:T(8,128)S(1)} %get-tuple-element.49), channel_id=1, source_target_pairs={{0,24},{8,0},{16,8},{24,16},{1,25},{9,1},{17,9},{25,17},{2,26},{10... | collective-permute-start | bytes 589832 | tf_op jit(solution)/shard_map/ppermute | solution.py:646
  56.3 3.3 %collective-permute-done.25.refs_7_ = f32[8,256]{1,0:T(8,128)S(1)} collective-permute-done((f32[8,256]{1,0:T(8,128)S(1)}, f32[8,256]{1,0:T(8,128)S(1)}, u32[]{:S(2)}, u32[]{:S(2)}) %collective-permute-start.25) | collective-permute-done | bytes 8224 | tf_op jit(solution)/shard_map/ppermute | solution.py:646
  59.6 2.5 %collective-permute-start.26 = (f32[8,256]{1,0:T(8,128)S(1)}, f32[8,256]{1,0:T(8,128)S(1)}, u32[]{:S(2)}, u32[]{:S(2)}) collective-permute-start(f32[8,256]{1,0:T(8,128)S(1)} %collective-permute-done.25.refs_7_), channel_id=1, source_target_pairs={{0,6},{1,7},{2,4},{3,5},{4,2},{5,3},{6,0},{7,1},{8,14},{9,15},{10,... | collective-permute-start | bytes 24584 | tf_op jit(solution)/shard_map/ppermute | solution.py:607
  62.1 1.5 %collective-permute-start.28 = (f32[8,256]{1,0:T(8,128)S(1)}, f32[8,256]{1,0:T(8,128)S(1)}, u32[]{:S(2)}, u32[]{:S(2)}) collective-permute-start(f32[8,256]{1,0:T(8,128)S(1)} %collective-permute-done.25.refs_7_), channel_id=1, source_target_pairs={{0,1},{1,0},{2,3},{3,2},{4,5},{5,4},{6,7},{7,6},{8,9},{9,8},{10,11... | collective-permute-start | bytes 24584 | tf_op jit(solution)/shard_map/ppermute | solution.py:607
  63.6 1.5 %collective-permute-done.26.refs_8_ = f32[8,256]{1,0:T(8,128)S(1)} collective-permute-done((f32[8,256]{1,0:T(8,128)S(1)}, f32[8,256]{1,0:T(8,128)S(1)}, u32[]{:S(2)}, u32[]{:S(2)}) %collective-permute-start.26) | collective-permute-done | bytes 8224 | tf_op jit(solution)/shard_map/ppermute | solution.py:607
  65.1 1.9 %collective-permute-done.27.refs_9_ = f32[8,256]{1,0:T(8,128)S(1)} collective-permute-done((f32[8,256]{1,0:T(8,128)S(1)}, f32[8,256]{1,0:T(8,128)S(1)}, u32[]{:S(2)}, u32[]{:S(2)}) %collective-permute-start.27) | collective-permute-done | bytes 8224 | tf_op jit(solution)/shard_map/ppermute | solution.py:607
  67.0 2.5 %collective-permute-start.34 = (f32[3,64,256]{2,1,0:T(8,128)S(1)}, f32[3,64,256]{2,1,0:T(8,128)S(1)}, u32[]{:S(2)}, u32[]{:S(2)}) collective-permute-start(f32[3,64,256]{2,1,0:T(8,128)S(1)} %get-tuple-element.52), channel_id=1, source_target_pairs={{0,24},{8,0},{16,8},{24,16},{1,25},{9,1},{17,9},{25,17},{2,26},{10... | collective-permute-start | bytes 589832 | tf_op jit(solution)/shard_map/ppermute | solution.py:646
  70.7 3.1 %collective-permute-done.30.refs_7_.refs_11_ = f32[8,256]{1,0:T(8,128)S(1)} collective-permute-done((f32[8,256]{1,0:T(8,128)S(1)}, f32[8,256]{1,0:T(8,128)S(1)}, u32[]{:S(2)}, u32[]{:S(2)}) %collective-permute-start.30) | collective-permute-done | bytes 8224 | tf_op jit(solution)/shard_map/ppermute | solution.py:646
  75.2 2.6 %collective-permute-start.33 = (f32[8,256]{1,0:T(8,128)S(1)}, f32[8,256]{1,0:T(8,128)S(1)}, u32[]{:S(2)}, u32[]{:S(2)}) collective-permute-start(f32[8,256]{1,0:T(8,128)S(1)} %collective-permute-done.30.refs_7_.refs_11_), channel_id=1, source_target_pairs={{0,1},{1,0},{2,3},{3,2},{4,5},{5,4},{6,7},{7,6},{8,9},{9,8},{10,11... | collective-permute-start | bytes 24584 | tf_op jit(solution)/shard_map/ppermute | solution.py:607
  77.8 1.5 %collective-permute-done.31.refs_8_.refs_12_ = f32[8,256]{1,0:T(8,128)S(1)} collective-permute-done((f32[8,256]{1,0:T(8,128)S(1)}, f32[8,256]{1,0:T(8,128)S(1)}, u32[]{:S(2)}, u32[]{:S(2)}) %collective-permute-start.31) | collective-permute-done | bytes 8224 | tf_op jit(solution)/shard_map/ppermute | solution.py:607
  80.1 2.9 %collective-permute-start.39 = (f32[3,64,256]{2,1,0:T(8,128)S(1)}, f32[3,64,256]{2,1,0:T(8,128)S(1)}, u32[]{:S(2)}, u32[]{:S(2)}) collective-permute-start(f32[3,64,256]{2,1,0:T(8,128)S(1)} %get-tuple-element.54), channel_id=1, source_target_pairs={{0,24},{8,0},{16,8},{24,16},{1,25},{9,1},{17,9},{25,17},{2,26},{10... | collective-permute-start | bytes 589832 | tf_op jit(solution)/shard_map/ppermute | solution.py:646
  83.0 9.8 %collective-permute-start.7 = (f32[192,256]{1,0:T(8,128)S(1)}, f32[192,256]{1,0:T(8,128)S(1)}, u32[]{:S(2)}, u32[]{:S(2)}) collective-permute-start(f32[192,256]{1,0:T(8,128)S(1)} %bitcast.6), channel_id=1, source_target_pairs={{0,2},{1,3},{2,0},{3,1},{4,6},{5,7},{6,4},{7,5},{8,10},{9,11},{10,... | collective-permute-start | bytes 589832 | tf_op jit(solution)/shard_map/ppermute | solution.py:600
  93.1 3.5 %collective-permute-done.35.refs_15_ = f32[8,256]{1,0:T(8,128)S(1)} collective-permute-done((f32[8,256]{1,0:T(8,128)S(1)}, f32[8,256]{1,0:T(8,128)S(1)}, u32[]{:S(2)}, u32[]{:S(2)}) %collective-permute-start.35) | collective-permute-done | bytes 8224 | tf_op jit(solution)/shard_map/ppermute | solution.py:646
  96.5 2.2 %collective-permute-start.36 = (f32[8,256]{1,0:T(8,128)S(1)}, f32[8,256]{1,0:T(8,128)S(1)}, u32[]{:S(2)}, u32[]{:S(2)}) collective-permute-start(f32[8,256]{1,0:T(8,128)S(1)} %collective-permute-done.35.refs_15_), channel_id=1, source_target_pairs={{0,6},{1,7},{2,4},{3,5},{4,2},{5,3},{6,0},{7,1},{8,14},{9,15},{10,... | collective-permute-start | bytes 24584 | tf_op jit(solution)/shard_map/ppermute | solution.py:607
  98.8 4.4 %collective-permute-done.36.refs_16_ = f32[8,256]{1,0:T(8,128)S(1)} collective-permute-done((f32[8,256]{1,0:T(8,128)S(1)}, f32[8,256]{1,0:T(8,128)S(1)}, u32[]{:S(2)}, u32[]{:S(2)}) %collective-permute-start.36) | collective-permute-done | bytes 8224 | tf_op jit(solution)/shard_map/ppermute | solution.py:607
  103.9 4.2 %collective-permute-done.37.refs_17_ = f32[8,256]{1,0:T(8,128)S(1)} collective-permute-done((f32[8,256]{1,0:T(8,128)S(1)}, f32[8,256]{1,0:T(8,128)S(1)}, u32[]{:S(2)}, u32[]{:S(2)}) %collective-permute-start.37) | collective-permute-done | bytes 8224 | tf_op jit(solution)/shard_map/ppermute | solution.py:607
  112.2 5.6 %collective-permute-done.40.refs_9_ = f32[256,256]{1,0:T(8,128)S(1)} collective-permute-done((f32[256,256]{1,0:T(8,128)S(1)}, f32[256,256]{1,0:T(8,128)S(1)}, u32[]{:S(2)}, u32[]{:S(2)}) %collective-permute-start.40) | collective-permute-done | bytes 262176 | tf_op jit(solution)/shard_map/ppermute | solution.py:600
  118.3 7.4 %collective-permute-done.42.refs_11_ = f32[224,256]{1,0:T(8,128)S(1)} collective-permute-done((f32[224,256]{1,0:T(8,128)S(1)}, f32[224,256]{1,0:T(8,128)S(1)}, u32[]{:S(2)}, u32[]{:S(2)}) %collective-permute-start.42) | collective-permute-done | bytes 229408 | tf_op jit(solution)/shard_map/ppermute | solution.py:600
  127.5 1.5 %shard_map.112 = f32[128,256]{1,0:T(8,128)} custom-call(f32[128,256]{1,0:T(8,128)S(1)} %copy-done.2, f32[128,256]{1,0:T(8,128)S(1)} %copy-done.3, f32[192,256]{1,0:T(8,128)S(1)} %bitcast.8, f32[192,256]{1,0:T(8,128)S(1)} %collective-permute-done.7.refs_1_, f32[192,256]{1,0:T(8,128)S(1)} %collective-permute-done.8.refs_2_, ...), custom_call_target="tpu_custom_call" | custom-call | tf_op jit(solution)/shard_map/pallas_call | solution.py:236
  129.0 2.2 %shard_map.118 = (f32[128,256]{1,0:T(8,128)}, f32[128,256]{1,0:T(8,128)}, f32[1,128]{1,0:T(1,128)}, f32[3,32,256]{2,1,0:T(8,128)}) custom-call(f32[128,256]{1,0:T(8,128)S(1)} %copy-done, f32[128,256]{1,0:T(8,128)S(1)} %copy-done.1, f32[1,128]{1,0:T(1,128)S(1)} %bitcast.11, f32[192,256]{1,0:T(8,128)S(1)} %bitcast.9, ...), custom_call_target="tpu_custom_call" | custom-call | tf_op jit(solution)/shard_map/pallas_call | solution.py:236
  (81 shorter events, 18.0 us)
Async XLA Ops:
  2.1 18.2 %collective-permute-start = (f32[384,256]{1,0:T(8,128)S(1)}, f32[384,256]{1,0:T(8,128)S(1)}, u32[]{:S(2)}, u32[]{:S(2)}) collective-permute-start(f32[384,256]{1,0:T(8,128)S(1)} %get-tuple-element.35), channel_id=1, source_target_pairs={{0,2},{1,3},{2,0},{3,1},{4,6},{5,7},{6,4},{7,5},{8,10},{9,11},{10,... | collective-permute-start | bytes 1179656 | tf_op jit(solution)/shard_map/ppermute | solution.py:600
  5.3 15.1 %collective-permute-start.18 = (f32[256,256]{1,0:T(8,128)S(1)}, f32[256,256]{1,0:T(8,128)S(1)}, u32[]{:S(2)}, u32[]{:S(2)}) collective-permute-start(f32[256,256]{1,0:T(8,128)S(1)} %get-tuple-element.47.refs_0_), channel_id=1, source_target_pairs={{0,2},{1,3},{2,0},{3,1},{4,6},{5,7},{6,4},{7,5},{8,10},{9,11},{10,... | collective-permute-start | bytes 786440 | tf_op jit(solution)/shard_map/ppermute | solution.py:600
  5.3 22.1 %collective-permute-start.1 = (f32[320,256]{1,0:T(8,128)S(1)}, f32[320,256]{1,0:T(8,128)S(1)}, u32[]{:S(2)}, u32[]{:S(2)}) collective-permute-start(f32[320,256]{1,0:T(8,128)S(1)} %get-tuple-element.36), channel_id=1, source_target_pairs={{0,4},{1,5},{6,2},{7,3},{8,12},{9,13},{14,10},{15,11},{16,20},{17,... | collective-permute-start | bytes 983048 | tf_op jit(solution)/shard_map/ppermute | solution.py:600
  10.2 17.2 %collective-permute-start.2 = (f32[320,256]{1,0:T(8,128)S(1)}, f32[320,256]{1,0:T(8,128)S(1)}, u32[]{:S(2)}, u32[]{:S(2)}) collective-permute-start(f32[320,256]{1,0:T(8,128)S(1)} %get-tuple-element.37), channel_id=1, source_target_pairs={{2,4},{3,5},{4,2},{5,3},{10,12},{11,13},{12,10},{13,11},{18,20},{1... | collective-permute-start | bytes 983048 | tf_op jit(solution)/shard_map/ppermute | solution.py:600
  10.9 21.0 %collective-permute-start.19 = (f32[256,256]{1,0:T(8,128)S(1)}, f32[256,256]{1,0:T(8,128)S(1)}, u32[]{:S(2)}, u32[]{:S(2)}) collective-permute-start(f32[256,256]{1,0:T(8,128)S(1)} %get-tuple-element.47.refs_0_), channel_id=1, source_target_pairs={{0,4},{1,5},{6,2},{7,3},{8,12},{9,13},{14,10},{15,11},{16,20},{17,... | collective-permute-start | bytes 786440 | tf_op jit(solution)/shard_map/ppermute | solution.py:600
  20.4 12.3 %collective-permute-start.3 = (f32[384,256]{1,0:T(8,128)S(1)}, f32[384,256]{1,0:T(8,128)S(1)}, u32[]{:S(2)}, u32[]{:S(2)}) collective-permute-start(f32[384,256]{1,0:T(8,128)S(1)} %get-tuple-element.34.refs_0_), channel_id=1, source_target_pairs={{0,1},{1,0},{2,3},{3,2},{4,5},{5,4},{6,7},{7,6},{8,9},{9,8},{10,11... | collective-permute-start | bytes 1179656 | tf_op jit(solution)/shard_map/ppermute | solution.py:47
  20.4 13.3 %collective-permute-start.4 = (f32[384,256]{1,0:T(8,128)S(1)}, f32[384,256]{1,0:T(8,128)S(1)}, u32[]{:S(2)}, u32[]{:S(2)}) collective-permute-start(f32[384,256]{1,0:T(8,128)S(1)} %collective-permute-done.refs_1_), channel_id=1, source_target_pairs={{0,1},{1,0},{2,3},{3,2},{4,5},{5,4},{6,7},{7,6},{8,9},{9,8},{10,11... | collective-permute-start | bytes 1179656 | tf_op jit(solution)/shard_map/ppermute | solution.py:47
  27.4 5.8 %collective-permute-start.5 = (f32[320,256]{1,0:T(8,128)S(1)}, f32[320,256]{1,0:T(8,128)S(1)}, u32[]{:S(2)}, u32[]{:S(2)}) collective-permute-start(f32[320,256]{1,0:T(8,128)S(1)} %collective-permute-done.1.refs_2_), channel_id=1, source_target_pairs={{0,1},{1,0},{2,3},{3,2},{4,5},{5,4},{6,7},{7,6},{8,9},{9,8},{10,11... | collective-permute-start | bytes 983048 | tf_op jit(solution)/shard_map/ppermute | solution.py:47
  27.4 5.8 %collective-permute-start.6 = (f32[320,256]{1,0:T(8,128)S(1)}, f32[320,256]{1,0:T(8,128)S(1)}, u32[]{:S(2)}, u32[]{:S(2)}) collective-permute-start(f32[320,256]{1,0:T(8,128)S(1)} %collective-permute-done.2.refs_3_), channel_id=1, source_target_pairs={{0,1},{1,0},{2,3},{3,2},{4,5},{5,4},{6,7},{7,6},{8,9},{9,8},{10,11... | collective-permute-start | bytes 983048 | tf_op jit(solution)/shard_map/ppermute | solution.py:47
  32.6 14.3 %collective-permute-start.21 = (f32[256,256]{1,0:T(8,128)S(1)}, f32[256,256]{1,0:T(8,128)S(1)}, u32[]{:S(2)}, u32[]{:S(2)}) collective-permute-start(f32[256,256]{1,0:T(8,128)S(1)} %get-tuple-element.47.refs_0_), channel_id=1, source_target_pairs={{0,1},{1,0},{2,3},{3,2},{4,5},{5,4},{6,7},{7,6},{8,9},{9,8},{10,11... | collective-permute-start | bytes 786440 | tf_op jit(solution)/shard_map/ppermute | solution.py:47
  32.7 14.2 %collective-permute-start.22 = (f32[256,256]{1,0:T(8,128)S(1)}, f32[256,256]{1,0:T(8,128)S(1)}, u32[]{:S(2)}, u32[]{:S(2)}) collective-permute-start(f32[256,256]{1,0:T(8,128)S(1)} %collective-permute-done.18.refs_1_), channel_id=1, source_target_pairs={{0,1},{1,0},{2,3},{3,2},{4,5},{5,4},{6,7},{7,6},{8,9},{9,8},{10,11... | collective-permute-start | bytes 786440 | tf_op jit(solution)/shard_map/ppermute | solution.py:47
  33.2 13.7 %collective-permute-start.23 = (f32[256,256]{1,0:T(8,128)S(1)}, f32[256,256]{1,0:T(8,128)S(1)}, u32[]{:S(2)}, u32[]{:S(2)}) collective-permute-start(f32[256,256]{1,0:T(8,128)S(1)} %collective-permute-done.19.refs_2_), channel_id=1, source_target_pairs={{0,1},{1,0},{2,3},{3,2},{4,5},{5,4},{6,7},{7,6},{8,9},{9,8},{10,11... | collective-permute-start | bytes 786440 | tf_op jit(solution)/shard_map/ppermute | solution.py:47
  33.2 13.7 %collective-permute-start.24 = (f32[256,256]{1,0:T(8,128)S(1)}, f32[256,256]{1,0:T(8,128)S(1)}, u32[]{:S(2)}, u32[]{:S(2)}) collective-permute-start(f32[256,256]{1,0:T(8,128)S(1)} %collective-permute-done.20.refs_3_), channel_id=1, source_target_pairs={{0,1},{1,0},{2,3},{3,2},{4,5},{5,4},{6,7},{7,6},{8,9},{9,8},{10,11... | collective-permute-start | bytes 786440 | tf_op jit(solution)/shard_map/ppermute | solution.py:47
  33.7 5.6 %collective-permute-start.14 = (f32[8,256]{1,0:T(8,128)S(1)}, f32[8,256]{1,0:T(8,128)S(1)}, u32[]{:S(2)}, u32[]{:S(2)}) collective-permute-start(f32[8,256]{1,0:T(8,128)S(1)} %get-tuple-element.41.refs_3_), channel_id=1, source_target_pairs={{0,6},{1,7},{2,4},{3,5},{4,2},{5,3},{6,0},{7,1},{8,14},{9,15},{10,... | collective-permute-start | bytes 24584 | tf_op jit(solution)/shard_map/ppermute | solution.py:607
  45.4 7.9 %collective-permute-start.17 = (f32[3,64,256]{2,1,0:T(8,128)S(1)}, f32[3,64,256]{2,1,0:T(8,128)S(1)}, u32[]{:S(2)}, u32[]{:S(2)}) collective-permute-start(f32[3,64,256]{2,1,0:T(8,128)S(1)} %get-tuple-element.39.refs_1_), channel_id=1, source_target_pairs={{0,8},{8,16},{16,24},{24,0},{1,9},{9,17},{17,25},{25,1},{2,10},{10... | collective-permute-start | bytes 589832 | tf_op jit(solution)/shard_map/ppermute | solution.py:651
  53.3 13.7 %collective-permute-start.29 = (f32[3,64,256]{2,1,0:T(8,128)S(1)}, f32[3,64,256]{2,1,0:T(8,128)S(1)}, u32[]{:S(2)}, u32[]{:S(2)}) collective-permute-start(f32[3,64,256]{2,1,0:T(8,128)S(1)} %get-tuple-element.49), channel_id=1, source_target_pairs={{0,24},{8,0},{16,8},{24,16},{1,25},{9,1},{17,9},{25,17},{2,26},{10... | collective-permute-start | bytes 589832 | tf_op jit(solution)/shard_map/ppermute | solution.py:646
  59.6 5.4 %collective-permute-start.26 = (f32[8,256]{1,0:T(8,128)S(1)}, f32[8,256]{1,0:T(8,128)S(1)}, u32[]{:S(2)}, u32[]{:S(2)}) collective-permute-start(f32[8,256]{1,0:T(8,128)S(1)} %collective-permute-done.25.refs_7_), channel_id=1, source_target_pairs={{0,6},{1,7},{2,4},{3,5},{4,2},{5,3},{6,0},{7,1},{8,14},{9,15},{10,... | collective-permute-start | bytes 24584 | tf_op jit(solution)/shard_map/ppermute | solution.py:607
  67.0 13.1 %collective-permute-start.34 = (f32[3,64,256]{2,1,0:T(8,128)S(1)}, f32[3,64,256]{2,1,0:T(8,128)S(1)}, u32[]{:S(2)}, u32[]{:S(2)}) collective-permute-start(f32[3,64,256]{2,1,0:T(8,128)S(1)} %get-tuple-element.52), channel_id=1, source_target_pairs={{0,24},{8,0},{16,8},{24,16},{1,25},{9,1},{17,9},{25,17},{2,26},{10... | collective-permute-start | bytes 589832 | tf_op jit(solution)/shard_map/ppermute | solution.py:646
  69.5 23.3 %collective-permute-start.8 = (f32[192,256]{1,0:T(8,128)S(1)}, f32[192,256]{1,0:T(8,128)S(1)}, u32[]{:S(2)}, u32[]{:S(2)}) collective-permute-start(f32[192,256]{1,0:T(8,128)S(1)} %bitcast.5), channel_id=1, source_target_pairs={{2,4},{3,5},{4,2},{5,3},{10,12},{11,13},{12,10},{13,11},{18,20},{1... | collective-permute-start | bytes 589832 | tf_op jit(solution)/shard_map/ppermute | solution.py:600
  73.9 5.4 %collective-permute-start.31 = (f32[8,256]{1,0:T(8,128)S(1)}, f32[8,256]{1,0:T(8,128)S(1)}, u32[]{:S(2)}, u32[]{:S(2)}) collective-permute-start(f32[8,256]{1,0:T(8,128)S(1)} %collective-permute-done.30.refs_7_.refs_11_), channel_id=1, source_target_pairs={{0,6},{1,7},{2,4},{3,5},{4,2},{5,3},{6,0},{7,1},{8,14},{9,15},{10,... | collective-permute-start | bytes 24584 | tf_op jit(solution)/shard_map/ppermute | solution.py:607
  80.1 29.1 %collective-permute-start.39 = (f32[3,64,256]{2,1,0:T(8,128)S(1)}, f32[3,64,256]{2,1,0:T(8,128)S(1)}, u32[]{:S(2)}, u32[]{:S(2)}) collective-permute-start(f32[3,64,256]{2,1,0:T(8,128)S(1)} %get-tuple-element.54), channel_id=1, source_target_pairs={{0,24},{8,0},{16,8},{24,16},{1,25},{9,1},{17,9},{25,17},{2,26},{10... | collective-permute-start | bytes 589832 | tf_op jit(solution)/shard_map/ppermute | solution.py:646
  83.0 26.6 %collective-permute-start.7 = (f32[192,256]{1,0:T(8,128)S(1)}, f32[192,256]{1,0:T(8,128)S(1)}, u32[]{:S(2)}, u32[]{:S(2)}) collective-permute-start(f32[192,256]{1,0:T(8,128)S(1)} %bitcast.6), channel_id=1, source_target_pairs={{0,2},{1,3},{2,0},{3,1},{4,6},{5,7},{6,4},{7,5},{8,10},{9,11},{10,... | collective-permute-start | bytes 589832 | tf_op jit(solution)/shard_map/ppermute | solution.py:600
  92.8 17.5 %collective-permute-start.10 = (f32[192,256]{1,0:T(8,128)S(1)}, f32[192,256]{1,0:T(8,128)S(1)}, u32[]{:S(2)}, u32[]{:S(2)}) collective-permute-start(f32[192,256]{1,0:T(8,128)S(1)} %bitcast.7), channel_id=1, source_target_pairs={{0,1},{1,0},{2,3},{3,2},{4,5},{5,4},{6,7},{7,6},{8,9},{9,8},{10,11... | collective-permute-start | bytes 589832 | tf_op jit(solution)/shard_map/ppermute | solution.py:47
  92.8 18.8 %collective-permute-start.9 = (f32[192,256]{1,0:T(8,128)S(1)}, f32[192,256]{1,0:T(8,128)S(1)}, u32[]{:S(2)}, u32[]{:S(2)}) collective-permute-start(f32[192,256]{1,0:T(8,128)S(1)} %collective-permute-done.8.refs_2_), channel_id=1, source_target_pairs={{0,2},{1,3},{2,0},{3,1},{4,6},{5,7},{6,4},{7,5},{8,10},{9,11},{10,... | collective-permute-start | bytes 589832 | tf_op jit(solution)/shard_map/ppermute | solution.py:600
  96.5 6.6 %collective-permute-start.36 = (f32[8,256]{1,0:T(8,128)S(1)}, f32[8,256]{1,0:T(8,128)S(1)}, u32[]{:S(2)}, u32[]{:S(2)}) collective-permute-start(f32[8,256]{1,0:T(8,128)S(1)} %collective-permute-done.35.refs_15_), channel_id=1, source_target_pairs={{0,6},{1,7},{2,4},{3,5},{4,2},{5,3},{6,0},{7,1},{8,14},{9,15},{10,... | collective-permute-start | bytes 24584 | tf_op jit(solution)/shard_map/ppermute | solution.py:607
  109.3 8.4 %collective-permute-start.40 = (f32[256,256]{1,0:T(8,128)S(1)}, f32[256,256]{1,0:T(8,128)S(1)}, u32[]{:S(2)}, u32[]{:S(2)}) collective-permute-start(f32[256,256]{1,0:T(8,128)S(1)} %get-tuple-element.56), channel_id=1, source_target_pairs={{0,2},{1,3},{2,0},{3,1},{4,6},{5,7},{6,4},{7,5},{8,10},{9,11},{10,... | collective-permute-start | bytes 786440 | tf_op jit(solution)/shard_map/ppermute | solution.py:600
  109.6 8.1 %collective-permute-start.41 = (f32[224,256]{1,0:T(8,128)S(1)}, f32[224,256]{1,0:T(8,128)S(1)}, u32[]{:S(2)}, u32[]{:S(2)}) collective-permute-start(f32[224,256]{1,0:T(8,128)S(1)} %get-tuple-element.57), channel_id=1, source_target_pairs={{2,4},{3,5},{4,2},{5,3},{10,12},{11,13},{12,10},{13,11},{18,20},{1... | collective-permute-start | bytes 688136 | tf_op jit(solution)/shard_map/ppermute | solution.py:600
  110.3 15.4 %collective-permute-start.42 = (f32[224,256]{1,0:T(8,128)S(1)}, f32[224,256]{1,0:T(8,128)S(1)}, u32[]{:S(2)}, u32[]{:S(2)}) collective-permute-start(f32[224,256]{1,0:T(8,128)S(1)} %get-tuple-element.58), channel_id=1, source_target_pairs={{2,6},{3,7},{4,0},{5,1},{10,14},{11,15},{12,8},{13,9},{18,22},{19,... | collective-permute-start | bytes 688136 | tf_op jit(solution)/shard_map/ppermute | solution.py:600
  111.6 14.0 %collective-permute-start.11 = (f32[192,256]{1,0:T(8,128)S(1)}, f32[192,256]{1,0:T(8,128)S(1)}, u32[]{:S(2)}, u32[]{:S(2)}) collective-permute-start(f32[192,256]{1,0:T(8,128)S(1)} %collective-permute-done.7.refs_1_), channel_id=1, source_target_pairs={{0,1},{1,0},{2,3},{3,2},{4,5},{5,4},{6,7},{7,6},{8,9},{9,8},{10,11... | collective-permute-start | bytes 589832 | tf_op jit(solution)/shard_map/ppermute | solution.py:47
  112.1 16.9 %collective-permute-start.43 = (f32[256,256]{1,0:T(8,128)S(1)}, f32[256,256]{1,0:T(8,128)S(1)}, u32[]{:S(2)}, u32[]{:S(2)}) collective-permute-start(f32[256,256]{1,0:T(8,128)S(1)} %get-tuple-element.55.refs_8_), channel_id=1, source_target_pairs={{0,1},{1,0},{2,3},{3,2},{4,5},{5,4},{6,7},{7,6},{8,9},{9,8},{10,11... | collective-permute-start | bytes 786440 | tf_op jit(solution)/shard_map/ppermute | solution.py:47
  117.8 11.2 %collective-permute-start.44 = (f32[256,256]{1,0:T(8,128)S(1)}, f32[256,256]{1,0:T(8,128)S(1)}, u32[]{:S(2)}, u32[]{:S(2)}) collective-permute-start(f32[256,256]{1,0:T(8,128)S(1)} %collective-permute-done.40.refs_9_), channel_id=1, source_target_pairs={{0,1},{1,0},{2,3},{3,2},{4,5},{5,4},{6,7},{7,6},{8,9},{9,8},{10,11... | collective-permute-start | bytes 786440 | tf_op jit(solution)/shard_map/ppermute | solution.py:47
  117.8 11.2 %collective-permute-start.45 = (f32[224,256]{1,0:T(8,128)S(1)}, f32[224,256]{1,0:T(8,128)S(1)}, u32[]{:S(2)}, u32[]{:S(2)}) collective-permute-start(f32[224,256]{1,0:T(8,128)S(1)} %collective-permute-done.41.refs_10_), channel_id=1, source_target_pairs={{0,1},{1,0},{2,3},{3,2},{4,5},{5,4},{6,7},{7,6},{8,9},{9,8},{10,11... | collective-permute-start | bytes 688136 | tf_op jit(solution)/shard_map/ppermute | solution.py:47
  (20 other events, 180.4 us)

commit v3 on v2

--- a/solution.py
+++ b/solution.py
@@ -596,16 +596,23 @@
     d_rows[2] = taken(cots[0], slice(3 * span + depth, None))
 
 
-def by_xor(array, by, chips):
-    return lax.ppermute(array, "tok", [(2 * a + core, 2 * (a ^ by) + core) for a in chips for core in range(2)])
+def over_chips(array, moves):
+    pairs = [(2 * a + core, 2 * b + (core if a != b else 1 - core)) for a, b in enumerate(moves) for core in range(2)]
+    return lax.ppermute(array, "tok", pairs)
+
+
+def by_xor(array, by):
+    return over_chips(array, [chip ^ by for chip in range(CHIPS)])
+
+
+ACROSS = (0, 2, 1, 3)
+INWARD = (2, 0, 3, 1)
+OUTWARD = (1, 3, 0, 2)
 
 
 def exchanged(array):
-    size = lax.axis_size("tok")
-    gathered = [array]
-    for bits in (2 * (LOW ^ HIGH_CHIP), 2 * (LOW ^ HIGH_CHIP) + 1, 1):
-        gathered.append(lax.ppermute(array, "tok", [(j, j ^ bits) for j in range(size)]))
-    return gathered
+    turned = [(2 * a + core, 2 * b + 1 - core) for a, b in enumerate(ACROSS) for core in range(2)]
+    return [array, over_chips(array, ACROSS), lax.ppermute(array, "tok", turned), core_swap(array)]
 
 
 def both_cores(pieces):
@@ -615,29 +622,26 @@
     return pieces + swapped
 
 
-def hops(arrays, near, far, across):
-    first = by_xor(arrays[1], 1, near)
-    second = by_xor(arrays[2], 2, far)
-    third = by_xor(arrays[3], 3, across)
+def hops(arrays, far):
+    first = by_xor(arrays[1], 1)
+    second = over_chips(arrays[2], far)
+    third = over_chips(arrays[3], ACROSS)
     return first, second, third
 
 
-ALL, MIDDLE, OUTER = tuple(range(CHIPS)), (LOW, HIGH_CHIP), (0, CHIPS - 1)
-
-
 def to_chain(arrays):
-    return both_cores([arrays[0], *hops(arrays, ALL, OUTER, MIDDLE)])
+    return both_cores([arrays[0], *hops(arrays, INWARD)])
 
 
 def from_chain(arrays):
-    near, far, across = hops(arrays, ALL, MIDDLE, MIDDLE)
+    near, far, across = hops(arrays, OUTWARD)
     return both_cores([arrays[0], near, across, far])
 
 
 def from_chain_relayed(array):
-    near = by_xor(array, 1, ALL)
-    across = by_xor(array, 3, MIDDLE)
-    far = by_xor(across, 1, ALL)
+    near = by_xor(array, 1)
+    across = over_chips(array, ACROSS)
+    far = by_xor(across, 1)
     return both_cores([array, near, across, far])
 
 

time: 131 us -> 124 us (0.947)
  waiting for transfers between devices: 71.1 us -> 60.5 us
  starting transfers between devices: 53.9 us -> 56.9 us
    ppermute x24 -> x20, waiting for transfers between devices: 53.5 us -> 39.9 us  [the longest x16 37.5 us: over_chips(): return lax.ppermute(array, 'tok', pairs)]
    ppermute x16 -> x20, waiting for transfers between devices: 1.29 us -> 4.52 us  [core_swap(): return lax.ppermute(array, 'tok', [(j, j ^ 1) for j in range(size)])]
    ppermute x6, starting transfers between devices: 9.19 us -> 10.9 us  [to_earlier(): lax.ppermute(array, 'block', [(i, (i - 1) % groups) for i in range(groups)])]
    ppermute x24 -> x20, starting transfers between devices: 39.3 us -> 40.8 us  [the longest x16 39.5 us: over_chips(): return lax.ppermute(array, 'tok', pairs)]
    ppermute x16 -> x20, starting transfers between devices: 3.92 us -> 3.55 us  [core_swap(): return lax.ppermute(array, 'tok', [(j, j ^ 1) for j in range(size)])]
  transfers between devices with their start and end apart: 47 -> 47, of which waited for: 20 -> 24; matrix products, arithmetic and copies ran while one was open for 0% -> 0% of each run, Pallas kernels for 1% -> 1%
where the time goes in v3:
time: 124 us
  waiting for transfers between devices  60.5 us (49%)
  starting transfers between devices  56.9 us (46%)
  Pallas kernels  5.34 us (4%)
    ppermute x16, starting transfers between devices, over_chips(): return lax.ppermute(array, 'tok', pairs)  39.5 us
    ppermute x16, waiting for transfers between devices, over_chips(): return lax.ppermute(array, 'tok', pairs)  37.5 us
    ppermute x6, starting transfers between devices, to_earlier(): lax.ppermute(array, 'block', [(i, (i - 1) % groups) for i in range(groups)])  10.9 us
    ppermute x6, waiting for transfers between devices, to_earlier(): lax.ppermute(array, 'block', [(i, (i - 1) % groups) for i in range(groups)])  9.92 us
    ppermute x1, waiting for transfers between devices, to_later(): lax.ppermute(array, 'block', [(i, (i + 1) % groups) for i in range(groups)])  6.19 us
    pallas_call x9, Pallas kernels, kernel_call(): pl.pallas_call(body, in_specs=[pl.BlockSpec(memory_space=space) for _ in...  5.34 us
    ppermute x20, waiting for transfers between devices, core_swap(): return lax.ppermute(array, 'tok', [(j, j ^ 1) for j in range(size)])  4.52 us
    ppermute x20, starting transfers between devices, core_swap(): return lax.ppermute(array, 'tok', [(j, j ^ 1) for j in range(size)])  3.55 us
  transfers between devices with their start and end apart: 47, of which 24 were waited for; matrix products, arithmetic and copies ran while one was open for 0% of the time, Pallas kernels for 1%

profile of v3, /device:TPU:0, one launch (start us, length us, event | category | flops | bytes accessed | tf_op | source)
XLA Modules:
  0.0 123.5 jit_solution(18273211972463579215)
XLA Ops:
  0.6 1.5 %shard_map.110 = (f32[384,256]{1,0:T(8,128)S(1)}, f32[384,256]{1,0:T(8,128)S(1)}, f32[320,256]{1,0:T(8,128)S(1)}, f32[320,256]{1,0:T(8,128)S(1)}, f32[256,256]{1,0:T(8,128)S(1)}) custom-call(f32[128,256]{1,0:T(8,128)} %keys.1, f32[128,256]{1,0:T(8,128)} %values.1, f32[1,128]{1,0:T(1,128)} %bitcast.10, f32[3,32,256]{2,1,0:T(8,128)} %bitcast.12, ...), custom_call_target="tpu_custom_call" | custom-call | tf_op jit(solution)/shard_map/pallas_call | solution.py:236
  2.1 3.1 %collective-permute-start = (f32[384,256]{1,0:T(8,128)S(1)}, f32[384,256]{1,0:T(8,128)S(1)}, u32[]{:S(2)}, u32[]{:S(2)}) collective-permute-start(f32[384,256]{1,0:T(8,128)S(1)} %get-tuple-element.35), channel_id=1, source_target_pairs={{0,2},{1,3},{2,0},{3,1},{4,6},{5,7},{6,4},{7,5},{8,10},{9,11},{10,... | collective-permute-start | bytes 1179656 | tf_op jit(solution)/shard_map/ppermute | solution.py:601
  5.3 3.0 %collective-permute-start.1 = (f32[320,256]{1,0:T(8,128)S(1)}, f32[320,256]{1,0:T(8,128)S(1)}, u32[]{:S(2)}, u32[]{:S(2)}) collective-permute-start(f32[320,256]{1,0:T(8,128)S(1)} %get-tuple-element.36), channel_id=1, source_target_pairs={{0,4},{1,5},{2,0},{3,1},{4,6},{5,7},{6,2},{7,3},{8,12},{9,13},{10,... | collective-permute-start | bytes 983048 | tf_op jit(solution)/shard_map/ppermute | solution.py:601
  8.3 1.6 %collective-permute-start.19 = (f32[256,256]{1,0:T(8,128)S(1)}, f32[256,256]{1,0:T(8,128)S(1)}, u32[]{:S(2)}, u32[]{:S(2)}) collective-permute-start(f32[256,256]{1,0:T(8,128)S(1)} %get-tuple-element.47.refs_0_), channel_id=1, source_target_pairs={{0,4},{1,5},{2,0},{3,1},{4,6},{5,7},{6,2},{7,3},{8,12},{9,13},{10,... | collective-permute-start | bytes 786440 | tf_op jit(solution)/shard_map/ppermute | solution.py:601
  9.9 11.0 %collective-permute-done.18.refs_1_ = f32[256,256]{1,0:T(8,128)S(1)} collective-permute-done((f32[256,256]{1,0:T(8,128)S(1)}, f32[256,256]{1,0:T(8,128)S(1)}, u32[]{:S(2)}, u32[]{:S(2)}) %collective-permute-start.18) | collective-permute-done | bytes 262176 | tf_op jit(solution)/shard_map/ppermute | solution.py:601
  21.4 6.5 %collective-permute-done.1.refs_2_ = f32[320,256]{1,0:T(8,128)S(1)} collective-permute-done((f32[320,256]{1,0:T(8,128)S(1)}, f32[320,256]{1,0:T(8,128)S(1)}, u32[]{:S(2)}, u32[]{:S(2)}) %collective-permute-start.1) | collective-permute-done | bytes 327712 | tf_op jit(solution)/shard_map/ppermute | solution.py:601
  28.4 4.3 %collective-permute-done.19.refs_2_ = f32[256,256]{1,0:T(8,128)S(1)} collective-permute-done((f32[256,256]{1,0:T(8,128)S(1)}, f32[256,256]{1,0:T(8,128)S(1)}, u32[]{:S(2)}, u32[]{:S(2)}) %collective-permute-start.19) | collective-permute-done | bytes 262176 | tf_op jit(solution)/shard_map/ppermute | solution.py:601
  32.6 1.5 %collective-permute-done.20.refs_3_ = f32[256,256]{1,0:T(8,128)S(1)} collective-permute-done((f32[256,256]{1,0:T(8,128)S(1)}, f32[256,256]{1,0:T(8,128)S(1)}, u32[]{:S(2)}, u32[]{:S(2)}) %collective-permute-start.20) | collective-permute-done | bytes 262176 | tf_op jit(solution)/shard_map/ppermute | solution.py:601
  35.4 1.4 %collective-permute-done.14.refs_4_ = f32[8,256]{1,0:T(8,128)S(1)} collective-permute-done((f32[8,256]{1,0:T(8,128)S(1)}, f32[8,256]{1,0:T(8,128)S(1)}, u32[]{:S(2)}, u32[]{:S(2)}) %collective-permute-start.14) | collective-permute-done | bytes 8224 | tf_op jit(solution)/shard_map/ppermute | solution.py:601
  37.0 1.0 collective-permute-done.15.refs_5_
  38.2 1.0 collective-permute-done.16.refs_6_
  39.2 1.7 %collective-permute-start.17 = (f32[3,64,256]{2,1,0:T(8,128)S(1)}, f32[3,64,256]{2,1,0:T(8,128)S(1)}, u32[]{:S(2)}, u32[]{:S(2)}) collective-permute-start(f32[3,64,256]{2,1,0:T(8,128)S(1)} %get-tuple-element.39.refs_1_), channel_id=1, source_target_pairs={{0,8},{8,16},{16,24},{24,0},{1,9},{9,17},{17,25},{25,1},{2,10},{10... | collective-permute-start | bytes 589832 | tf_op jit(solution)/shard_map/ppermute | solution.py:655
  40.9 6.2 %collective-permute-done.17.earlier.refs_18_ = f32[3,64,256]{2,1,0:T(8,128)S(1)} collective-permute-done((f32[3,64,256]{2,1,0:T(8,128)S(1)}, f32[3,64,256]{2,1,0:T(8,128)S(1)}, u32[]{:S(2)}, u32[]{:S(2)}) %collective-permute-start.17) | collective-permute-done | bytes 196640 | tf_op jit(solution)/shard_map/ppermute | solution.py:655
  47.1 1.8 %collective-permute-start.29 = (f32[3,64,256]{2,1,0:T(8,128)S(1)}, f32[3,64,256]{2,1,0:T(8,128)S(1)}, u32[]{:S(2)}, u32[]{:S(2)}) collective-permute-start(f32[3,64,256]{2,1,0:T(8,128)S(1)} %get-tuple-element.49), channel_id=1, source_target_pairs={{0,24},{8,0},{16,8},{24,16},{1,25},{9,1},{17,9},{25,17},{2,26},{10... | collective-permute-start | bytes 589832 | tf_op jit(solution)/shard_map/ppermute | solution.py:650
  48.8 1.4 %collective-permute-start.25 = (f32[8,256]{1,0:T(8,128)S(1)}, f32[8,256]{1,0:T(8,128)S(1)}, u32[]{:S(2)}, u32[]{:S(2)}) collective-permute-start(f32[8,256]{1,0:T(8,128)S(1)} %get-tuple-element.48), channel_id=1, source_target_pairs={{0,24},{8,0},{16,8},{24,16},{1,25},{9,1},{17,9},{25,17},{2,26},{10... | collective-permute-start | bytes 24584 | tf_op jit(solution)/shard_map/ppermute | solution.py:650
  50.3 3.1 %collective-permute-done.25.refs_7_ = f32[8,256]{1,0:T(8,128)S(1)} collective-permute-done((f32[8,256]{1,0:T(8,128)S(1)}, f32[8,256]{1,0:T(8,128)S(1)}, u32[]{:S(2)}, u32[]{:S(2)}) %collective-permute-start.25) | collective-permute-done | bytes 8224 | tf_op jit(solution)/shard_map/ppermute | solution.py:650
  55.1 2.7 %collective-permute-start.34 = (f32[3,64,256]{2,1,0:T(8,128)S(1)}, f32[3,64,256]{2,1,0:T(8,128)S(1)}, u32[]{:S(2)}, u32[]{:S(2)}) collective-permute-start(f32[3,64,256]{2,1,0:T(8,128)S(1)} %get-tuple-element.52), channel_id=1, source_target_pairs={{0,24},{8,0},{16,8},{24,16},{1,25},{9,1},{17,9},{25,17},{2,26},{10... | collective-permute-start | bytes 589832 | tf_op jit(solution)/shard_map/ppermute | solution.py:650
  58.3 4.1 %collective-permute-done.30.refs_7_.refs_11_ = f32[8,256]{1,0:T(8,128)S(1)} collective-permute-done((f32[8,256]{1,0:T(8,128)S(1)}, f32[8,256]{1,0:T(8,128)S(1)}, u32[]{:S(2)}, u32[]{:S(2)}) %collective-permute-start.30) | collective-permute-done | bytes 8224 | tf_op jit(solution)/shard_map/ppermute | solution.py:650
  63.0 0.7 collective-permute-done.31.refs_8_.refs_12_
  64.2 3.4 %collective-permute-start.39 = (f32[3,64,256]{2,1,0:T(8,128)S(1)}, f32[3,64,256]{2,1,0:T(8,128)S(1)}, u32[]{:S(2)}, u32[]{:S(2)}) collective-permute-start(f32[3,64,256]{2,1,0:T(8,128)S(1)} %get-tuple-element.54), channel_id=1, source_target_pairs={{0,24},{8,0},{16,8},{24,16},{1,25},{9,1},{17,9},{25,17},{2,26},{10... | collective-permute-start | bytes 589832 | tf_op jit(solution)/shard_map/ppermute | solution.py:650
  67.6 21.1 %collective-permute-start.7 = (f32[192,256]{1,0:T(8,128)S(1)}, f32[192,256]{1,0:T(8,128)S(1)}, u32[]{:S(2)}, u32[]{:S(2)}) collective-permute-start(f32[192,256]{1,0:T(8,128)S(1)} %bitcast.6), channel_id=1, source_target_pairs={{0,2},{1,3},{2,0},{3,1},{4,6},{5,7},{6,4},{7,5},{8,10},{9,11},{10,... | collective-permute-start | bytes 589832 | tf_op jit(solution)/shard_map/ppermute | solution.py:601
  88.8 1.0 collective-permute-start.35
  89.8 2.6 %collective-permute-done.35.refs_15_ = f32[8,256]{1,0:T(8,128)S(1)} collective-permute-done((f32[8,256]{1,0:T(8,128)S(1)}, f32[8,256]{1,0:T(8,128)S(1)}, u32[]{:S(2)}, u32[]{:S(2)}) %collective-permute-start.35) | collective-permute-done | bytes 8224 | tf_op jit(solution)/shard_map/ppermute | solution.py:650
  92.4 1.2 collective-permute-done.36.refs_16_
  93.8 1.0 collective-permute-done.37.refs_17_
  95.0 1.0 collective-permute-done.38.refs_18_
  96.1 9.5 %collective-permute-start.40 = (f32[256,256]{1,0:T(8,128)S(1)}, f32[256,256]{1,0:T(8,128)S(1)}, u32[]{:S(2)}, u32[]{:S(2)}) collective-permute-start(f32[256,256]{1,0:T(8,128)S(1)} %get-tuple-element.56), channel_id=1, source_target_pairs={{0,2},{1,3},{2,0},{3,1},{4,6},{5,7},{6,4},{7,5},{8,10},{9,11},{10,... | collective-permute-start | bytes 786440 | tf_op jit(solution)/shard_map/ppermute | solution.py:601
  107.1 5.1 %collective-permute-done.40.refs_9_ = f32[256,256]{1,0:T(8,128)S(1)} collective-permute-done((f32[256,256]{1,0:T(8,128)S(1)}, f32[256,256]{1,0:T(8,128)S(1)}, u32[]{:S(2)}, u32[]{:S(2)}) %collective-permute-start.40) | collective-permute-done | bytes 262176 | tf_op jit(solution)/shard_map/ppermute | solution.py:601
  112.8 5.2 %collective-permute-done.42.refs_11_ = f32[224,256]{1,0:T(8,128)S(1)} collective-permute-done((f32[224,256]{1,0:T(8,128)S(1)}, f32[224,256]{1,0:T(8,128)S(1)}, u32[]{:S(2)}, u32[]{:S(2)}) %collective-permute-start.42) | collective-permute-done | bytes 229408 | tf_op jit(solution)/shard_map/ppermute | solution.py:601
  118.5 1.3 %collective-permute-done.13.refs_7_ = f32[192,256]{1,0:T(8,128)S(1)} collective-permute-done((f32[192,256]{1,0:T(8,128)S(1)}, f32[192,256]{1,0:T(8,128)S(1)}, u32[]{:S(2)}, u32[]{:S(2)}) %collective-permute-start.13) | collective-permute-done | bytes 196640 | tf_op jit(solution)/shard_map/ppermute | solution.py:47
  119.8 1.5 %shard_map.112 = f32[128,256]{1,0:T(8,128)} custom-call(f32[128,256]{1,0:T(8,128)S(1)} %copy-done.2, f32[128,256]{1,0:T(8,128)S(1)} %copy-done.3, f32[192,256]{1,0:T(8,128)S(1)} %bitcast.8, f32[192,256]{1,0:T(8,128)S(1)} %collective-permute-done.7.refs_1_, f32[192,256]{1,0:T(8,128)S(1)} %collective-permute-done.8.refs_2_, ...), custom_call_target="tpu_custom_call" | custom-call | tf_op jit(solution)/shard_map/pallas_call | solution.py:236
  121.4 2.2 %shard_map.118 = (f32[128,256]{1,0:T(8,128)}, f32[128,256]{1,0:T(8,128)}, f32[1,128]{1,0:T(1,128)}, f32[3,32,256]{2,1,0:T(8,128)}) custom-call(f32[128,256]{1,0:T(8,128)S(1)} %copy-done, f32[128,256]{1,0:T(8,128)S(1)} %copy-done.1, f32[1,128]{1,0:T(1,128)S(1)} %bitcast.11, f32[192,256]{1,0:T(8,128)S(1)} %bitcast.9, ...), custom_call_target="tpu_custom_call" | custom-call | tf_op jit(solution)/shard_map/pallas_call | solution.py:236
  (81 shorter events, 9.1 us)
Async XLA Ops:
  2.1 18.7 %collective-permute-start = (f32[384,256]{1,0:T(8,128)S(1)}, f32[384,256]{1,0:T(8,128)S(1)}, u32[]{:S(2)}, u32[]{:S(2)}) collective-permute-start(f32[384,256]{1,0:T(8,128)S(1)} %get-tuple-element.35), channel_id=1, source_target_pairs={{0,2},{1,3},{2,0},{3,1},{4,6},{5,7},{6,4},{7,5},{8,10},{9,11},{10,... | collective-permute-start | bytes 1179656 | tf_op jit(solution)/shard_map/ppermute | solution.py:601
  5.3 15.6 %collective-permute-start.18 = (f32[256,256]{1,0:T(8,128)S(1)}, f32[256,256]{1,0:T(8,128)S(1)}, u32[]{:S(2)}, u32[]{:S(2)}) collective-permute-start(f32[256,256]{1,0:T(8,128)S(1)} %get-tuple-element.47.refs_0_), channel_id=1, source_target_pairs={{0,2},{1,3},{2,0},{3,1},{4,6},{5,7},{6,4},{7,5},{8,10},{9,11},{10,... | collective-permute-start | bytes 786440 | tf_op jit(solution)/shard_map/ppermute | solution.py:601
  5.3 22.5 %collective-permute-start.1 = (f32[320,256]{1,0:T(8,128)S(1)}, f32[320,256]{1,0:T(8,128)S(1)}, u32[]{:S(2)}, u32[]{:S(2)}) collective-permute-start(f32[320,256]{1,0:T(8,128)S(1)} %get-tuple-element.36), channel_id=1, source_target_pairs={{0,4},{1,5},{2,0},{3,1},{4,6},{5,7},{6,2},{7,3},{8,12},{9,13},{10,... | collective-permute-start | bytes 983048 | tf_op jit(solution)/shard_map/ppermute | solution.py:601
  8.3 19.6 %collective-permute-start.2 = (f32[320,256]{1,0:T(8,128)S(1)}, f32[320,256]{1,0:T(8,128)S(1)}, u32[]{:S(2)}, u32[]{:S(2)}) collective-permute-start(f32[320,256]{1,0:T(8,128)S(1)} %get-tuple-element.37), channel_id=1, source_target_pairs={{0,1},{1,0},{2,4},{3,5},{4,2},{5,3},{6,7},{7,6},{8,9},{9,8},{10,12... | collective-permute-start | bytes 983048 | tf_op jit(solution)/shard_map/ppermute | solution.py:601
  8.3 24.3 %collective-permute-start.19 = (f32[256,256]{1,0:T(8,128)S(1)}, f32[256,256]{1,0:T(8,128)S(1)}, u32[]{:S(2)}, u32[]{:S(2)}) collective-permute-start(f32[256,256]{1,0:T(8,128)S(1)} %get-tuple-element.47.refs_0_), channel_id=1, source_target_pairs={{0,4},{1,5},{2,0},{3,1},{4,6},{5,7},{6,2},{7,3},{8,12},{9,13},{10,... | collective-permute-start | bytes 786440 | tf_op jit(solution)/shard_map/ppermute | solution.py:601
  20.8 13.5 %collective-permute-start.3 = (f32[384,256]{1,0:T(8,128)S(1)}, f32[384,256]{1,0:T(8,128)S(1)}, u32[]{:S(2)}, u32[]{:S(2)}) collective-permute-start(f32[384,256]{1,0:T(8,128)S(1)} %get-tuple-element.34.refs_0_), channel_id=1, source_target_pairs={{0,1},{1,0},{2,3},{3,2},{4,5},{5,4},{6,7},{7,6},{8,9},{9,8},{10,11... | collective-permute-start | bytes 1179656 | tf_op jit(solution)/shard_map/ppermute | solution.py:47
  20.8 14.4 %collective-permute-start.4 = (f32[384,256]{1,0:T(8,128)S(1)}, f32[384,256]{1,0:T(8,128)S(1)}, u32[]{:S(2)}, u32[]{:S(2)}) collective-permute-start(f32[384,256]{1,0:T(8,128)S(1)} %collective-permute-done.refs_1_), channel_id=1, source_target_pairs={{0,1},{1,0},{2,3},{3,2},{4,5},{5,4},{6,7},{7,6},{8,9},{9,8},{10,11... | collective-permute-start | bytes 1179656 | tf_op jit(solution)/shard_map/ppermute | solution.py:47
  27.9 6.8 %collective-permute-start.5 = (f32[320,256]{1,0:T(8,128)S(1)}, f32[320,256]{1,0:T(8,128)S(1)}, u32[]{:S(2)}, u32[]{:S(2)}) collective-permute-start(f32[320,256]{1,0:T(8,128)S(1)} %collective-permute-done.1.refs_2_), channel_id=1, source_target_pairs={{0,1},{1,0},{2,3},{3,2},{4,5},{5,4},{6,7},{7,6},{8,9},{9,8},{10,11... | collective-permute-start | bytes 983048 | tf_op jit(solution)/shard_map/ppermute | solution.py:47
  27.9 7.0 %collective-permute-start.6 = (f32[320,256]{1,0:T(8,128)S(1)}, f32[320,256]{1,0:T(8,128)S(1)}, u32[]{:S(2)}, u32[]{:S(2)}) collective-permute-start(f32[320,256]{1,0:T(8,128)S(1)} %collective-permute-done.2.refs_3_), channel_id=1, source_target_pairs={{0,1},{1,0},{2,3},{3,2},{4,5},{5,4},{6,7},{7,6},{8,9},{9,8},{10,11... | collective-permute-start | bytes 983048 | tf_op jit(solution)/shard_map/ppermute | solution.py:47
  34.2 6.7 %collective-permute-start.21 = (f32[256,256]{1,0:T(8,128)S(1)}, f32[256,256]{1,0:T(8,128)S(1)}, u32[]{:S(2)}, u32[]{:S(2)}) collective-permute-start(f32[256,256]{1,0:T(8,128)S(1)} %get-tuple-element.47.refs_0_), channel_id=1, source_target_pairs={{0,1},{1,0},{2,3},{3,2},{4,5},{5,4},{6,7},{7,6},{8,9},{9,8},{10,11... | collective-permute-start | bytes 786440 | tf_op jit(solution)/shard_map/ppermute | solution.py:47
  34.3 6.5 %collective-permute-start.22 = (f32[256,256]{1,0:T(8,128)S(1)}, f32[256,256]{1,0:T(8,128)S(1)}, u32[]{:S(2)}, u32[]{:S(2)}) collective-permute-start(f32[256,256]{1,0:T(8,128)S(1)} %collective-permute-done.18.refs_1_), channel_id=1, source_target_pairs={{0,1},{1,0},{2,3},{3,2},{4,5},{5,4},{6,7},{7,6},{8,9},{9,8},{10,11... | collective-permute-start | bytes 786440 | tf_op jit(solution)/shard_map/ppermute | solution.py:47
  34.7 6.2 %collective-permute-start.23 = (f32[256,256]{1,0:T(8,128)S(1)}, f32[256,256]{1,0:T(8,128)S(1)}, u32[]{:S(2)}, u32[]{:S(2)}) collective-permute-start(f32[256,256]{1,0:T(8,128)S(1)} %collective-permute-done.19.refs_2_), channel_id=1, source_target_pairs={{0,1},{1,0},{2,3},{3,2},{4,5},{5,4},{6,7},{7,6},{8,9},{9,8},{10,11... | collective-permute-start | bytes 786440 | tf_op jit(solution)/shard_map/ppermute | solution.py:47
  34.8 6.0 %collective-permute-start.24 = (f32[256,256]{1,0:T(8,128)S(1)}, f32[256,256]{1,0:T(8,128)S(1)}, u32[]{:S(2)}, u32[]{:S(2)}) collective-permute-start(f32[256,256]{1,0:T(8,128)S(1)} %collective-permute-done.20.refs_3_), channel_id=1, source_target_pairs={{0,1},{1,0},{2,3},{3,2},{4,5},{5,4},{6,7},{7,6},{8,9},{9,8},{10,11... | collective-permute-start | bytes 786440 | tf_op jit(solution)/shard_map/ppermute | solution.py:47
  39.2 7.9 %collective-permute-start.17 = (f32[3,64,256]{2,1,0:T(8,128)S(1)}, f32[3,64,256]{2,1,0:T(8,128)S(1)}, u32[]{:S(2)}, u32[]{:S(2)}) collective-permute-start(f32[3,64,256]{2,1,0:T(8,128)S(1)} %get-tuple-element.39.refs_1_), channel_id=1, source_target_pairs={{0,8},{8,16},{16,24},{24,0},{1,9},{9,17},{17,25},{25,1},{2,10},{10... | collective-permute-start | bytes 589832 | tf_op jit(solution)/shard_map/ppermute | solution.py:655
  47.1 8.0 %collective-permute-start.29 = (f32[3,64,256]{2,1,0:T(8,128)S(1)}, f32[3,64,256]{2,1,0:T(8,128)S(1)}, u32[]{:S(2)}, u32[]{:S(2)}) collective-permute-start(f32[3,64,256]{2,1,0:T(8,128)S(1)} %get-tuple-element.49), channel_id=1, source_target_pairs={{0,24},{8,0},{16,8},{24,16},{1,25},{9,1},{17,9},{25,17},{2,26},{10... | collective-permute-start | bytes 589832 | tf_op jit(solution)/shard_map/ppermute | solution.py:650
  48.8 4.6 %collective-permute-start.25 = (f32[8,256]{1,0:T(8,128)S(1)}, f32[8,256]{1,0:T(8,128)S(1)}, u32[]{:S(2)}, u32[]{:S(2)}) collective-permute-start(f32[8,256]{1,0:T(8,128)S(1)} %get-tuple-element.48), channel_id=1, source_target_pairs={{0,24},{8,0},{16,8},{24,16},{1,25},{9,1},{17,9},{25,17},{2,26},{10... | collective-permute-start | bytes 24584 | tf_op jit(solution)/shard_map/ppermute | solution.py:650
  55.1 9.0 %collective-permute-start.34 = (f32[3,64,256]{2,1,0:T(8,128)S(1)}, f32[3,64,256]{2,1,0:T(8,128)S(1)}, u32[]{:S(2)}, u32[]{:S(2)}) collective-permute-start(f32[3,64,256]{2,1,0:T(8,128)S(1)} %get-tuple-element.52), channel_id=1, source_target_pairs={{0,24},{8,0},{16,8},{24,16},{1,25},{9,1},{17,9},{25,17},{2,26},{10... | collective-permute-start | bytes 589832 | tf_op jit(solution)/shard_map/ppermute | solution.py:650
  57.8 30.9 %collective-permute-start.8 = (f32[192,256]{1,0:T(8,128)S(1)}, f32[192,256]{1,0:T(8,128)S(1)}, u32[]{:S(2)}, u32[]{:S(2)}) collective-permute-start(f32[192,256]{1,0:T(8,128)S(1)} %bitcast.5), channel_id=1, source_target_pairs={{0,1},{1,0},{2,4},{3,5},{4,2},{5,3},{6,7},{7,6},{8,9},{9,8},{10,12... | collective-permute-start | bytes 589832 | tf_op jit(solution)/shard_map/ppermute | solution.py:601
  57.8 4.7 %collective-permute-start.30 = (f32[8,256]{1,0:T(8,128)S(1)}, f32[8,256]{1,0:T(8,128)S(1)}, u32[]{:S(2)}, u32[]{:S(2)}) collective-permute-start(f32[8,256]{1,0:T(8,128)S(1)} %get-tuple-element.51), channel_id=1, source_target_pairs={{0,24},{8,0},{16,8},{24,16},{1,25},{9,1},{17,9},{25,17},{2,26},{10... | collective-permute-start | bytes 24584 | tf_op jit(solution)/shard_map/ppermute | solution.py:650
  64.2 31.8 %collective-permute-start.39 = (f32[3,64,256]{2,1,0:T(8,128)S(1)}, f32[3,64,256]{2,1,0:T(8,128)S(1)}, u32[]{:S(2)}, u32[]{:S(2)}) collective-permute-start(f32[3,64,256]{2,1,0:T(8,128)S(1)} %get-tuple-element.54), channel_id=1, source_target_pairs={{0,24},{8,0},{16,8},{24,16},{1,25},{9,1},{17,9},{25,17},{2,26},{10... | collective-permute-start | bytes 589832 | tf_op jit(solution)/shard_map/ppermute | solution.py:650
  67.6 38.0 %collective-permute-start.7 = (f32[192,256]{1,0:T(8,128)S(1)}, f32[192,256]{1,0:T(8,128)S(1)}, u32[]{:S(2)}, u32[]{:S(2)}) collective-permute-start(f32[192,256]{1,0:T(8,128)S(1)} %bitcast.6), channel_id=1, source_target_pairs={{0,2},{1,3},{2,0},{3,1},{4,6},{5,7},{6,4},{7,5},{8,10},{9,11},{10,... | collective-permute-start | bytes 589832 | tf_op jit(solution)/shard_map/ppermute | solution.py:601
  88.7 17.4 %collective-permute-start.10 = (f32[192,256]{1,0:T(8,128)S(1)}, f32[192,256]{1,0:T(8,128)S(1)}, u32[]{:S(2)}, u32[]{:S(2)}) collective-permute-start(f32[192,256]{1,0:T(8,128)S(1)} %bitcast.7), channel_id=1, source_target_pairs={{0,1},{1,0},{2,3},{3,2},{4,5},{5,4},{6,7},{7,6},{8,9},{9,8},{10,11... | collective-permute-start | bytes 589832 | tf_op jit(solution)/shard_map/ppermute | solution.py:47
  88.7 17.8 %collective-permute-start.9 = (f32[192,256]{1,0:T(8,128)S(1)}, f32[192,256]{1,0:T(8,128)S(1)}, u32[]{:S(2)}, u32[]{:S(2)}) collective-permute-start(f32[192,256]{1,0:T(8,128)S(1)} %collective-permute-done.8.refs_2_), channel_id=1, source_target_pairs={{0,2},{1,3},{2,0},{3,1},{4,6},{5,7},{6,4},{7,5},{8,10},{9,11},{10,... | collective-permute-start | bytes 589832 | tf_op jit(solution)/shard_map/ppermute | solution.py:601
  88.8 3.7 %collective-permute-start.35 = (f32[8,256]{1,0:T(8,128)S(1)}, f32[8,256]{1,0:T(8,128)S(1)}, u32[]{:S(2)}, u32[]{:S(2)}) collective-permute-start(f32[8,256]{1,0:T(8,128)S(1)} %get-tuple-element.53), channel_id=1, source_target_pairs={{0,24},{8,0},{16,8},{24,16},{1,25},{9,1},{17,9},{25,17},{2,26},{10... | collective-permute-start | bytes 24584 | tf_op jit(solution)/shard_map/ppermute | solution.py:650
  96.1 16.2 %collective-permute-start.40 = (f32[256,256]{1,0:T(8,128)S(1)}, f32[256,256]{1,0:T(8,128)S(1)}, u32[]{:S(2)}, u32[]{:S(2)}) collective-permute-start(f32[256,256]{1,0:T(8,128)S(1)} %get-tuple-element.56), channel_id=1, source_target_pairs={{0,2},{1,3},{2,0},{3,1},{4,6},{5,7},{6,4},{7,5},{8,10},{9,11},{10,... | collective-permute-start | bytes 786440 | tf_op jit(solution)/shard_map/ppermute | solution.py:601
  105.6 6.7 %collective-permute-start.41 = (f32[224,256]{1,0:T(8,128)S(1)}, f32[224,256]{1,0:T(8,128)S(1)}, u32[]{:S(2)}, u32[]{:S(2)}) collective-permute-start(f32[224,256]{1,0:T(8,128)S(1)} %get-tuple-element.57), channel_id=1, source_target_pairs={{0,1},{1,0},{2,4},{3,5},{4,2},{5,3},{6,7},{7,6},{8,9},{9,8},{10,12... | collective-permute-start | bytes 688136 | tf_op jit(solution)/shard_map/ppermute | solution.py:601
  106.1 11.9 %collective-permute-start.42 = (f32[224,256]{1,0:T(8,128)S(1)}, f32[224,256]{1,0:T(8,128)S(1)}, u32[]{:S(2)}, u32[]{:S(2)}) collective-permute-start(f32[224,256]{1,0:T(8,128)S(1)} %get-tuple-element.58), channel_id=1, source_target_pairs={{0,2},{1,3},{2,6},{3,7},{4,0},{5,1},{6,4},{7,5},{8,10},{9,11},{10,... | collective-permute-start | bytes 688136 | tf_op jit(solution)/shard_map/ppermute | solution.py:601
  106.5 11.5 %collective-permute-start.11 = (f32[192,256]{1,0:T(8,128)S(1)}, f32[192,256]{1,0:T(8,128)S(1)}, u32[]{:S(2)}, u32[]{:S(2)}) collective-permute-start(f32[192,256]{1,0:T(8,128)S(1)} %collective-permute-done.7.refs_1_), channel_id=1, source_target_pairs={{0,1},{1,0},{2,3},{3,2},{4,5},{5,4},{6,7},{7,6},{8,9},{9,8},{10,11... | collective-permute-start | bytes 589832 | tf_op jit(solution)/shard_map/ppermute | solution.py:47
  107.0 14.3 %collective-permute-start.43 = (f32[256,256]{1,0:T(8,128)S(1)}, f32[256,256]{1,0:T(8,128)S(1)}, u32[]{:S(2)}, u32[]{:S(2)}) collective-permute-start(f32[256,256]{1,0:T(8,128)S(1)} %get-tuple-element.55.refs_8_), channel_id=1, source_target_pairs={{0,1},{1,0},{2,3},{3,2},{4,5},{5,4},{6,7},{7,6},{8,9},{9,8},{10,11... | collective-permute-start | bytes 786440 | tf_op jit(solution)/shard_map/ppermute | solution.py:47
  112.3 9.1 %collective-permute-start.44 = (f32[256,256]{1,0:T(8,128)S(1)}, f32[256,256]{1,0:T(8,128)S(1)}, u32[]{:S(2)}, u32[]{:S(2)}) collective-permute-start(f32[256,256]{1,0:T(8,128)S(1)} %collective-permute-done.40.refs_9_), channel_id=1, source_target_pairs={{0,1},{1,0},{2,3},{3,2},{4,5},{5,4},{6,7},{7,6},{8,9},{9,8},{10,11... | collective-permute-start | bytes 786440 | tf_op jit(solution)/shard_map/ppermute | solution.py:47
  112.3 9.1 %collective-permute-start.45 = (f32[224,256]{1,0:T(8,128)S(1)}, f32[224,256]{1,0:T(8,128)S(1)}, u32[]{:S(2)}, u32[]{:S(2)}) collective-permute-start(f32[224,256]{1,0:T(8,128)S(1)} %collective-permute-done.41.refs_10_), channel_id=1, source_target_pairs={{0,1},{1,0},{2,3},{3,2},{4,5},{5,4},{6,7},{7,6},{8,9},{9,8},{10,11... | collective-permute-start | bytes 688136 | tf_op jit(solution)/shard_map/ppermute | solution.py:47
  118.0 3.3 %collective-permute-start.46 = (f32[224,256]{1,0:T(8,128)S(1)}, f32[224,256]{1,0:T(8,128)S(1)}, u32[]{:S(2)}, u32[]{:S(2)}) collective-permute-start(f32[224,256]{1,0:T(8,128)S(1)} %collective-permute-done.42.refs_11_), channel_id=1, source_target_pairs={{0,1},{1,0},{2,3},{3,2},{4,5},{5,4},{6,7},{7,6},{8,9},{9,8},{10,11... | collective-permute-start | bytes 688136 | tf_op jit(solution)/shard_map/ppermute | solution.py:47
  (20 other events, 157.5 us)

commit v4 on v3

--- a/solution.py
+++ b/solution.py
@@ -497,6 +497,21 @@
         finish([row + applied[m * span : (m + 1) * span, :] for m, row in enumerate(rows)], earlier, payload, partial)
 
 
+def terms_body(count, *refs):
+    cot = refs[-1]
+    span = refs[0].shape[1]
+
+    @pl.when(~in_chain())
+    def _():
+        cot[...] = jnp.zeros(cot.shape, jnp.float32)
+
+    @pl.when(in_chain())
+    def _():
+        cots, _ = state_terms(*refs[:3], refs[3:7], refs[7 : 7 + 4 * count], refs[7 + 4 * count : 7 + 5 * count])
+        for m in range(3):
+            cot[m * span : (m + 1) * span, :] = cots[m]
+
+
 def final_body(count, *refs):
     applied, outs, table = refs[-6], refs[-5:-1], refs[-1]
     span = refs[0].shape[1]
@@ -510,21 +525,17 @@
 
     @pl.when(in_chain())
     def _():
-        cots, rows = section_rows(count, refs)
-        for out in outs:
-            for m in range(3):
-                out[m * span : (m + 1) * span, :] = cots[m]
+        _, rows = section_rows(count, refs)
         rows = [row + applied[m * span : (m + 1) * span, :] for m, row in enumerate(rows)]
         table[...] = jnp.concatenate(rows[:2]).T
         for by, out in enumerate(outs):
             start = jnp.bitwise_xor(chip, by) * 2 * depth
             for core in range(2):
-                lanes = slice(core * 128, (core + 1) * 128)
-                out[3 * span : 3 * span + depth, lanes] = table[rows_at(start + core * depth, depth), :]
+                out[:depth, core * 128 : (core + 1) * 128] = table[rows_at(start + core * depth, depth), :]
         low = chip == LOW
         upper, lower = rows[2][:depth], rows[2][depth:]
-        outs[0][3 * span + depth :] = jnp.where(low, lower, upper)
-        outs[1][3 * span + depth :] = jnp.where(low, upper, lower)
+        outs[0][depth:] = jnp.where(low, lower, upper)
+        outs[1][depth:] = jnp.where(low, upper, lower)
 
 
 def joined(refs):
@@ -554,7 +565,8 @@
 
 def token_body(keys, values, rates, *refs):
     weights, cots = joined(refs[:8]), joined(refs[8:16])
-    d_keys, d_values, d_rates, d_rows = refs[16:]
+    ends = joined(refs[16:24])
+    d_keys, d_values, d_rates, d_rows = refs[24:]
     width = keys.shape[1]
     span = width // len(weights)
     one, three, two = [load_halves(weights, part, span) for part in range(3)]
@@ -578,9 +590,9 @@
     d_rates[...] = -jnp.sum((values[...] * t_out).T, axis=0, keepdims=True)
     depth = d_rows.shape[1]
     low_side, upper_core = my_chip() <= LOW, my_core() == 0
-    block = slice(3 * span, 3 * span + depth)
+    block = slice(0, depth)
     sides = []
-    for near, far in (cots[:2], cots[2:]):
+    for near, far in (ends[:2], ends[2:]):
         near, far = taken(near, block), taken(far, block)
         near, far = [jnp.where(upper_core, piece[:, :128], piece[:, 128:]) for piece in (near, far)]
         sides.append([jnp.where(low_side, near, far), jnp.where(low_side, far, near)])
@@ -593,7 +605,7 @@
                     start = (2 * m + i) * depth
                     parts.append(by_core[core][side][:, start : start + depth])
         d_rows[m] = jnp.concatenate(parts, axis=1)
-    d_rows[2] = taken(cots[0], slice(3 * span + depth, None))
+    d_rows[2] = taken(ends[0], slice(depth, None))
 
 
 def over_chips(array, moves):
@@ -706,17 +718,18 @@
         arrived.append(to_earlier(payload))
         inners += exchanged(straight)
     received = [*common, *inners, *arrived]
-    long, short = f32(4 * span, width), f32(3 * span + rows, width)
+    (cot,) = kernel_call(functools.partial(terms_body, groups - 1), [wide], *received)
+    cots = from_chain([cot] * CHIPS)
     ends = kernel_call(
         functools.partial(final_body, groups - 1),
-        [long, long, short, short],
+        [f32(2 * rows, width)] * 2 + [f32(rows, width)] * 2,
         *received,
         *halved,
         kept,
         applied,
         scratch=[pltpu.VMEM((width, 128), jnp.float32)],
     )
-    cots = from_chain(ends)
+    end_pieces = from_chain(ends)
     (d_queries,) = kernel_call(query_body, [square], queries, out_cot, *weights, spill=True)
     d_keys, d_values, d_rates, d_rows = kernel_call(
         token_body,
@@ -726,6 +739,7 @@
         rates_row,
         *weights,
         *cots,
+        *end_pieces,
         spill=True,
     )
     return (d_queries, d_keys, d_values, d_rates.reshape(depth), d_rows[None])

time: 124 us -> 124 us (level)
  starting transfers between devices: 56.9 us -> 67.9 us
  waiting for transfers between devices: 60.5 us -> 49.6 us
    ppermute x16 -> x19, waiting for transfers between devices: 37.5 us -> 28.4 us  [over_chips(): return lax.ppermute(array, 'tok', pairs)]
    ppermute x16 -> x19, starting transfers between devices: 39.5 us -> 47.5 us  [over_chips(): return lax.ppermute(array, 'tok', pairs)]
    ppermute x20 -> x24, starting transfers between devices: 3.55 us -> 5.55 us  [core_swap(): return lax.ppermute(array, 'tok', [(j, j ^ 1) for j in range(size)])]
    ppermute x6, waiting for transfers between devices: 9.92 us -> 8.59 us  [to_earlier(): lax.ppermute(array, 'block', [(i, (i - 1) % groups) for i in range(groups)])]
    ppermute x20 -> x24, waiting for transfers between devices: 4.52 us -> 5.15 us  [core_swap(): return lax.ppermute(array, 'tok', [(j, j ^ 1) for j in range(size)])]
    pallas_call x9 -> x10, Pallas kernels: 5.34 us -> 5.34 us  [kernel_call(): pl.pallas_call(body, in_specs=[pl.BlockSpec(memory_space=space) for _ in...]
  transfers between devices with their start and end apart: 47 -> 54, of which waited for: 24 -> 22; matrix products, arithmetic and copies ran while one was open for 0% -> 0% of each run, Pallas kernels for 1% -> 1%
where the time goes in v4:
time: 124 us
  starting transfers between devices  67.9 us (55%)
  waiting for transfers between devices  49.6 us (40%)
  Pallas kernels  5.34 us (4%)
    ppermute x19, starting transfers between devices, over_chips(): return lax.ppermute(array, 'tok', pairs)  47.5 us
    ppermute x19, waiting for transfers between devices, over_chips(): return lax.ppermute(array, 'tok', pairs)  28.4 us
    ppermute x6, starting transfers between devices, to_earlier(): lax.ppermute(array, 'block', [(i, (i - 1) % groups) for i in range(groups)])  11.5 us
    ppermute x6, waiting for transfers between devices, to_earlier(): lax.ppermute(array, 'block', [(i, (i - 1) % groups) for i in range(groups)])  8.59 us
    ppermute x1, waiting for transfers between devices, to_later(): lax.ppermute(array, 'block', [(i, (i + 1) % groups) for i in range(groups)])  6.19 us
    ppermute x24, starting transfers between devices, core_swap(): return lax.ppermute(array, 'tok', [(j, j ^ 1) for j in range(size)])  5.55 us
    pallas_call x10, Pallas kernels, kernel_call(): pl.pallas_call(body, in_specs=[pl.BlockSpec(memory_space=space) for _ in...  5.34 us
    ppermute x24, waiting for transfers between devices, core_swap(): return lax.ppermute(array, 'tok', [(j, j ^ 1) for j in range(size)])  5.15 us
  transfers between devices with their start and end apart: 54, of which 22 were waited for; matrix products, arithmetic and copies ran while one was open for 0% of the time, Pallas kernels for 1%

profile of v4, /device:TPU:0, one launch (start us, length us, event | category | flops | bytes accessed | tf_op | source)
XLA Modules:
  0.0 123.7 jit_solution(2927908602436564958)
XLA Ops:
  0.6 1.5 %shard_map.110 = (f32[384,256]{1,0:T(8,128)S(1)}, f32[384,256]{1,0:T(8,128)S(1)}, f32[320,256]{1,0:T(8,128)S(1)}, f32[320,256]{1,0:T(8,128)S(1)}, f32[256,256]{1,0:T(8,128)S(1)}) custom-call(f32[128,256]{1,0:T(8,128)} %keys.1, f32[128,256]{1,0:T(8,128)} %values.1, f32[1,128]{1,0:T(1,128)} %bitcast.10, f32[3,32,256]{2,1,0:T(8,128)} %bitcast.12, ...), custom_call_target="tpu_custom_call" | custom-call | tf_op jit(solution)/shard_map/pallas_call | solution.py:236
  2.1 3.1 %collective-permute-start = (f32[384,256]{1,0:T(8,128)S(1)}, f32[384,256]{1,0:T(8,128)S(1)}, u32[]{:S(2)}, u32[]{:S(2)}) collective-permute-start(f32[384,256]{1,0:T(8,128)S(1)} %get-tuple-element.35), channel_id=1, source_target_pairs={{0,2},{1,3},{2,0},{3,1},{4,6},{5,7},{6,4},{7,5},{8,10},{9,11},{10,... | collective-permute-start | bytes 1179656 | tf_op jit(solution)/shard_map/ppermute | solution.py:613
  5.3 3.0 %collective-permute-start.1 = (f32[320,256]{1,0:T(8,128)S(1)}, f32[320,256]{1,0:T(8,128)S(1)}, u32[]{:S(2)}, u32[]{:S(2)}) collective-permute-start(f32[320,256]{1,0:T(8,128)S(1)} %get-tuple-element.36), channel_id=1, source_target_pairs={{0,4},{1,5},{2,0},{3,1},{4,6},{5,7},{6,2},{7,3},{8,12},{9,13},{10,... | collective-permute-start | bytes 983048 | tf_op jit(solution)/shard_map/ppermute | solution.py:613
  8.3 1.6 %collective-permute-start.19 = (f32[256,256]{1,0:T(8,128)S(1)}, f32[256,256]{1,0:T(8,128)S(1)}, u32[]{:S(2)}, u32[]{:S(2)}) collective-permute-start(f32[256,256]{1,0:T(8,128)S(1)} %get-tuple-element.47.refs_0_), channel_id=1, source_target_pairs={{0,4},{1,5},{2,0},{3,1},{4,6},{5,7},{6,2},{7,3},{8,12},{9,13},{10,... | collective-permute-start | bytes 786440 | tf_op jit(solution)/shard_map/ppermute | solution.py:613
  9.9 11.0 %collective-permute-done.18.refs_1_ = f32[256,256]{1,0:T(8,128)S(1)} collective-permute-done((f32[256,256]{1,0:T(8,128)S(1)}, f32[256,256]{1,0:T(8,128)S(1)}, u32[]{:S(2)}, u32[]{:S(2)}) %collective-permute-start.18) | collective-permute-done | bytes 262176 | tf_op jit(solution)/shard_map/ppermute | solution.py:613
  21.4 6.5 %collective-permute-done.1.refs_2_ = f32[320,256]{1,0:T(8,128)S(1)} collective-permute-done((f32[320,256]{1,0:T(8,128)S(1)}, f32[320,256]{1,0:T(8,128)S(1)}, u32[]{:S(2)}, u32[]{:S(2)}) %collective-permute-start.1) | collective-permute-done | bytes 327712 | tf_op jit(solution)/shard_map/ppermute | solution.py:613
  28.4 4.3 %collective-permute-done.19.refs_2_ = f32[256,256]{1,0:T(8,128)S(1)} collective-permute-done((f32[256,256]{1,0:T(8,128)S(1)}, f32[256,256]{1,0:T(8,128)S(1)}, u32[]{:S(2)}, u32[]{:S(2)}) %collective-permute-start.19) | collective-permute-done | bytes 262176 | tf_op jit(solution)/shard_map/ppermute | solution.py:613
  32.6 1.5 %collective-permute-done.20.refs_3_ = f32[256,256]{1,0:T(8,128)S(1)} collective-permute-done((f32[256,256]{1,0:T(8,128)S(1)}, f32[256,256]{1,0:T(8,128)S(1)}, u32[]{:S(2)}, u32[]{:S(2)}) %collective-permute-start.20) | collective-permute-done | bytes 262176 | tf_op jit(solution)/shard_map/ppermute | solution.py:613
  35.4 1.4 %collective-permute-done.14.refs_4_ = f32[8,256]{1,0:T(8,128)S(1)} collective-permute-done((f32[8,256]{1,0:T(8,128)S(1)}, f32[8,256]{1,0:T(8,128)S(1)}, u32[]{:S(2)}, u32[]{:S(2)}) %collective-permute-start.14) | collective-permute-done | bytes 8224 | tf_op jit(solution)/shard_map/ppermute | solution.py:613
  37.0 1.0 collective-permute-done.15.refs_5_
  38.2 1.0 collective-permute-done.16.refs_6_
  39.2 1.7 %collective-permute-start.17 = (f32[3,64,256]{2,1,0:T(8,128)S(1)}, f32[3,64,256]{2,1,0:T(8,128)S(1)}, u32[]{:S(2)}, u32[]{:S(2)}) collective-permute-start(f32[3,64,256]{2,1,0:T(8,128)S(1)} %get-tuple-element.39.refs_1_), channel_id=1, source_target_pairs={{0,8},{8,16},{16,24},{24,0},{1,9},{9,17},{17,25},{25,1},{2,10},{10... | collective-permute-start | bytes 589832 | tf_op jit(solution)/shard_map/ppermute | solution.py:667
  40.9 6.2 %collective-permute-done.17.earlier.refs_18_ = f32[3,64,256]{2,1,0:T(8,128)S(1)} collective-permute-done((f32[3,64,256]{2,1,0:T(8,128)S(1)}, f32[3,64,256]{2,1,0:T(8,128)S(1)}, u32[]{:S(2)}, u32[]{:S(2)}) %collective-permute-start.17) | collective-permute-done | bytes 196640 | tf_op jit(solution)/shard_map/ppermute | solution.py:667
  47.1 1.8 %collective-permute-start.29 = (f32[3,64,256]{2,1,0:T(8,128)S(1)}, f32[3,64,256]{2,1,0:T(8,128)S(1)}, u32[]{:S(2)}, u32[]{:S(2)}) collective-permute-start(f32[3,64,256]{2,1,0:T(8,128)S(1)} %get-tuple-element.49), channel_id=1, source_target_pairs={{0,24},{8,0},{16,8},{24,16},{1,25},{9,1},{17,9},{25,17},{2,26},{10... | collective-permute-start | bytes 589832 | tf_op jit(solution)/shard_map/ppermute | solution.py:662
  48.8 1.4 %collective-permute-start.25 = (f32[8,256]{1,0:T(8,128)S(1)}, f32[8,256]{1,0:T(8,128)S(1)}, u32[]{:S(2)}, u32[]{:S(2)}) collective-permute-start(f32[8,256]{1,0:T(8,128)S(1)} %get-tuple-element.48), channel_id=1, source_target_pairs={{0,24},{8,0},{16,8},{24,16},{1,25},{9,1},{17,9},{25,17},{2,26},{10... | collective-permute-start | bytes 24584 | tf_op jit(solution)/shard_map/ppermute | solution.py:662
  50.3 3.1 %collective-permute-done.25.refs_7_ = f32[8,256]{1,0:T(8,128)S(1)} collective-permute-done((f32[8,256]{1,0:T(8,128)S(1)}, f32[8,256]{1,0:T(8,128)S(1)}, u32[]{:S(2)}, u32[]{:S(2)}) %collective-permute-start.25) | collective-permute-done | bytes 8224 | tf_op jit(solution)/shard_map/ppermute | solution.py:662
  55.1 2.7 %collective-permute-start.34 = (f32[3,64,256]{2,1,0:T(8,128)S(1)}, f32[3,64,256]{2,1,0:T(8,128)S(1)}, u32[]{:S(2)}, u32[]{:S(2)}) collective-permute-start(f32[3,64,256]{2,1,0:T(8,128)S(1)} %get-tuple-element.52), channel_id=1, source_target_pairs={{0,24},{8,0},{16,8},{24,16},{1,25},{9,1},{17,9},{25,17},{2,26},{10... | collective-permute-start | bytes 589832 | tf_op jit(solution)/shard_map/ppermute | solution.py:662
  57.8 18.7 %collective-permute-start.7 = (f32[192,256]{1,0:T(8,128)S(1)}, f32[192,256]{1,0:T(8,128)S(1)}, u32[]{:S(2)}, u32[]{:S(2)}) collective-permute-start(f32[192,256]{1,0:T(8,128)S(1)} %bitcast.6), channel_id=1, source_target_pairs={{0,2},{1,3},{2,0},{3,1},{4,6},{5,7},{6,4},{7,5},{8,10},{9,11},{10,... | collective-permute-start | bytes 589832 | tf_op jit(solution)/shard_map/ppermute | solution.py:613
  76.5 2.4 %collective-permute-start.30 = (f32[8,256]{1,0:T(8,128)S(1)}, f32[8,256]{1,0:T(8,128)S(1)}, u32[]{:S(2)}, u32[]{:S(2)}) collective-permute-start(f32[8,256]{1,0:T(8,128)S(1)} %get-tuple-element.51), channel_id=1, source_target_pairs={{0,24},{8,0},{16,8},{24,16},{1,25},{9,1},{17,9},{25,17},{2,26},{10... | collective-permute-start | bytes 24584 | tf_op jit(solution)/shard_map/ppermute | solution.py:662
  78.9 1.4 %collective-permute-done.30.refs_7_.refs_11_ = f32[8,256]{1,0:T(8,128)S(1)} collective-permute-done((f32[8,256]{1,0:T(8,128)S(1)}, f32[8,256]{1,0:T(8,128)S(1)}, u32[]{:S(2)}, u32[]{:S(2)}) %collective-permute-start.30) | collective-permute-done | bytes 8224 | tf_op jit(solution)/shard_map/ppermute | solution.py:662
  80.8 0.7 collective-permute-done.31.refs_8_.refs_12_
  81.6 1.0 collective-permute-done.33.refs_10_.refs_14_
  82.6 3.2 %collective-permute-start.39 = (f32[3,64,256]{2,1,0:T(8,128)S(1)}, f32[3,64,256]{2,1,0:T(8,128)S(1)}, u32[]{:S(2)}, u32[]{:S(2)}) collective-permute-start(f32[3,64,256]{2,1,0:T(8,128)S(1)} %get-tuple-element.54), channel_id=1, source_target_pairs={{0,24},{8,0},{16,8},{24,16},{1,25},{9,1},{17,9},{25,17},{2,26},{10... | collective-permute-start | bytes 589832 | tf_op jit(solution)/shard_map/ppermute | solution.py:662
  86.5 4.1 %collective-permute-done.35.refs_15_ = f32[8,256]{1,0:T(8,128)S(1)} collective-permute-done((f32[8,256]{1,0:T(8,128)S(1)}, f32[8,256]{1,0:T(8,128)S(1)}, u32[]{:S(2)}, u32[]{:S(2)}) %collective-permute-start.35) | collective-permute-done | bytes 8224 | tf_op jit(solution)/shard_map/ppermute | solution.py:662
  93.1 8.7 %collective-permute-start.40 = (f32[192,256]{1,0:T(8,128)S(1)}, f32[192,256]{1,0:T(8,128)S(1)}, u32[]{:S(2)}, u32[]{:S(2)}) collective-permute-start(f32[192,256]{1,0:T(8,128)S(1)} %shard_map.117.refs_8_), channel_id=1, source_target_pairs={{0,2},{1,3},{2,0},{3,1},{4,6},{5,7},{6,4},{7,5},{8,10},{9,11},{10,... | collective-permute-start | bytes 589832 | tf_op jit(solution)/shard_map/ppermute | solution.py:613
  102.7 5.0 %collective-permute-start.47 = (f32[64,256]{1,0:T(8,128)S(1)}, f32[64,256]{1,0:T(8,128)S(1)}, u32[]{:S(2)}, u32[]{:S(2)}) collective-permute-start(f32[64,256]{1,0:T(8,128)S(1)} %get-tuple-element.56), channel_id=1, source_target_pairs={{0,2},{1,3},{2,0},{3,1},{4,6},{5,7},{6,4},{7,5},{8,10},{9,11},{10,... | collective-permute-start | bytes 196616 | tf_op jit(solution)/shard_map/ppermute | solution.py:613
  107.6 6.3 %collective-permute-start.49 = (f32[32,256]{1,0:T(8,128)S(1)}, f32[32,256]{1,0:T(8,128)S(1)}, u32[]{:S(2)}, u32[]{:S(2)}) collective-permute-start(f32[32,256]{1,0:T(8,128)S(1)} %get-tuple-element.58), channel_id=1, source_target_pairs={{0,2},{1,3},{2,6},{3,7},{4,0},{5,1},{6,4},{7,5},{8,10},{9,11},{10,... | collective-permute-start | bytes 98312 | tf_op jit(solution)/shard_map/ppermute | solution.py:613
  114.0 1.8 %collective-permute-done.49.refs_19_ = f32[32,256]{1,0:T(8,128)S(1)} collective-permute-done((f32[32,256]{1,0:T(8,128)S(1)}, f32[32,256]{1,0:T(8,128)S(1)}, u32[]{:S(2)}, u32[]{:S(2)}) %collective-permute-start.49) | collective-permute-done | bytes 32800 | tf_op jit(solution)/shard_map/ppermute | solution.py:613
  117.3 1.0 collective-permute-done.53.refs_23_
  118.6 1.0 collective-permute-done.50.refs_20_
  119.9 1.5 %shard_map.112 = f32[128,256]{1,0:T(8,128)} custom-call(f32[128,256]{1,0:T(8,128)S(1)} %copy-done.2, f32[128,256]{1,0:T(8,128)S(1)} %copy-done.3, f32[192,256]{1,0:T(8,128)S(1)} %bitcast.8, f32[192,256]{1,0:T(8,128)S(1)} %collective-permute-done.7.refs_1_, f32[192,256]{1,0:T(8,128)S(1)} %collective-permute-done.8.refs_2_, ...), custom_call_target="tpu_custom_call" | custom-call | tf_op jit(solution)/shard_map/pallas_call | solution.py:236
  121.5 2.2 %shard_map.119 = (f32[128,256]{1,0:T(8,128)}, f32[128,256]{1,0:T(8,128)}, f32[1,128]{1,0:T(1,128)}, f32[3,32,256]{2,1,0:T(8,128)}) custom-call(f32[128,256]{1,0:T(8,128)S(1)} %copy-done, f32[128,256]{1,0:T(8,128)S(1)} %copy-done.1, f32[1,128]{1,0:T(1,128)S(1)} %bitcast.11, f32[192,256]{1,0:T(8,128)S(1)} %bitcast.9, ...), custom_call_target="tpu_custom_call" | custom-call | tf_op jit(solution)/shard_map/pallas_call | solution.py:236
  (96 shorter events, 11.2 us)
Async XLA Ops:
  2.1 18.7 %collective-permute-start = (f32[384,256]{1,0:T(8,128)S(1)}, f32[384,256]{1,0:T(8,128)S(1)}, u32[]{:S(2)}, u32[]{:S(2)}) collective-permute-start(f32[384,256]{1,0:T(8,128)S(1)} %get-tuple-element.35), channel_id=1, source_target_pairs={{0,2},{1,3},{2,0},{3,1},{4,6},{5,7},{6,4},{7,5},{8,10},{9,11},{10,... | collective-permute-start | bytes 1179656 | tf_op jit(solution)/shard_map/ppermute | solution.py:613
  5.3 15.6 %collective-permute-start.18 = (f32[256,256]{1,0:T(8,128)S(1)}, f32[256,256]{1,0:T(8,128)S(1)}, u32[]{:S(2)}, u32[]{:S(2)}) collective-permute-start(f32[256,256]{1,0:T(8,128)S(1)} %get-tuple-element.47.refs_0_), channel_id=1, source_target_pairs={{0,2},{1,3},{2,0},{3,1},{4,6},{5,7},{6,4},{7,5},{8,10},{9,11},{10,... | collective-permute-start | bytes 786440 | tf_op jit(solution)/shard_map/ppermute | solution.py:613
  5.3 22.5 %collective-permute-start.1 = (f32[320,256]{1,0:T(8,128)S(1)}, f32[320,256]{1,0:T(8,128)S(1)}, u32[]{:S(2)}, u32[]{:S(2)}) collective-permute-start(f32[320,256]{1,0:T(8,128)S(1)} %get-tuple-element.36), channel_id=1, source_target_pairs={{0,4},{1,5},{2,0},{3,1},{4,6},{5,7},{6,2},{7,3},{8,12},{9,13},{10,... | collective-permute-start | bytes 983048 | tf_op jit(solution)/shard_map/ppermute | solution.py:613
  8.3 19.6 %collective-permute-start.2 = (f32[320,256]{1,0:T(8,128)S(1)}, f32[320,256]{1,0:T(8,128)S(1)}, u32[]{:S(2)}, u32[]{:S(2)}) collective-permute-start(f32[320,256]{1,0:T(8,128)S(1)} %get-tuple-element.37), channel_id=1, source_target_pairs={{0,1},{1,0},{2,4},{3,5},{4,2},{5,3},{6,7},{7,6},{8,9},{9,8},{10,12... | collective-permute-start | bytes 983048 | tf_op jit(solution)/shard_map/ppermute | solution.py:613
  8.3 24.3 %collective-permute-start.19 = (f32[256,256]{1,0:T(8,128)S(1)}, f32[256,256]{1,0:T(8,128)S(1)}, u32[]{:S(2)}, u32[]{:S(2)}) collective-permute-start(f32[256,256]{1,0:T(8,128)S(1)} %get-tuple-element.47.refs_0_), channel_id=1, source_target_pairs={{0,4},{1,5},{2,0},{3,1},{4,6},{5,7},{6,2},{7,3},{8,12},{9,13},{10,... | collective-permute-start | bytes 786440 | tf_op jit(solution)/shard_map/ppermute | solution.py:613
  20.8 13.5 %collective-permute-start.3 = (f32[384,256]{1,0:T(8,128)S(1)}, f32[384,256]{1,0:T(8,128)S(1)}, u32[]{:S(2)}, u32[]{:S(2)}) collective-permute-start(f32[384,256]{1,0:T(8,128)S(1)} %get-tuple-element.34.refs_0_), channel_id=1, source_target_pairs={{0,1},{1,0},{2,3},{3,2},{4,5},{5,4},{6,7},{7,6},{8,9},{9,8},{10,11... | collective-permute-start | bytes 1179656 | tf_op jit(solution)/shard_map/ppermute | solution.py:47
  20.8 14.4 %collective-permute-start.4 = (f32[384,256]{1,0:T(8,128)S(1)}, f32[384,256]{1,0:T(8,128)S(1)}, u32[]{:S(2)}, u32[]{:S(2)}) collective-permute-start(f32[384,256]{1,0:T(8,128)S(1)} %collective-permute-done.refs_1_), channel_id=1, source_target_pairs={{0,1},{1,0},{2,3},{3,2},{4,5},{5,4},{6,7},{7,6},{8,9},{9,8},{10,11... | collective-permute-start | bytes 1179656 | tf_op jit(solution)/shard_map/ppermute | solution.py:47
  27.9 6.8 %collective-permute-start.5 = (f32[320,256]{1,0:T(8,128)S(1)}, f32[320,256]{1,0:T(8,128)S(1)}, u32[]{:S(2)}, u32[]{:S(2)}) collective-permute-start(f32[320,256]{1,0:T(8,128)S(1)} %collective-permute-done.1.refs_2_), channel_id=1, source_target_pairs={{0,1},{1,0},{2,3},{3,2},{4,5},{5,4},{6,7},{7,6},{8,9},{9,8},{10,11... | collective-permute-start | bytes 983048 | tf_op jit(solution)/shard_map/ppermute | solution.py:47
  27.9 7.0 %collective-permute-start.6 = (f32[320,256]{1,0:T(8,128)S(1)}, f32[320,256]{1,0:T(8,128)S(1)}, u32[]{:S(2)}, u32[]{:S(2)}) collective-permute-start(f32[320,256]{1,0:T(8,128)S(1)} %collective-permute-done.2.refs_3_), channel_id=1, source_target_pairs={{0,1},{1,0},{2,3},{3,2},{4,5},{5,4},{6,7},{7,6},{8,9},{9,8},{10,11... | collective-permute-start | bytes 983048 | tf_op jit(solution)/shard_map/ppermute | solution.py:47
  34.2 6.7 %collective-permute-start.21 = (f32[256,256]{1,0:T(8,128)S(1)}, f32[256,256]{1,0:T(8,128)S(1)}, u32[]{:S(2)}, u32[]{:S(2)}) collective-permute-start(f32[256,256]{1,0:T(8,128)S(1)} %get-tuple-element.47.refs_0_), channel_id=1, source_target_pairs={{0,1},{1,0},{2,3},{3,2},{4,5},{5,4},{6,7},{7,6},{8,9},{9,8},{10,11... | collective-permute-start | bytes 786440 | tf_op jit(solution)/shard_map/ppermute | solution.py:47
  34.3 6.5 %collective-permute-start.22 = (f32[256,256]{1,0:T(8,128)S(1)}, f32[256,256]{1,0:T(8,128)S(1)}, u32[]{:S(2)}, u32[]{:S(2)}) collective-permute-start(f32[256,256]{1,0:T(8,128)S(1)} %collective-permute-done.18.refs_1_), channel_id=1, source_target_pairs={{0,1},{1,0},{2,3},{3,2},{4,5},{5,4},{6,7},{7,6},{8,9},{9,8},{10,11... | collective-permute-start | bytes 786440 | tf_op jit(solution)/shard_map/ppermute | solution.py:47
  34.7 6.2 %collective-permute-start.23 = (f32[256,256]{1,0:T(8,128)S(1)}, f32[256,256]{1,0:T(8,128)S(1)}, u32[]{:S(2)}, u32[]{:S(2)}) collective-permute-start(f32[256,256]{1,0:T(8,128)S(1)} %collective-permute-done.19.refs_2_), channel_id=1, source_target_pairs={{0,1},{1,0},{2,3},{3,2},{4,5},{5,4},{6,7},{7,6},{8,9},{9,8},{10,11... | collective-permute-start | bytes 786440 | tf_op jit(solution)/shard_map/ppermute | solution.py:47
  34.8 6.0 %collective-permute-start.24 = (f32[256,256]{1,0:T(8,128)S(1)}, f32[256,256]{1,0:T(8,128)S(1)}, u32[]{:S(2)}, u32[]{:S(2)}) collective-permute-start(f32[256,256]{1,0:T(8,128)S(1)} %collective-permute-done.20.refs_3_), channel_id=1, source_target_pairs={{0,1},{1,0},{2,3},{3,2},{4,5},{5,4},{6,7},{7,6},{8,9},{9,8},{10,11... | collective-permute-start | bytes 786440 | tf_op jit(solution)/shard_map/ppermute | solution.py:47
  39.2 7.9 %collective-permute-start.17 = (f32[3,64,256]{2,1,0:T(8,128)S(1)}, f32[3,64,256]{2,1,0:T(8,128)S(1)}, u32[]{:S(2)}, u32[]{:S(2)}) collective-permute-start(f32[3,64,256]{2,1,0:T(8,128)S(1)} %get-tuple-element.39.refs_1_), channel_id=1, source_target_pairs={{0,8},{8,16},{16,24},{24,0},{1,9},{9,17},{17,25},{25,1},{2,10},{10... | collective-permute-start | bytes 589832 | tf_op jit(solution)/shard_map/ppermute | solution.py:667
  47.1 8.0 %collective-permute-start.29 = (f32[3,64,256]{2,1,0:T(8,128)S(1)}, f32[3,64,256]{2,1,0:T(8,128)S(1)}, u32[]{:S(2)}, u32[]{:S(2)}) collective-permute-start(f32[3,64,256]{2,1,0:T(8,128)S(1)} %get-tuple-element.49), channel_id=1, source_target_pairs={{0,24},{8,0},{16,8},{24,16},{1,25},{9,1},{17,9},{25,17},{2,26},{10... | collective-permute-start | bytes 589832 | tf_op jit(solution)/shard_map/ppermute | solution.py:662
  48.8 27.6 %collective-permute-start.8 = (f32[192,256]{1,0:T(8,128)S(1)}, f32[192,256]{1,0:T(8,128)S(1)}, u32[]{:S(2)}, u32[]{:S(2)}) collective-permute-start(f32[192,256]{1,0:T(8,128)S(1)} %bitcast.5), channel_id=1, source_target_pairs={{0,1},{1,0},{2,4},{3,5},{4,2},{5,3},{6,7},{7,6},{8,9},{9,8},{10,12... | collective-permute-start | bytes 589832 | tf_op jit(solution)/shard_map/ppermute | solution.py:613
  55.1 27.5 %collective-permute-start.34 = (f32[3,64,256]{2,1,0:T(8,128)S(1)}, f32[3,64,256]{2,1,0:T(8,128)S(1)}, u32[]{:S(2)}, u32[]{:S(2)}) collective-permute-start(f32[3,64,256]{2,1,0:T(8,128)S(1)} %get-tuple-element.52), channel_id=1, source_target_pairs={{0,24},{8,0},{16,8},{24,16},{1,25},{9,1},{17,9},{25,17},{2,26},{10... | collective-permute-start | bytes 589832 | tf_op jit(solution)/shard_map/ppermute | solution.py:662
  57.8 28.6 %collective-permute-start.7 = (f32[192,256]{1,0:T(8,128)S(1)}, f32[192,256]{1,0:T(8,128)S(1)}, u32[]{:S(2)}, u32[]{:S(2)}) collective-permute-start(f32[192,256]{1,0:T(8,128)S(1)} %bitcast.6), channel_id=1, source_target_pairs={{0,2},{1,3},{2,0},{3,1},{4,6},{5,7},{6,4},{7,5},{8,10},{9,11},{10,... | collective-permute-start | bytes 589832 | tf_op jit(solution)/shard_map/ppermute | solution.py:613
  76.5 14.0 %collective-permute-start.9 = (f32[192,256]{1,0:T(8,128)S(1)}, f32[192,256]{1,0:T(8,128)S(1)}, u32[]{:S(2)}, u32[]{:S(2)}) collective-permute-start(f32[192,256]{1,0:T(8,128)S(1)} %collective-permute-done.8.refs_2_), channel_id=1, source_target_pairs={{0,2},{1,3},{2,0},{3,1},{4,6},{5,7},{6,4},{7,5},{8,10},{9,11},{10,... | collective-permute-start | bytes 589832 | tf_op jit(solution)/shard_map/ppermute | solution.py:613
  82.6 10.4 %collective-permute-start.39 = (f32[3,64,256]{2,1,0:T(8,128)S(1)}, f32[3,64,256]{2,1,0:T(8,128)S(1)}, u32[]{:S(2)}, u32[]{:S(2)}) collective-permute-start(f32[3,64,256]{2,1,0:T(8,128)S(1)} %get-tuple-element.54), channel_id=1, source_target_pairs={{0,24},{8,0},{16,8},{24,16},{1,25},{9,1},{17,9},{25,17},{2,26},{10... | collective-permute-start | bytes 589832 | tf_op jit(solution)/shard_map/ppermute | solution.py:662
  85.9 15.9 %collective-permute-start.10 = (f32[192,256]{1,0:T(8,128)S(1)}, f32[192,256]{1,0:T(8,128)S(1)}, u32[]{:S(2)}, u32[]{:S(2)}) collective-permute-start(f32[192,256]{1,0:T(8,128)S(1)} %bitcast.7), channel_id=1, source_target_pairs={{0,1},{1,0},{2,3},{3,2},{4,5},{5,4},{6,7},{7,6},{8,9},{9,8},{10,11... | collective-permute-start | bytes 589832 | tf_op jit(solution)/shard_map/ppermute | solution.py:47
  85.9 16.0 %collective-permute-start.12 = (f32[192,256]{1,0:T(8,128)S(1)}, f32[192,256]{1,0:T(8,128)S(1)}, u32[]{:S(2)}, u32[]{:S(2)}) collective-permute-start(f32[192,256]{1,0:T(8,128)S(1)} %collective-permute-done.8.refs_2_), channel_id=1, source_target_pairs={{0,1},{1,0},{2,3},{3,2},{4,5},{5,4},{6,7},{7,6},{8,9},{9,8},{10,11... | collective-permute-start | bytes 589832 | tf_op jit(solution)/shard_map/ppermute | solution.py:47
  91.9 10.7 %collective-permute-start.11 = (f32[192,256]{1,0:T(8,128)S(1)}, f32[192,256]{1,0:T(8,128)S(1)}, u32[]{:S(2)}, u32[]{:S(2)}) collective-permute-start(f32[192,256]{1,0:T(8,128)S(1)} %collective-permute-done.7.refs_1_), channel_id=1, source_target_pairs={{0,1},{1,0},{2,3},{3,2},{4,5},{5,4},{6,7},{7,6},{8,9},{9,8},{10,11... | collective-permute-start | bytes 589832 | tf_op jit(solution)/shard_map/ppermute | solution.py:47
  92.9 9.8 %collective-permute-start.13 = (f32[192,256]{1,0:T(8,128)S(1)}, f32[192,256]{1,0:T(8,128)S(1)}, u32[]{:S(2)}, u32[]{:S(2)}) collective-permute-start(f32[192,256]{1,0:T(8,128)S(1)} %collective-permute-done.9.refs_3_), channel_id=1, source_target_pairs={{0,1},{1,0},{2,3},{3,2},{4,5},{5,4},{6,7},{7,6},{8,9},{9,8},{10,11... | collective-permute-start | bytes 589832 | tf_op jit(solution)/shard_map/ppermute | solution.py:47
  93.1 23.2 %collective-permute-start.40 = (f32[192,256]{1,0:T(8,128)S(1)}, f32[192,256]{1,0:T(8,128)S(1)}, u32[]{:S(2)}, u32[]{:S(2)}) collective-permute-start(f32[192,256]{1,0:T(8,128)S(1)} %shard_map.117.refs_8_), channel_id=1, source_target_pairs={{0,2},{1,3},{2,0},{3,1},{4,6},{5,7},{6,4},{7,5},{8,10},{9,11},{10,... | collective-permute-start | bytes 589832 | tf_op jit(solution)/shard_map/ppermute | solution.py:613
  101.8 14.6 %collective-permute-start.41 = (f32[192,256]{1,0:T(8,128)S(1)}, f32[192,256]{1,0:T(8,128)S(1)}, u32[]{:S(2)}, u32[]{:S(2)}) collective-permute-start(f32[192,256]{1,0:T(8,128)S(1)} %shard_map.117.refs_8_), channel_id=1, source_target_pairs={{0,1},{1,0},{2,4},{3,5},{4,2},{5,3},{6,7},{7,6},{8,9},{9,8},{10,12... | collective-permute-start | bytes 589832 | tf_op jit(solution)/shard_map/ppermute | solution.py:613
  101.9 15.0 %collective-permute-start.42 = (f32[192,256]{1,0:T(8,128)S(1)}, f32[192,256]{1,0:T(8,128)S(1)}, u32[]{:S(2)}, u32[]{:S(2)}) collective-permute-start(f32[192,256]{1,0:T(8,128)S(1)} %shard_map.117.refs_8_), channel_id=1, source_target_pairs={{0,2},{1,3},{2,6},{3,7},{4,0},{5,1},{6,4},{7,5},{8,10},{9,11},{10,... | collective-permute-start | bytes 589832 | tf_op jit(solution)/shard_map/ppermute | solution.py:613
  102.6 5.1 %collective-permute-start.48 = (f32[32,256]{1,0:T(8,128)S(1)}, f32[32,256]{1,0:T(8,128)S(1)}, u32[]{:S(2)}, u32[]{:S(2)}) collective-permute-start(f32[32,256]{1,0:T(8,128)S(1)} %get-tuple-element.57), channel_id=1, source_target_pairs={{0,1},{1,0},{2,4},{3,5},{4,2},{5,3},{6,7},{7,6},{8,9},{9,8},{10,12... | collective-permute-start | bytes 98312 | tf_op jit(solution)/shard_map/ppermute | solution.py:613
  102.7 13.1 %collective-permute-start.47 = (f32[64,256]{1,0:T(8,128)S(1)}, f32[64,256]{1,0:T(8,128)S(1)}, u32[]{:S(2)}, u32[]{:S(2)}) collective-permute-start(f32[64,256]{1,0:T(8,128)S(1)} %get-tuple-element.56), channel_id=1, source_target_pairs={{0,2},{1,3},{2,0},{3,1},{4,6},{5,7},{6,4},{7,5},{8,10},{9,11},{10,... | collective-permute-start | bytes 196616 | tf_op jit(solution)/shard_map/ppermute | solution.py:613
  107.6 8.1 %collective-permute-start.49 = (f32[32,256]{1,0:T(8,128)S(1)}, f32[32,256]{1,0:T(8,128)S(1)}, u32[]{:S(2)}, u32[]{:S(2)}) collective-permute-start(f32[32,256]{1,0:T(8,128)S(1)} %get-tuple-element.58), channel_id=1, source_target_pairs={{0,2},{1,3},{2,6},{3,7},{4,0},{5,1},{6,4},{7,5},{8,10},{9,11},{10,... | collective-permute-start | bytes 98312 | tf_op jit(solution)/shard_map/ppermute | solution.py:613
  115.8 5.6 %collective-permute-start.43 = (f32[192,256]{1,0:T(8,128)S(1)}, f32[192,256]{1,0:T(8,128)S(1)}, u32[]{:S(2)}, u32[]{:S(2)}) collective-permute-start(f32[192,256]{1,0:T(8,128)S(1)} %shard_map.117.refs_8_), channel_id=1, source_target_pairs={{0,1},{1,0},{2,3},{3,2},{4,5},{5,4},{6,7},{7,6},{8,9},{9,8},{10,11... | collective-permute-start | bytes 589832 | tf_op jit(solution)/shard_map/ppermute | solution.py:47
  116.3 5.1 %collective-permute-start.44 = (f32[192,256]{1,0:T(8,128)S(1)}, f32[192,256]{1,0:T(8,128)S(1)}, u32[]{:S(2)}, u32[]{:S(2)}) collective-permute-start(f32[192,256]{1,0:T(8,128)S(1)} %collective-permute-done.40.refs_9_), channel_id=1, source_target_pairs={{0,1},{1,0},{2,3},{3,2},{4,5},{5,4},{6,7},{7,6},{8,9},{9,8},{10,11... | collective-permute-start | bytes 589832 | tf_op jit(solution)/shard_map/ppermute | solution.py:47
  (27 other events, 154.7 us)

commit v5 on v4

--- a/solution.py
+++ b/solution.py
@@ -220,7 +220,9 @@
     def one(a, b):
         return lax.dot_general(a, b, (((1,), (contract,)), ((), ())), preferred_element_type=jnp.float32)
 
-    return one(left[0], right[0]) + (one(left[0], right[1]) + one(left[1], right[0]))
+    rows = left[0].shape[0]
+    upper = one(jnp.concatenate(left), right[0])
+    return upper[:rows] + (upper[rows:] + one(left[0], right[1]))
 
 
 def nn(left, right):
@@ -270,7 +272,7 @@
 
 CHIPS = 4
 LOW, HIGH_CHIP = 1, 2
-CHUNK = 256
+CHUNK = 512
 PACK_LIMIT = 61 * 1024 * 1024
 
 
@@ -397,10 +399,10 @@
         pair = halves(jnp.concatenate([own[0], own[1]]))
         second = halves(own[2])
         out_pair, out_second = 0.0, 0.0
-        for index in range(0, len(pieces), 2):
-            one, two = pieces[index], pieces[index + 1]
-            query = halves(jnp.concatenate([one[:depth, :], two[:depth, :]]))
-            cot = halves(jnp.concatenate([one[depth:, :], two[depth:, :]]))
+        step = CHUNK // depth
+        for index in range(0, len(pieces), step):
+            query = halves(jnp.concatenate([piece[:depth, :] for piece in pieces[index : index + step]]))
+            cot = halves(jnp.concatenate([piece[depth:, :] for piece in pieces[index : index + step]]))
             both = nt(pair, query)
             d_mixed = nt(second, cot)
             first, gate = both[:span], both[span:]

time: 124 us -> 121 us (0.976)
  starting transfers between devices: 67.9 us -> 64.4 us
    ppermute x19, starting transfers between devices: 47.5 us -> 45.3 us  [over_chips(): return lax.ppermute(array, 'tok', pairs)]
    ppermute x6, starting transfers between devices: 11.5 us -> 10.2 us  [to_earlier(): lax.ppermute(array, 'block', [(i, (i - 1) % groups) for i in range(groups)])]
where the time goes in v5:
time: 121 us; the launch traced here: 120 us
  starting transfers between devices  64.4 us (53%)
  waiting for transfers between devices  50.2 us (41%)
  Pallas kernels  4.92 us (4%)
    ppermute x19, starting transfers between devices, over_chips(): return lax.ppermute(array, 'tok', pairs)  45.3 us
    ppermute x19, waiting for transfers between devices, over_chips(): return lax.ppermute(array, 'tok', pairs)  28.5 us
    ppermute x6, starting transfers between devices, to_earlier(): lax.ppermute(array, 'block', [(i, (i - 1) % groups) for i in range(groups)])  10.2 us
    ppermute x6, waiting for transfers between devices, to_earlier(): lax.ppermute(array, 'block', [(i, (i - 1) % groups) for i in range(groups)])  9.2 us
    ppermute x1, waiting for transfers between devices, to_later(): lax.ppermute(array, 'block', [(i, (i + 1) % groups) for i in range(groups)])  6.19 us
    ppermute x24, starting transfers between devices, core_swap(): return lax.ppermute(array, 'tok', [(j, j ^ 1) for j in range(size)])  5.55 us
    ppermute x24, waiting for transfers between devices, core_swap(): return lax.ppermute(array, 'tok', [(j, j ^ 1) for j in range(size)])  5.15 us
    pallas_call x10, Pallas kernels, kernel_call(): pl.pallas_call(body, in_specs=[pl.BlockSpec(memory_space=space) for _ in...  4.92 us
  transfers between devices with their start and end apart: 54, of which 22 were waited for; matrix products, arithmetic and copies ran while one was open for 0% of the time, Pallas kernels for 1%

profile of v5, /device:TPU:0, one launch (start us, length us, event | category | flops | bytes accessed | tf_op | source)
XLA Modules:
  0.0 120.4 jit_solution(4432867645720698504)
XLA Ops:
  0.6 1.5 %shard_map.110 = (f32[384,256]{1,0:T(8,128)S(1)}, f32[384,256]{1,0:T(8,128)S(1)}, f32[320,256]{1,0:T(8,128)S(1)}, f32[320,256]{1,0:T(8,128)S(1)}, f32[256,256]{1,0:T(8,128)S(1)}) custom-call(f32[128,256]{1,0:T(8,128)} %keys.1, f32[128,256]{1,0:T(8,128)} %values.1, f32[1,128]{1,0:T(1,128)} %bitcast.10, f32[3,32,256]{2,1,0:T(8,128)} %bitcast.12, ...), custom_call_target="tpu_custom_call" | custom-call | tf_op jit(solution)/shard_map/pallas_call | solution.py:238
  2.1 3.1 %collective-permute-start = (f32[384,256]{1,0:T(8,128)S(1)}, f32[384,256]{1,0:T(8,128)S(1)}, u32[]{:S(2)}, u32[]{:S(2)}) collective-permute-start(f32[384,256]{1,0:T(8,128)S(1)} %get-tuple-element.35), channel_id=1, source_target_pairs={{0,2},{1,3},{2,0},{3,1},{4,6},{5,7},{6,4},{7,5},{8,10},{9,11},{10,... | collective-permute-start | bytes 1179656 | tf_op jit(solution)/shard_map/ppermute | solution.py:615
  5.3 3.0 %collective-permute-start.1 = (f32[320,256]{1,0:T(8,128)S(1)}, f32[320,256]{1,0:T(8,128)S(1)}, u32[]{:S(2)}, u32[]{:S(2)}) collective-permute-start(f32[320,256]{1,0:T(8,128)S(1)} %get-tuple-element.36), channel_id=1, source_target_pairs={{0,4},{1,5},{2,0},{3,1},{4,6},{5,7},{6,2},{7,3},{8,12},{9,13},{10,... | collective-permute-start | bytes 983048 | tf_op jit(solution)/shard_map/ppermute | solution.py:615
  8.3 1.6 %collective-permute-start.19 = (f32[256,256]{1,0:T(8,128)S(1)}, f32[256,256]{1,0:T(8,128)S(1)}, u32[]{:S(2)}, u32[]{:S(2)}) collective-permute-start(f32[256,256]{1,0:T(8,128)S(1)} %get-tuple-element.47.refs_0_), channel_id=1, source_target_pairs={{0,4},{1,5},{2,0},{3,1},{4,6},{5,7},{6,2},{7,3},{8,12},{9,13},{10,... | collective-permute-start | bytes 786440 | tf_op jit(solution)/shard_map/ppermute | solution.py:615
  9.9 11.0 %collective-permute-done.18.refs_1_ = f32[256,256]{1,0:T(8,128)S(1)} collective-permute-done((f32[256,256]{1,0:T(8,128)S(1)}, f32[256,256]{1,0:T(8,128)S(1)}, u32[]{:S(2)}, u32[]{:S(2)}) %collective-permute-start.18) | collective-permute-done | bytes 262176 | tf_op jit(solution)/shard_map/ppermute | solution.py:615
  21.4 6.5 %collective-permute-done.1.refs_2_ = f32[320,256]{1,0:T(8,128)S(1)} collective-permute-done((f32[320,256]{1,0:T(8,128)S(1)}, f32[320,256]{1,0:T(8,128)S(1)}, u32[]{:S(2)}, u32[]{:S(2)}) %collective-permute-start.1) | collective-permute-done | bytes 327712 | tf_op jit(solution)/shard_map/ppermute | solution.py:615
  28.4 4.3 %collective-permute-done.19.refs_2_ = f32[256,256]{1,0:T(8,128)S(1)} collective-permute-done((f32[256,256]{1,0:T(8,128)S(1)}, f32[256,256]{1,0:T(8,128)S(1)}, u32[]{:S(2)}, u32[]{:S(2)}) %collective-permute-start.19) | collective-permute-done | bytes 262176 | tf_op jit(solution)/shard_map/ppermute | solution.py:615
  32.6 1.5 %collective-permute-done.20.refs_3_ = f32[256,256]{1,0:T(8,128)S(1)} collective-permute-done((f32[256,256]{1,0:T(8,128)S(1)}, f32[256,256]{1,0:T(8,128)S(1)}, u32[]{:S(2)}, u32[]{:S(2)}) %collective-permute-start.20) | collective-permute-done | bytes 262176 | tf_op jit(solution)/shard_map/ppermute | solution.py:615
  35.4 1.4 %collective-permute-done.14.refs_4_ = f32[8,256]{1,0:T(8,128)S(1)} collective-permute-done((f32[8,256]{1,0:T(8,128)S(1)}, f32[8,256]{1,0:T(8,128)S(1)}, u32[]{:S(2)}, u32[]{:S(2)}) %collective-permute-start.14) | collective-permute-done | bytes 8224 | tf_op jit(solution)/shard_map/ppermute | solution.py:615
  37.0 1.0 collective-permute-done.15.refs_5_
  38.2 1.0 collective-permute-done.16.refs_6_
  39.2 1.7 %collective-permute-start.17 = (f32[3,64,256]{2,1,0:T(8,128)S(1)}, f32[3,64,256]{2,1,0:T(8,128)S(1)}, u32[]{:S(2)}, u32[]{:S(2)}) collective-permute-start(f32[3,64,256]{2,1,0:T(8,128)S(1)} %get-tuple-element.39.refs_1_), channel_id=1, source_target_pairs={{0,8},{8,16},{16,24},{24,0},{1,9},{9,17},{17,25},{25,1},{2,10},{10... | collective-permute-start | bytes 589832 | tf_op jit(solution)/shard_map/ppermute | solution.py:669
  40.9 6.2 %collective-permute-done.17.earlier.refs_18_ = f32[3,64,256]{2,1,0:T(8,128)S(1)} collective-permute-done((f32[3,64,256]{2,1,0:T(8,128)S(1)}, f32[3,64,256]{2,1,0:T(8,128)S(1)}, u32[]{:S(2)}, u32[]{:S(2)}) %collective-permute-start.17) | collective-permute-done | bytes 196640 | tf_op jit(solution)/shard_map/ppermute | solution.py:669
  47.1 1.8 %collective-permute-start.29 = (f32[3,64,256]{2,1,0:T(8,128)S(1)}, f32[3,64,256]{2,1,0:T(8,128)S(1)}, u32[]{:S(2)}, u32[]{:S(2)}) collective-permute-start(f32[3,64,256]{2,1,0:T(8,128)S(1)} %get-tuple-element.49), channel_id=1, source_target_pairs={{0,24},{8,0},{16,8},{24,16},{1,25},{9,1},{17,9},{25,17},{2,26},{10... | collective-permute-start | bytes 589832 | tf_op jit(solution)/shard_map/ppermute | solution.py:664
  48.8 1.4 %collective-permute-start.25 = (f32[8,256]{1,0:T(8,128)S(1)}, f32[8,256]{1,0:T(8,128)S(1)}, u32[]{:S(2)}, u32[]{:S(2)}) collective-permute-start(f32[8,256]{1,0:T(8,128)S(1)} %get-tuple-element.48), channel_id=1, source_target_pairs={{0,24},{8,0},{16,8},{24,16},{1,25},{9,1},{17,9},{25,17},{2,26},{10... | collective-permute-start | bytes 24584 | tf_op jit(solution)/shard_map/ppermute | solution.py:664
  50.3 3.1 %collective-permute-done.25.refs_7_ = f32[8,256]{1,0:T(8,128)S(1)} collective-permute-done((f32[8,256]{1,0:T(8,128)S(1)}, f32[8,256]{1,0:T(8,128)S(1)}, u32[]{:S(2)}, u32[]{:S(2)}) %collective-permute-start.25) | collective-permute-done | bytes 8224 | tf_op jit(solution)/shard_map/ppermute | solution.py:664
  55.1 2.7 %collective-permute-start.34 = (f32[3,64,256]{2,1,0:T(8,128)S(1)}, f32[3,64,256]{2,1,0:T(8,128)S(1)}, u32[]{:S(2)}, u32[]{:S(2)}) collective-permute-start(f32[3,64,256]{2,1,0:T(8,128)S(1)} %get-tuple-element.52), channel_id=1, source_target_pairs={{0,24},{8,0},{16,8},{24,16},{1,25},{9,1},{17,9},{25,17},{2,26},{10... | collective-permute-start | bytes 589832 | tf_op jit(solution)/shard_map/ppermute | solution.py:664
  57.8 17.1 %collective-permute-start.7 = (f32[192,256]{1,0:T(8,128)S(1)}, f32[192,256]{1,0:T(8,128)S(1)}, u32[]{:S(2)}, u32[]{:S(2)}) collective-permute-start(f32[192,256]{1,0:T(8,128)S(1)} %bitcast.6), channel_id=1, source_target_pairs={{0,2},{1,3},{2,0},{3,1},{4,6},{5,7},{6,4},{7,5},{8,10},{9,11},{10,... | collective-permute-start | bytes 589832 | tf_op jit(solution)/shard_map/ppermute | solution.py:615
  74.9 1.7 %collective-permute-start.30 = (f32[8,256]{1,0:T(8,128)S(1)}, f32[8,256]{1,0:T(8,128)S(1)}, u32[]{:S(2)}, u32[]{:S(2)}) collective-permute-start(f32[8,256]{1,0:T(8,128)S(1)} %get-tuple-element.51), channel_id=1, source_target_pairs={{0,24},{8,0},{16,8},{24,16},{1,25},{9,1},{17,9},{25,17},{2,26},{10... | collective-permute-start | bytes 24584 | tf_op jit(solution)/shard_map/ppermute | solution.py:664
  76.6 2.0 %collective-permute-done.30.refs_7_.refs_11_ = f32[8,256]{1,0:T(8,128)S(1)} collective-permute-done((f32[8,256]{1,0:T(8,128)S(1)}, f32[8,256]{1,0:T(8,128)S(1)}, u32[]{:S(2)}, u32[]{:S(2)}) %collective-permute-start.30) | collective-permute-done | bytes 8224 | tf_op jit(solution)/shard_map/ppermute | solution.py:664
  79.1 0.7 collective-permute-done.31.refs_8_.refs_12_
  79.9 1.0 collective-permute-done.33.refs_10_.refs_14_
  80.9 2.6 %collective-permute-start.39 = (f32[3,64,256]{2,1,0:T(8,128)S(1)}, f32[3,64,256]{2,1,0:T(8,128)S(1)}, u32[]{:S(2)}, u32[]{:S(2)}) collective-permute-start(f32[3,64,256]{2,1,0:T(8,128)S(1)} %get-tuple-element.54), channel_id=1, source_target_pairs={{0,24},{8,0},{16,8},{24,16},{1,25},{9,1},{17,9},{25,17},{2,26},{10... | collective-permute-start | bytes 589832 | tf_op jit(solution)/shard_map/ppermute | solution.py:664
  84.1 4.1 %collective-permute-done.35.refs_15_ = f32[8,256]{1,0:T(8,128)S(1)} collective-permute-done((f32[8,256]{1,0:T(8,128)S(1)}, f32[8,256]{1,0:T(8,128)S(1)}, u32[]{:S(2)}, u32[]{:S(2)}) %collective-permute-start.35) | collective-permute-done | bytes 8224 | tf_op jit(solution)/shard_map/ppermute | solution.py:664
  90.8 8.1 %collective-permute-start.40 = (f32[192,256]{1,0:T(8,128)S(1)}, f32[192,256]{1,0:T(8,128)S(1)}, u32[]{:S(2)}, u32[]{:S(2)}) collective-permute-start(f32[192,256]{1,0:T(8,128)S(1)} %shard_map.117.refs_8_), channel_id=1, source_target_pairs={{0,2},{1,3},{2,0},{3,1},{4,6},{5,7},{6,4},{7,5},{8,10},{9,11},{10,... | collective-permute-start | bytes 589832 | tf_op jit(solution)/shard_map/ppermute | solution.py:615
  99.7 4.3 %collective-permute-start.47 = (f32[64,256]{1,0:T(8,128)S(1)}, f32[64,256]{1,0:T(8,128)S(1)}, u32[]{:S(2)}, u32[]{:S(2)}) collective-permute-start(f32[64,256]{1,0:T(8,128)S(1)} %get-tuple-element.56), channel_id=1, source_target_pairs={{0,2},{1,3},{2,0},{3,1},{4,6},{5,7},{6,4},{7,5},{8,10},{9,11},{10,... | collective-permute-start | bytes 196616 | tf_op jit(solution)/shard_map/ppermute | solution.py:615
  104.0 7.1 %collective-permute-start.49 = (f32[32,256]{1,0:T(8,128)S(1)}, f32[32,256]{1,0:T(8,128)S(1)}, u32[]{:S(2)}, u32[]{:S(2)}) collective-permute-start(f32[32,256]{1,0:T(8,128)S(1)} %get-tuple-element.58), channel_id=1, source_target_pairs={{0,2},{1,3},{2,6},{3,7},{4,0},{5,1},{6,4},{7,5},{8,10},{9,11},{10,... | collective-permute-start | bytes 98312 | tf_op jit(solution)/shard_map/ppermute | solution.py:615
  111.1 1.8 %collective-permute-done.49.refs_19_ = f32[32,256]{1,0:T(8,128)S(1)} collective-permute-done((f32[32,256]{1,0:T(8,128)S(1)}, f32[32,256]{1,0:T(8,128)S(1)}, u32[]{:S(2)}, u32[]{:S(2)}) %collective-permute-start.49) | collective-permute-done | bytes 32800 | tf_op jit(solution)/shard_map/ppermute | solution.py:615
  114.5 1.0 collective-permute-done.53.refs_23_
  115.8 1.0 collective-permute-done.50.refs_20_
  117.1 1.4 %shard_map.112 = f32[128,256]{1,0:T(8,128)} custom-call(f32[128,256]{1,0:T(8,128)S(1)} %copy-done.2, f32[128,256]{1,0:T(8,128)S(1)} %copy-done.3, f32[192,256]{1,0:T(8,128)S(1)} %bitcast.8, f32[192,256]{1,0:T(8,128)S(1)} %collective-permute-done.7.refs_1_, f32[192,256]{1,0:T(8,128)S(1)} %collective-permute-done.8.refs_2_, ...), custom_call_target="tpu_custom_call" | custom-call | tf_op jit(solution)/shard_map/pallas_call | solution.py:238
  118.5 1.9 %shard_map.119 = (f32[128,256]{1,0:T(8,128)}, f32[128,256]{1,0:T(8,128)}, f32[1,128]{1,0:T(1,128)}, f32[3,32,256]{2,1,0:T(8,128)}) custom-call(f32[128,256]{1,0:T(8,128)S(1)} %copy-done, f32[128,256]{1,0:T(8,128)S(1)} %copy-done.1, f32[1,128]{1,0:T(1,128)S(1)} %bitcast.11, f32[192,256]{1,0:T(8,128)S(1)} %bitcast.9, ...), custom_call_target="tpu_custom_call" | custom-call | tf_op jit(solution)/shard_map/pallas_call | solution.py:238
  (96 shorter events, 11.1 us)
Async XLA Ops:
  2.1 18.7 %collective-permute-start = (f32[384,256]{1,0:T(8,128)S(1)}, f32[384,256]{1,0:T(8,128)S(1)}, u32[]{:S(2)}, u32[]{:S(2)}) collective-permute-start(f32[384,256]{1,0:T(8,128)S(1)} %get-tuple-element.35), channel_id=1, source_target_pairs={{0,2},{1,3},{2,0},{3,1},{4,6},{5,7},{6,4},{7,5},{8,10},{9,11},{10,... | collective-permute-start | bytes 1179656 | tf_op jit(solution)/shard_map/ppermute | solution.py:615
  5.3 15.6 %collective-permute-start.18 = (f32[256,256]{1,0:T(8,128)S(1)}, f32[256,256]{1,0:T(8,128)S(1)}, u32[]{:S(2)}, u32[]{:S(2)}) collective-permute-start(f32[256,256]{1,0:T(8,128)S(1)} %get-tuple-element.47.refs_0_), channel_id=1, source_target_pairs={{0,2},{1,3},{2,0},{3,1},{4,6},{5,7},{6,4},{7,5},{8,10},{9,11},{10,... | collective-permute-start | bytes 786440 | tf_op jit(solution)/shard_map/ppermute | solution.py:615
  5.3 22.5 %collective-permute-start.1 = (f32[320,256]{1,0:T(8,128)S(1)}, f32[320,256]{1,0:T(8,128)S(1)}, u32[]{:S(2)}, u32[]{:S(2)}) collective-permute-start(f32[320,256]{1,0:T(8,128)S(1)} %get-tuple-element.36), channel_id=1, source_target_pairs={{0,4},{1,5},{2,0},{3,1},{4,6},{5,7},{6,2},{7,3},{8,12},{9,13},{10,... | collective-permute-start | bytes 983048 | tf_op jit(solution)/shard_map/ppermute | solution.py:615
  8.3 19.6 %collective-permute-start.2 = (f32[320,256]{1,0:T(8,128)S(1)}, f32[320,256]{1,0:T(8,128)S(1)}, u32[]{:S(2)}, u32[]{:S(2)}) collective-permute-start(f32[320,256]{1,0:T(8,128)S(1)} %get-tuple-element.37), channel_id=1, source_target_pairs={{0,1},{1,0},{2,4},{3,5},{4,2},{5,3},{6,7},{7,6},{8,9},{9,8},{10,12... | collective-permute-start | bytes 983048 | tf_op jit(solution)/shard_map/ppermute | solution.py:615
  8.3 24.3 %collective-permute-start.19 = (f32[256,256]{1,0:T(8,128)S(1)}, f32[256,256]{1,0:T(8,128)S(1)}, u32[]{:S(2)}, u32[]{:S(2)}) collective-permute-start(f32[256,256]{1,0:T(8,128)S(1)} %get-tuple-element.47.refs_0_), channel_id=1, source_target_pairs={{0,4},{1,5},{2,0},{3,1},{4,6},{5,7},{6,2},{7,3},{8,12},{9,13},{10,... | collective-permute-start | bytes 786440 | tf_op jit(solution)/shard_map/ppermute | solution.py:615
  20.8 13.5 %collective-permute-start.3 = (f32[384,256]{1,0:T(8,128)S(1)}, f32[384,256]{1,0:T(8,128)S(1)}, u32[]{:S(2)}, u32[]{:S(2)}) collective-permute-start(f32[384,256]{1,0:T(8,128)S(1)} %get-tuple-element.34.refs_0_), channel_id=1, source_target_pairs={{0,1},{1,0},{2,3},{3,2},{4,5},{5,4},{6,7},{7,6},{8,9},{9,8},{10,11... | collective-permute-start | bytes 1179656 | tf_op jit(solution)/shard_map/ppermute | solution.py:47
  20.8 14.4 %collective-permute-start.4 = (f32[384,256]{1,0:T(8,128)S(1)}, f32[384,256]{1,0:T(8,128)S(1)}, u32[]{:S(2)}, u32[]{:S(2)}) collective-permute-start(f32[384,256]{1,0:T(8,128)S(1)} %collective-permute-done.refs_1_), channel_id=1, source_target_pairs={{0,1},{1,0},{2,3},{3,2},{4,5},{5,4},{6,7},{7,6},{8,9},{9,8},{10,11... | collective-permute-start | bytes 1179656 | tf_op jit(solution)/shard_map/ppermute | solution.py:47
  27.9 6.8 %collective-permute-start.5 = (f32[320,256]{1,0:T(8,128)S(1)}, f32[320,256]{1,0:T(8,128)S(1)}, u32[]{:S(2)}, u32[]{:S(2)}) collective-permute-start(f32[320,256]{1,0:T(8,128)S(1)} %collective-permute-done.1.refs_2_), channel_id=1, source_target_pairs={{0,1},{1,0},{2,3},{3,2},{4,5},{5,4},{6,7},{7,6},{8,9},{9,8},{10,11... | collective-permute-start | bytes 983048 | tf_op jit(solution)/shard_map/ppermute | solution.py:47
  27.9 7.0 %collective-permute-start.6 = (f32[320,256]{1,0:T(8,128)S(1)}, f32[320,256]{1,0:T(8,128)S(1)}, u32[]{:S(2)}, u32[]{:S(2)}) collective-permute-start(f32[320,256]{1,0:T(8,128)S(1)} %collective-permute-done.2.refs_3_), channel_id=1, source_target_pairs={{0,1},{1,0},{2,3},{3,2},{4,5},{5,4},{6,7},{7,6},{8,9},{9,8},{10,11... | collective-permute-start | bytes 983048 | tf_op jit(solution)/shard_map/ppermute | solution.py:47
  34.2 6.7 %collective-permute-start.21 = (f32[256,256]{1,0:T(8,128)S(1)}, f32[256,256]{1,0:T(8,128)S(1)}, u32[]{:S(2)}, u32[]{:S(2)}) collective-permute-start(f32[256,256]{1,0:T(8,128)S(1)} %get-tuple-element.47.refs_0_), channel_id=1, source_target_pairs={{0,1},{1,0},{2,3},{3,2},{4,5},{5,4},{6,7},{7,6},{8,9},{9,8},{10,11... | collective-permute-start | bytes 786440 | tf_op jit(solution)/shard_map/ppermute | solution.py:47
  34.3 6.5 %collective-permute-start.22 = (f32[256,256]{1,0:T(8,128)S(1)}, f32[256,256]{1,0:T(8,128)S(1)}, u32[]{:S(2)}, u32[]{:S(2)}) collective-permute-start(f32[256,256]{1,0:T(8,128)S(1)} %collective-permute-done.18.refs_1_), channel_id=1, source_target_pairs={{0,1},{1,0},{2,3},{3,2},{4,5},{5,4},{6,7},{7,6},{8,9},{9,8},{10,11... | collective-permute-start | bytes 786440 | tf_op jit(solution)/shard_map/ppermute | solution.py:47
  34.7 6.2 %collective-permute-start.23 = (f32[256,256]{1,0:T(8,128)S(1)}, f32[256,256]{1,0:T(8,128)S(1)}, u32[]{:S(2)}, u32[]{:S(2)}) collective-permute-start(f32[256,256]{1,0:T(8,128)S(1)} %collective-permute-done.19.refs_2_), channel_id=1, source_target_pairs={{0,1},{1,0},{2,3},{3,2},{4,5},{5,4},{6,7},{7,6},{8,9},{9,8},{10,11... | collective-permute-start | bytes 786440 | tf_op jit(solution)/shard_map/ppermute | solution.py:47
  34.8 6.0 %collective-permute-start.24 = (f32[256,256]{1,0:T(8,128)S(1)}, f32[256,256]{1,0:T(8,128)S(1)}, u32[]{:S(2)}, u32[]{:S(2)}) collective-permute-start(f32[256,256]{1,0:T(8,128)S(1)} %collective-permute-done.20.refs_3_), channel_id=1, source_target_pairs={{0,1},{1,0},{2,3},{3,2},{4,5},{5,4},{6,7},{7,6},{8,9},{9,8},{10,11... | collective-permute-start | bytes 786440 | tf_op jit(solution)/shard_map/ppermute | solution.py:47
  39.2 7.9 %collective-permute-start.17 = (f32[3,64,256]{2,1,0:T(8,128)S(1)}, f32[3,64,256]{2,1,0:T(8,128)S(1)}, u32[]{:S(2)}, u32[]{:S(2)}) collective-permute-start(f32[3,64,256]{2,1,0:T(8,128)S(1)} %get-tuple-element.39.refs_1_), channel_id=1, source_target_pairs={{0,8},{8,16},{16,24},{24,0},{1,9},{9,17},{17,25},{25,1},{2,10},{10... | collective-permute-start | bytes 589832 | tf_op jit(solution)/shard_map/ppermute | solution.py:669
  47.1 8.0 %collective-permute-start.29 = (f32[3,64,256]{2,1,0:T(8,128)S(1)}, f32[3,64,256]{2,1,0:T(8,128)S(1)}, u32[]{:S(2)}, u32[]{:S(2)}) collective-permute-start(f32[3,64,256]{2,1,0:T(8,128)S(1)} %get-tuple-element.49), channel_id=1, source_target_pairs={{0,24},{8,0},{16,8},{24,16},{1,25},{9,1},{17,9},{25,17},{2,26},{10... | collective-permute-start | bytes 589832 | tf_op jit(solution)/shard_map/ppermute | solution.py:664
  48.8 26.0 %collective-permute-start.8 = (f32[192,256]{1,0:T(8,128)S(1)}, f32[192,256]{1,0:T(8,128)S(1)}, u32[]{:S(2)}, u32[]{:S(2)}) collective-permute-start(f32[192,256]{1,0:T(8,128)S(1)} %bitcast.5), channel_id=1, source_target_pairs={{0,1},{1,0},{2,4},{3,5},{4,2},{5,3},{6,7},{7,6},{8,9},{9,8},{10,12... | collective-permute-start | bytes 589832 | tf_op jit(solution)/shard_map/ppermute | solution.py:615
  55.1 25.8 %collective-permute-start.34 = (f32[3,64,256]{2,1,0:T(8,128)S(1)}, f32[3,64,256]{2,1,0:T(8,128)S(1)}, u32[]{:S(2)}, u32[]{:S(2)}) collective-permute-start(f32[3,64,256]{2,1,0:T(8,128)S(1)} %get-tuple-element.52), channel_id=1, source_target_pairs={{0,24},{8,0},{16,8},{24,16},{1,25},{9,1},{17,9},{25,17},{2,26},{10... | collective-permute-start | bytes 589832 | tf_op jit(solution)/shard_map/ppermute | solution.py:664
  57.8 26.3 %collective-permute-start.7 = (f32[192,256]{1,0:T(8,128)S(1)}, f32[192,256]{1,0:T(8,128)S(1)}, u32[]{:S(2)}, u32[]{:S(2)}) collective-permute-start(f32[192,256]{1,0:T(8,128)S(1)} %bitcast.6), channel_id=1, source_target_pairs={{0,2},{1,3},{2,0},{3,1},{4,6},{5,7},{6,4},{7,5},{8,10},{9,11},{10,... | collective-permute-start | bytes 589832 | tf_op jit(solution)/shard_map/ppermute | solution.py:615
  74.9 13.3 %collective-permute-start.9 = (f32[192,256]{1,0:T(8,128)S(1)}, f32[192,256]{1,0:T(8,128)S(1)}, u32[]{:S(2)}, u32[]{:S(2)}) collective-permute-start(f32[192,256]{1,0:T(8,128)S(1)} %collective-permute-done.8.refs_2_), channel_id=1, source_target_pairs={{0,2},{1,3},{2,0},{3,1},{4,6},{5,7},{6,4},{7,5},{8,10},{9,11},{10,... | collective-permute-start | bytes 589832 | tf_op jit(solution)/shard_map/ppermute | solution.py:615
  80.9 9.8 %collective-permute-start.39 = (f32[3,64,256]{2,1,0:T(8,128)S(1)}, f32[3,64,256]{2,1,0:T(8,128)S(1)}, u32[]{:S(2)}, u32[]{:S(2)}) collective-permute-start(f32[3,64,256]{2,1,0:T(8,128)S(1)} %get-tuple-element.54), channel_id=1, source_target_pairs={{0,24},{8,0},{16,8},{24,16},{1,25},{9,1},{17,9},{25,17},{2,26},{10... | collective-permute-start | bytes 589832 | tf_op jit(solution)/shard_map/ppermute | solution.py:664
  83.6 15.4 %collective-permute-start.10 = (f32[192,256]{1,0:T(8,128)S(1)}, f32[192,256]{1,0:T(8,128)S(1)}, u32[]{:S(2)}, u32[]{:S(2)}) collective-permute-start(f32[192,256]{1,0:T(8,128)S(1)} %bitcast.7), channel_id=1, source_target_pairs={{0,1},{1,0},{2,3},{3,2},{4,5},{5,4},{6,7},{7,6},{8,9},{9,8},{10,11... | collective-permute-start | bytes 589832 | tf_op jit(solution)/shard_map/ppermute | solution.py:47
  83.6 15.4 %collective-permute-start.12 = (f32[192,256]{1,0:T(8,128)S(1)}, f32[192,256]{1,0:T(8,128)S(1)}, u32[]{:S(2)}, u32[]{:S(2)}) collective-permute-start(f32[192,256]{1,0:T(8,128)S(1)} %collective-permute-done.8.refs_2_), channel_id=1, source_target_pairs={{0,1},{1,0},{2,3},{3,2},{4,5},{5,4},{6,7},{7,6},{8,9},{9,8},{10,11... | collective-permute-start | bytes 589832 | tf_op jit(solution)/shard_map/ppermute | solution.py:47
  89.6 10.1 %collective-permute-start.11 = (f32[192,256]{1,0:T(8,128)S(1)}, f32[192,256]{1,0:T(8,128)S(1)}, u32[]{:S(2)}, u32[]{:S(2)}) collective-permute-start(f32[192,256]{1,0:T(8,128)S(1)} %collective-permute-done.7.refs_1_), channel_id=1, source_target_pairs={{0,1},{1,0},{2,3},{3,2},{4,5},{5,4},{6,7},{7,6},{8,9},{9,8},{10,11... | collective-permute-start | bytes 589832 | tf_op jit(solution)/shard_map/ppermute | solution.py:47
  90.6 9.1 %collective-permute-start.13 = (f32[192,256]{1,0:T(8,128)S(1)}, f32[192,256]{1,0:T(8,128)S(1)}, u32[]{:S(2)}, u32[]{:S(2)}) collective-permute-start(f32[192,256]{1,0:T(8,128)S(1)} %collective-permute-done.9.refs_3_), channel_id=1, source_target_pairs={{0,1},{1,0},{2,3},{3,2},{4,5},{5,4},{6,7},{7,6},{8,9},{9,8},{10,11... | collective-permute-start | bytes 589832 | tf_op jit(solution)/shard_map/ppermute | solution.py:47
  90.8 22.7 %collective-permute-start.40 = (f32[192,256]{1,0:T(8,128)S(1)}, f32[192,256]{1,0:T(8,128)S(1)}, u32[]{:S(2)}, u32[]{:S(2)}) collective-permute-start(f32[192,256]{1,0:T(8,128)S(1)} %shard_map.117.refs_8_), channel_id=1, source_target_pairs={{0,2},{1,3},{2,0},{3,1},{4,6},{5,7},{6,4},{7,5},{8,10},{9,11},{10,... | collective-permute-start | bytes 589832 | tf_op jit(solution)/shard_map/ppermute | solution.py:615
  98.9 14.6 %collective-permute-start.41 = (f32[192,256]{1,0:T(8,128)S(1)}, f32[192,256]{1,0:T(8,128)S(1)}, u32[]{:S(2)}, u32[]{:S(2)}) collective-permute-start(f32[192,256]{1,0:T(8,128)S(1)} %shard_map.117.refs_8_), channel_id=1, source_target_pairs={{0,1},{1,0},{2,4},{3,5},{4,2},{5,3},{6,7},{7,6},{8,9},{9,8},{10,12... | collective-permute-start | bytes 589832 | tf_op jit(solution)/shard_map/ppermute | solution.py:615
  99.0 15.0 %collective-permute-start.42 = (f32[192,256]{1,0:T(8,128)S(1)}, f32[192,256]{1,0:T(8,128)S(1)}, u32[]{:S(2)}, u32[]{:S(2)}) collective-permute-start(f32[192,256]{1,0:T(8,128)S(1)} %shard_map.117.refs_8_), channel_id=1, source_target_pairs={{0,2},{1,3},{2,6},{3,7},{4,0},{5,1},{6,4},{7,5},{8,10},{9,11},{10,... | collective-permute-start | bytes 589832 | tf_op jit(solution)/shard_map/ppermute | solution.py:615
  99.7 13.2 %collective-permute-start.47 = (f32[64,256]{1,0:T(8,128)S(1)}, f32[64,256]{1,0:T(8,128)S(1)}, u32[]{:S(2)}, u32[]{:S(2)}) collective-permute-start(f32[64,256]{1,0:T(8,128)S(1)} %get-tuple-element.56), channel_id=1, source_target_pairs={{0,2},{1,3},{2,0},{3,1},{4,6},{5,7},{6,4},{7,5},{8,10},{9,11},{10,... | collective-permute-start | bytes 196616 | tf_op jit(solution)/shard_map/ppermute | solution.py:615
  104.0 8.9 %collective-permute-start.49 = (f32[32,256]{1,0:T(8,128)S(1)}, f32[32,256]{1,0:T(8,128)S(1)}, u32[]{:S(2)}, u32[]{:S(2)}) collective-permute-start(f32[32,256]{1,0:T(8,128)S(1)} %get-tuple-element.58), channel_id=1, source_target_pairs={{0,2},{1,3},{2,6},{3,7},{4,0},{5,1},{6,4},{7,5},{8,10},{9,11},{10,... | collective-permute-start | bytes 98312 | tf_op jit(solution)/shard_map/ppermute | solution.py:615
  113.0 5.5 %collective-permute-start.43 = (f32[192,256]{1,0:T(8,128)S(1)}, f32[192,256]{1,0:T(8,128)S(1)}, u32[]{:S(2)}, u32[]{:S(2)}) collective-permute-start(f32[192,256]{1,0:T(8,128)S(1)} %shard_map.117.refs_8_), channel_id=1, source_target_pairs={{0,1},{1,0},{2,3},{3,2},{4,5},{5,4},{6,7},{7,6},{8,9},{9,8},{10,11... | collective-permute-start | bytes 589832 | tf_op jit(solution)/shard_map/ppermute | solution.py:47
  113.5 5.0 %collective-permute-start.44 = (f32[192,256]{1,0:T(8,128)S(1)}, f32[192,256]{1,0:T(8,128)S(1)}, u32[]{:S(2)}, u32[]{:S(2)}) collective-permute-start(f32[192,256]{1,0:T(8,128)S(1)} %collective-permute-done.40.refs_9_), channel_id=1, source_target_pairs={{0,1},{1,0},{2,3},{3,2},{4,5},{5,4},{6,7},{7,6},{8,9},{9,8},{10,11... | collective-permute-start | bytes 589832 | tf_op jit(solution)/shard_map/ppermute | solution.py:47
  113.5 4.9 %collective-permute-start.45 = (f32[192,256]{1,0:T(8,128)S(1)}, f32[192,256]{1,0:T(8,128)S(1)}, u32[]{:S(2)}, u32[]{:S(2)}) collective-permute-start(f32[192,256]{1,0:T(8,128)S(1)} %collective-permute-done.41.refs_10_), channel_id=1, source_target_pairs={{0,1},{1,0},{2,3},{3,2},{4,5},{5,4},{6,7},{7,6},{8,9},{9,8},{10,11... | collective-permute-start | bytes 589832 | tf_op jit(solution)/shard_map/ppermute | solution.py:47
  (27 other events, 152.6 us)

commit v6 on v5

--- a/solution.py
+++ b/solution.py
@@ -233,13 +233,13 @@
     return product(left, right, 1)
 
 
-def kernel_call(body, outs, *operands, scratch=(), raw=False, spill=False, limit=24 * 1024 * 1024):
+def kernel_call(body, outs, *operands, scratch=(), raw=False, spill=0, limit=24 * 1024 * 1024):
     space = pltpu.MemorySpace.HBM if raw else pltpu.VMEM
     return pl.pallas_call(
         body,
         in_specs=[pl.BlockSpec(memory_space=space) for _ in operands],
         out_specs=[pl.BlockSpec(memory_space=pltpu.VMEM) for _ in outs],
-        out_shape=[(jax.ShapeDtypeStruct if spill else pltpu.VMEM)(shape, dtype) for shape, dtype in outs],
+        out_shape=[(jax.ShapeDtypeStruct if i < spill else pltpu.VMEM)(*out) for i, out in enumerate(outs)],
         scratch_shapes=list(scratch),
         compiler_params=pltpu.CompilerParams(vmem_limit_bytes=limit),
     )(*operands)
@@ -341,14 +341,14 @@
 
 def forward_body(*refs):
     packs, mates = refs[:CHIPS], refs[CHIPS : 2 * CHIPS]
-    own, last, key_high, key_low, scaled_high, scaled_low, kept, shifted, sums, table = refs[2 * CHIPS :]
+    own, last, key_high, key_low, scaled_high, scaled_low, kept, shifted, lead, sums, table = refs[2 * CHIPS :]
     pieces = packs + mates
     depth = key_high.shape[0] // len(pieces)
     span = own.shape[1]
 
     @pl.when(~in_chain())
     def _():
-        for out in (own, shifted, sums):
+        for out in (own, shifted, lead, sums):
             out[...] = jnp.zeros(out.shape, jnp.float32)
 
     @pl.when(in_chain())
@@ -381,6 +381,8 @@
         sums[...] = jnp.concatenate(rows + [jnp.zeros((2, own.shape[2]), jnp.float32)])
         for m in range(3):
             shifted[m] = moved[m]
+        for m in range(2):
+            lead[m] = moved[m]
 
 
 def apply_body(source, own, raw, earlier, *refs):
@@ -527,13 +529,16 @@
 
     @pl.when(in_chain())
     def _():
-        _, rows = section_rows(count, refs)
+        cots, rows = section_rows(count, refs)
         rows = [row + applied[m * span : (m + 1) * span, :] for m, row in enumerate(rows)]
         table[...] = jnp.concatenate(rows[:2]).T
-        for by, out in enumerate(outs):
+        for m in range(3):
+            outs[2][m * span : (m + 1) * span, :] = cots[m]
+        for by, (out, place) in enumerate(zip(outs, (0, 0, 3 * span, 0))):
             start = jnp.bitwise_xor(chip, by) * 2 * depth
             for core in range(2):
-                out[:depth, core * 128 : (core + 1) * 128] = table[rows_at(start + core * depth, depth), :]
+                lanes = slice(core * 128, (core + 1) * 128)
+                out[place : place + depth, lanes] = table[rows_at(start + core * depth, depth), :]
         low = chip == LOW
         upper, lower = rows[2][:depth], rows[2][depth:]
         outs[0][depth:] = jnp.where(low, lower, upper)
@@ -552,34 +557,39 @@
     return halves(jnp.concatenate([taken(pair, slice(part * span, (part + 1) * span)) for pair in pieces]))
 
 
-def query_body(queries, out_cot, *refs):
-    pieces, d_queries = joined(refs[:8]), refs[8]
+def query_body(queries, out_cot, keys, values, rates, *refs):
+    pieces = joined(refs[:8])
+    d_queries, kept, high, low, key_high, key_low, scaled_high, scaled_low = refs[8:]
     span = queries.shape[1] // len(pieces)
-    one, three, two = [load_halves(pieces, part, span) for part in range(3)]
+    weights = [load_halves(pieces, part, span) for part in range(3)]
+    for part in range(3):
+        high[part], low[part] = weights[part]
+    one, three, two = weights
     query, cot = halves(queries[...]), halves(out_cot[...])
     first, gate = nt(query, one), nt(query, three)
     value, d_one, _ = silu_parts(first)
     d_mixed = nt(cot, two)
-    d_gate = d_mixed * value
-    d_first = d_mixed * gate * d_one
-    d_queries[...] = nn(halves(d_first), one) + nn(halves(d_gate), three)
-
-
-def token_body(keys, values, rates, *refs):
-    weights, cots = joined(refs[:8]), joined(refs[8:16])
-    ends = joined(refs[16:24])
-    d_keys, d_values, d_rates, d_rows = refs[24:]
-    width = keys.shape[1]
-    span = width // len(weights)
-    one, three, two = [load_halves(weights, part, span) for part in range(3)]
-    c_one, c_three, c_two = [load_halves(cots, part, span) for part in range(3)]
-    rate = column(rates[...], width)
-    key, scaled = halves(keys[...]), halves(-rate * values[...])
+    d_queries[...] = nn(halves(d_mixed * gate * d_one), one) + nn(halves(d_mixed * value), three)
+    key, scaled = halves(keys[...]), halves(-column(rates[...], keys.shape[1]) * values[...])
+    key_high[...], key_low[...] = key
+    scaled_high[...], scaled_low[...] = scaled
     first, gate = nt(key, one), nt(key, three)
     value, d_one, d_two = silu_parts(first)
-    d_mixed = nt(scaled, two)
+    for place, array in enumerate((gate, value, d_one, d_two, nt(scaled, two))):
+        kept[place] = array
+
+
+def token_body(values, rates, kept, high, low, key_high, key_low, scaled_high, scaled_low, *refs):
+    cots = [[refs[i], refs[i + 1]] for i in (0, 2, 7, 9)]
+    ends = [refs[4:7], refs[11:14]]
+    d_keys, d_values, d_rates, d_rows = refs[14:]
+    width = values.shape[1]
+    span = width // len(cots)
+    one, three, two = [(high[part], low[part]) for part in range(3)]
+    c_one, c_three, c_two = [load_halves(cots, part, span) for part in range(3)]
+    key, scaled = (key_high[...], key_low[...]), (scaled_high[...], scaled_low[...])
+    gate, value, d_one, d_two, d_mixed = [kept[place] for place in range(5)]
     t_first, t_gate, p_mixed = nt(key, c_one), nt(key, c_three), nt(scaled, c_two)
-    mixed = value * gate
     d_gate = d_mixed * value
     d_first = d_mixed * gate * d_one
     lift = d_one * t_first
@@ -587,15 +597,14 @@
     c_gate = p_mixed * value + d_mixed * lift
     c_first = p_mixed * gate * d_one + d_mixed * (d_two * t_first * gate + d_one * t_gate)
     d_keys[...] = nn(halves(c_first), one) + nn(halves(c_gate), three) + nn(halves(d_first), c_one) + nn(halves(d_gate), c_three)
-    t_out = nn(halves(t_mixed), two) + nn(halves(mixed), c_two)
-    d_values[...] = -rate * t_out
+    t_out = nn(halves(t_mixed), two) + nn(halves(value * gate), c_two)
+    d_values[...] = -column(rates[...], width) * t_out
     d_rates[...] = -jnp.sum((values[...] * t_out).T, axis=0, keepdims=True)
     depth = d_rows.shape[1]
     low_side, upper_core = my_chip() <= LOW, my_core() == 0
-    block = slice(0, depth)
     sides = []
-    for near, far in (ends[:2], ends[2:]):
-        near, far = taken(near, block), taken(far, block)
+    for (own, beside, across), (_, far) in zip(ends, cots[1::2]):
+        near, far = own[:depth] + beside[:depth], across[...] + far[3 * span :]
         near, far = [jnp.where(upper_core, piece[:, :128], piece[:, 128:]) for piece in (near, far)]
         sides.append([jnp.where(low_side, near, far), jnp.where(low_side, far, near)])
     by_core = [[jnp.where(upper_core, a, b) for a, b in zip(*sides)], [jnp.where(upper_core, b, a) for a, b in zip(*sides)]]
@@ -607,7 +616,7 @@
                     start = (2 * m + i) * depth
                     parts.append(by_core[core][side][:, start : start + depth])
         d_rows[m] = jnp.concatenate(parts, axis=1)
-    d_rows[2] = taken(ends[0], slice(depth, None))
+    d_rows[2] = ends[0][0][depth:] + ends[0][1][depth:]
 
 
 def over_chips(array, moves):
@@ -645,11 +654,6 @@
 
 def to_chain(arrays):
     return both_cores([arrays[0], *hops(arrays, INWARD)])
-
-
-def from_chain(arrays):
-    near, far, across = hops(arrays, OUTWARD)
-    return both_cores([arrays[0], near, across, far])
 
 
 def from_chain_relayed(array):
@@ -692,14 +696,14 @@
     pieces = to_chain(packs)
     ahead_pieces = to_chain([ahead] * CHIPS)
     half = bf16(tokens, width)
-    own, last, *halved, kept, shifted, sums = kernel_call(
+    own, last, *halved, kept, shifted, lead, sums = kernel_call(
         forward_body,
-        [state, state, half, half, half, half, f32(5, span, tokens), state, f32(8, width)],
+        [state, state, half, half, half, half, f32(5, span, tokens), state, f32(2, span, width), f32(8, width)],
         *pieces,
         scratch=[pltpu.VMEM((width, 4 * span), jnp.float32)],
     )
     all_sums = exchanged(sums)
-    earlier = to_later(shifted)
+    earlier = to_later(lead)
     weights = from_chain_relayed(own.reshape(3 * span, width))
 
     inners, arrived = [], []
@@ -721,28 +725,39 @@
         inners += exchanged(straight)
     received = [*common, *inners, *arrived]
     (cot,) = kernel_call(functools.partial(terms_body, groups - 1), [wide], *received)
-    cots = from_chain([cot] * CHIPS)
-    ends = kernel_call(
+    near = by_xor(cot, 1)
+    across = over_chips(cot, ACROSS)
+    own_end, near_end, far, across_end = kernel_call(
         functools.partial(final_body, groups - 1),
-        [f32(2 * rows, width)] * 2 + [f32(rows, width)] * 2,
+        [f32(2 * rows, width)] * 2 + [f32(3 * span + rows, width), f32(rows, width)],
         *received,
         *halved,
         kept,
         applied,
         scratch=[pltpu.VMEM((width, 128), jnp.float32)],
     )
-    end_pieces = from_chain(ends)
-    (d_queries,) = kernel_call(query_body, [square], queries, out_cot, *weights, spill=True)
-    d_keys, d_values, d_rates, d_rows = kernel_call(
-        token_body,
-        [square, square, f32(1, depth), f32(3, rows, width)],
+    near_end = by_xor(near_end, 1)
+    across_end = over_chips(across_end, ACROSS)
+    far = over_chips(far, OUTWARD)
+    cots = [cot, near, across, far, own_end, near_end, across_end]
+    swapped = []
+    for piece in cots:
+        swapped.append(core_swap(piece))
+    cots = cots + swapped
+    small, whole = bf16(depth, width), bf16(3, width, width)
+    d_queries, *saved = kernel_call(
+        query_body,
+        [square, f32(5, depth, width), whole, whole, small, small, small, small],
+        queries,
+        out_cot,
         keys,
         values,
         rates_row,
         *weights,
-        *cots,
-        *end_pieces,
-        spill=True,
+        spill=1,
+    )
+    d_keys, d_values, d_rates, d_rows = kernel_call(
+        token_body, [square, square, f32(1, depth), f32(3, rows, width)], values, rates_row, *saved, *cots, spill=4
     )
     return (d_queries, d_keys, d_values, d_rates.reshape(depth), d_rows[None])
 

time: 121 us -> 116 us (0.959)
  starting transfers between devices: 64.4 us -> 54.3 us
  waiting for transfers between devices: 50.2 us -> 55.5 us
    ppermute x19 -> x18, starting transfers between devices: 45.3 us -> 35.9 us  [over_chips(): return lax.ppermute(array, 'tok', pairs)]
    ppermute x19 -> x18, waiting for transfers between devices: 28.5 us -> 34.4 us  [over_chips(): return lax.ppermute(array, 'tok', pairs)]
    ppermute x1, waiting for transfers between devices: 6.19 us -> 4.79 us  [to_later(): lax.ppermute(array, 'block', [(i, (i + 1) % groups) for i in range(groups)])]
    ppermute x24 -> x23, starting transfers between devices: 5.55 us -> 4.34 us  [core_swap(): return lax.ppermute(array, 'tok', [(j, j ^ 1) for j in range(size)])]
    ppermute x24 -> x23, waiting for transfers between devices: 5.15 us -> 5.04 us  [core_swap(): return lax.ppermute(array, 'tok', [(j, j ^ 1) for j in range(size)])]
  transfers between devices with their start and end apart: 54 -> 52, of which waited for: 22 -> 25; matrix products, arithmetic and copies ran while one was open for 0% -> 0% of each run, Pallas kernels for 1% -> 1%
where the time goes in v6:
time: 116 us
  waiting for transfers between devices  55.5 us (48%)
  starting transfers between devices  54.3 us (47%)
  Pallas kernels  4.88 us (4%)
    ppermute x18, starting transfers between devices, over_chips(): return lax.ppermute(array, 'tok', pairs)  35.9 us
    ppermute x18, waiting for transfers between devices, over_chips(): return lax.ppermute(array, 'tok', pairs)  34.4 us
    ppermute x6, starting transfers between devices, to_earlier(): lax.ppermute(array, 'block', [(i, (i - 1) % groups) for i in range(groups)])  10.8 us
    ppermute x6, waiting for transfers between devices, to_earlier(): lax.ppermute(array, 'block', [(i, (i - 1) % groups) for i in range(groups)])  9.95 us
    ppermute x23, waiting for transfers between devices, core_swap(): return lax.ppermute(array, 'tok', [(j, j ^ 1) for j in range(size)])  5.04 us
    pallas_call x10, Pallas kernels, kernel_call(): pl.pallas_call(body, in_specs=[pl.BlockSpec(memory_space=space) for _ in...  4.88 us
    ppermute x1, waiting for transfers between devices, to_later(): lax.ppermute(array, 'block', [(i, (i + 1) % groups) for i in range(groups)])  4.79 us
    ppermute x23, starting transfers between devices, core_swap(): return lax.ppermute(array, 'tok', [(j, j ^ 1) for j in range(size)])  4.34 us
  transfers between devices with their start and end apart: 52, of which 25 were waited for; matrix products, arithmetic and copies ran while one was open for 0% of the time, Pallas kernels for 1%

profile of v6, /device:TPU:0, one launch (start us, length us, event | category | flops | bytes accessed | tf_op | source)
XLA Modules:
  0.0 115.6 jit_solution(5620635900815712992)
XLA Ops:
  0.6 1.5 %shard_map.110 = (f32[384,256]{1,0:T(8,128)S(1)}, f32[384,256]{1,0:T(8,128)S(1)}, f32[320,256]{1,0:T(8,128)S(1)}, f32[320,256]{1,0:T(8,128)S(1)}, f32[256,256]{1,0:T(8,128)S(1)}) custom-call(f32[128,256]{1,0:T(8,128)} %keys.1, f32[128,256]{1,0:T(8,128)} %values.3, f32[1,128]{1,0:T(1,128)} %bitcast.9, f32[3,32,256]{2,1,0:T(8,128)} %bitcast.12, ...), custom_call_target="tpu_custom_call" | custom-call | tf_op jit(solution)/shard_map/pallas_call | solution.py:238
  2.1 3.1 %collective-permute-start = (f32[384,256]{1,0:T(8,128)S(1)}, f32[384,256]{1,0:T(8,128)S(1)}, u32[]{:S(2)}, u32[]{:S(2)}) collective-permute-start(f32[384,256]{1,0:T(8,128)S(1)} %get-tuple-element.44), channel_id=1, source_target_pairs={{0,2},{1,3},{2,0},{3,1},{4,6},{5,7},{6,4},{7,5},{8,10},{9,11},{10,... | collective-permute-start | bytes 1179656 | tf_op jit(solution)/shard_map/ppermute | solution.py:624
  5.3 3.0 %collective-permute-start.1 = (f32[320,256]{1,0:T(8,128)S(1)}, f32[320,256]{1,0:T(8,128)S(1)}, u32[]{:S(2)}, u32[]{:S(2)}) collective-permute-start(f32[320,256]{1,0:T(8,128)S(1)} %get-tuple-element.45), channel_id=1, source_target_pairs={{0,4},{1,5},{2,0},{3,1},{4,6},{5,7},{6,2},{7,3},{8,12},{9,13},{10,... | collective-permute-start | bytes 983048 | tf_op jit(solution)/shard_map/ppermute | solution.py:624
  8.3 1.6 %collective-permute-start.19 = (f32[256,256]{1,0:T(8,128)S(1)}, f32[256,256]{1,0:T(8,128)S(1)}, u32[]{:S(2)}, u32[]{:S(2)}) collective-permute-start(f32[256,256]{1,0:T(8,128)S(1)} %get-tuple-element.65.refs_0_), channel_id=1, source_target_pairs={{0,4},{1,5},{2,0},{3,1},{4,6},{5,7},{6,2},{7,3},{8,12},{9,13},{10,... | collective-permute-start | bytes 786440 | tf_op jit(solution)/shard_map/ppermute | solution.py:624
  9.9 11.0 %collective-permute-done.18.refs_1_ = f32[256,256]{1,0:T(8,128)S(1)} collective-permute-done((f32[256,256]{1,0:T(8,128)S(1)}, f32[256,256]{1,0:T(8,128)S(1)}, u32[]{:S(2)}, u32[]{:S(2)}) %collective-permute-start.18) | collective-permute-done | bytes 262176 | tf_op jit(solution)/shard_map/ppermute | solution.py:624
  20.8 7.0 %collective-permute-done.1.refs_2_ = f32[320,256]{1,0:T(8,128)S(1)} collective-permute-done((f32[320,256]{1,0:T(8,128)S(1)}, f32[320,256]{1,0:T(8,128)S(1)}, u32[]{:S(2)}, u32[]{:S(2)}) %collective-permute-start.1) | collective-permute-done | bytes 327712 | tf_op jit(solution)/shard_map/ppermute | solution.py:624
  28.4 4.2 %collective-permute-done.19.refs_2_ = f32[256,256]{1,0:T(8,128)S(1)} collective-permute-done((f32[256,256]{1,0:T(8,128)S(1)}, f32[256,256]{1,0:T(8,128)S(1)}, u32[]{:S(2)}, u32[]{:S(2)}) %collective-permute-start.19) | collective-permute-done | bytes 262176 | tf_op jit(solution)/shard_map/ppermute | solution.py:624
  32.6 1.5 %collective-permute-done.20.refs_3_ = f32[256,256]{1,0:T(8,128)S(1)} collective-permute-done((f32[256,256]{1,0:T(8,128)S(1)}, f32[256,256]{1,0:T(8,128)S(1)}, u32[]{:S(2)}, u32[]{:S(2)}) %collective-permute-start.20) | collective-permute-done | bytes 262176 | tf_op jit(solution)/shard_map/ppermute | solution.py:624
  35.4 1.4 %collective-permute-done.14.refs_4_ = f32[8,256]{1,0:T(8,128)S(1)} collective-permute-done((f32[8,256]{1,0:T(8,128)S(1)}, f32[8,256]{1,0:T(8,128)S(1)}, u32[]{:S(2)}, u32[]{:S(2)}) %collective-permute-start.14) | collective-permute-done | bytes 8224 | tf_op jit(solution)/shard_map/ppermute | solution.py:624
  37.0 1.0 collective-permute-done.15.refs_5_
  38.2 1.0 collective-permute-done.16.refs_6_
  39.2 1.7 %collective-permute-start.17 = (f32[2,64,256]{2,1,0:T(8,128)S(1)}, f32[2,64,256]{2,1,0:T(8,128)S(1)}, u32[]{:S(2)}, u32[]{:S(2)}) collective-permute-start(f32[2,64,256]{2,1,0:T(8,128)S(1)} %get-tuple-element.64), channel_id=1, source_target_pairs={{0,8},{8,16},{16,24},{24,0},{1,9},{9,17},{17,25},{25,1},{2,10},{10... | collective-permute-start | bytes 393224 | tf_op jit(solution)/shard_map/ppermute | solution.py:673
  40.9 4.8 %collective-permute-done.17.earlier.refs_18_ = f32[2,64,256]{2,1,0:T(8,128)S(1)} collective-permute-done((f32[2,64,256]{2,1,0:T(8,128)S(1)}, f32[2,64,256]{2,1,0:T(8,128)S(1)}, u32[]{:S(2)}, u32[]{:S(2)}) %collective-permute-start.17) | collective-permute-done | bytes 131104 | tf_op jit(solution)/shard_map/ppermute | solution.py:673
  45.7 1.8 %collective-permute-start.29 = (f32[3,64,256]{2,1,0:T(8,128)S(1)}, f32[3,64,256]{2,1,0:T(8,128)S(1)}, u32[]{:S(2)}, u32[]{:S(2)}) collective-permute-start(f32[3,64,256]{2,1,0:T(8,128)S(1)} %get-tuple-element.67), channel_id=1, source_target_pairs={{0,24},{8,0},{16,8},{24,16},{1,25},{9,1},{17,9},{25,17},{2,26},{10... | collective-permute-start | bytes 589832 | tf_op jit(solution)/shard_map/ppermute | solution.py:668
  47.4 1.4 %collective-permute-start.25 = (f32[8,256]{1,0:T(8,128)S(1)}, f32[8,256]{1,0:T(8,128)S(1)}, u32[]{:S(2)}, u32[]{:S(2)}) collective-permute-start(f32[8,256]{1,0:T(8,128)S(1)} %get-tuple-element.66), channel_id=1, source_target_pairs={{0,24},{8,0},{16,8},{24,16},{1,25},{9,1},{17,9},{25,17},{2,26},{10... | collective-permute-start | bytes 24584 | tf_op jit(solution)/shard_map/ppermute | solution.py:668
  48.9 3.1 %collective-permute-done.25.refs_7_ = f32[8,256]{1,0:T(8,128)S(1)} collective-permute-done((f32[8,256]{1,0:T(8,128)S(1)}, f32[8,256]{1,0:T(8,128)S(1)}, u32[]{:S(2)}, u32[]{:S(2)}) %collective-permute-start.25) | collective-permute-done | bytes 8224 | tf_op jit(solution)/shard_map/ppermute | solution.py:668
  53.7 2.7 %collective-permute-start.34 = (f32[3,64,256]{2,1,0:T(8,128)S(1)}, f32[3,64,256]{2,1,0:T(8,128)S(1)}, u32[]{:S(2)}, u32[]{:S(2)}) collective-permute-start(f32[3,64,256]{2,1,0:T(8,128)S(1)} %get-tuple-element.70), channel_id=1, source_target_pairs={{0,24},{8,0},{16,8},{24,16},{1,25},{9,1},{17,9},{25,17},{2,26},{10... | collective-permute-start | bytes 589832 | tf_op jit(solution)/shard_map/ppermute | solution.py:668
  56.9 4.1 %collective-permute-done.30.refs_7_.refs_11_ = f32[8,256]{1,0:T(8,128)S(1)} collective-permute-done((f32[8,256]{1,0:T(8,128)S(1)}, f32[8,256]{1,0:T(8,128)S(1)}, u32[]{:S(2)}, u32[]{:S(2)}) %collective-permute-start.30) | collective-permute-done | bytes 8224 | tf_op jit(solution)/shard_map/ppermute | solution.py:668
  62.8 3.4 %collective-permute-start.39 = (f32[3,64,256]{2,1,0:T(8,128)S(1)}, f32[3,64,256]{2,1,0:T(8,128)S(1)}, u32[]{:S(2)}, u32[]{:S(2)}) collective-permute-start(f32[3,64,256]{2,1,0:T(8,128)S(1)} %get-tuple-element.72), channel_id=1, source_target_pairs={{0,24},{8,0},{16,8},{24,16},{1,25},{9,1},{17,9},{25,17},{2,26},{10... | collective-permute-start | bytes 589832 | tf_op jit(solution)/shard_map/ppermute | solution.py:668
  66.2 18.8 %collective-permute-start.7 = (f32[192,256]{1,0:T(8,128)S(1)}, f32[192,256]{1,0:T(8,128)S(1)}, u32[]{:S(2)}, u32[]{:S(2)}) collective-permute-start(f32[192,256]{1,0:T(8,128)S(1)} %bitcast.6), channel_id=1, source_target_pairs={{0,2},{1,3},{2,0},{3,1},{4,6},{5,7},{6,4},{7,5},{8,10},{9,11},{10,... | collective-permute-start | bytes 589832 | tf_op jit(solution)/shard_map/ppermute | solution.py:624
  85.0 1.0 collective-permute-start.35
  86.0 2.7 %collective-permute-done.35.refs_15_ = f32[8,256]{1,0:T(8,128)S(1)} collective-permute-done((f32[8,256]{1,0:T(8,128)S(1)}, f32[8,256]{1,0:T(8,128)S(1)}, u32[]{:S(2)}, u32[]{:S(2)}) %collective-permute-start.35) | collective-permute-done | bytes 8224 | tf_op jit(solution)/shard_map/ppermute | solution.py:668
  89.2 0.7 collective-permute-done.36.refs_16_
  91.3 6.2 %collective-permute-start.42 = (f32[224,256]{1,0:T(8,128)S(1)}, f32[224,256]{1,0:T(8,128)S(1)}, u32[]{:S(2)}, u32[]{:S(2)}) collective-permute-start(f32[224,256]{1,0:T(8,128)S(1)} %get-tuple-element.73), channel_id=1, source_target_pairs={{0,2},{1,3},{2,6},{3,7},{4,0},{5,1},{6,4},{7,5},{8,10},{9,11},{10,... | collective-permute-start | bytes 688136 | tf_op jit(solution)/shard_map/ppermute | solution.py:624
  98.9 2.6 %collective-permute-start.43 = (f32[64,256]{1,0:T(8,128)S(1)}, f32[64,256]{1,0:T(8,128)S(1)}, u32[]{:S(2)}, u32[]{:S(2)}) collective-permute-start(f32[64,256]{1,0:T(8,128)S(1)} %get-tuple-element.75), channel_id=1, source_target_pairs={{0,2},{1,3},{2,0},{3,1},{4,6},{5,7},{6,4},{7,5},{8,10},{9,11},{10,... | collective-permute-start | bytes 196616 | tf_op jit(solution)/shard_map/ppermute | solution.py:624
  101.5 3.1 %collective-permute-done.42.refs_3_ = f32[224,256]{1,0:T(8,128)S(1)} collective-permute-done((f32[224,256]{1,0:T(8,128)S(1)}, f32[224,256]{1,0:T(8,128)S(1)}, u32[]{:S(2)}, u32[]{:S(2)}) %collective-permute-start.42) | collective-permute-done | bytes 229408 | tf_op jit(solution)/shard_map/ppermute | solution.py:624
  105.1 3.4 %collective-permute-done.40.refs_1_ = f32[192,256]{1,0:T(8,128)S(1)} collective-permute-done((f32[192,256]{1,0:T(8,128)S(1)}, f32[192,256]{1,0:T(8,128)S(1)}, u32[]{:S(2)}, u32[]{:S(2)}) %collective-permute-start.40) | collective-permute-done | bytes 196640 | tf_op jit(solution)/shard_map/ppermute | solution.py:624
  109.0 0.8 collective-permute-done.43.refs_5_
  109.9 1.2 %collective-permute-done.51.refs_13_ = f32[32,256]{1,0:T(8,128)S(1)} collective-permute-done((f32[32,256]{1,0:T(8,128)S(1)}, f32[32,256]{1,0:T(8,128)S(1)}, u32[]{:S(2)}, u32[]{:S(2)}) %collective-permute-start.51) | collective-permute-done | bytes 32800 | tf_op jit(solution)/shard_map/ppermute | solution.py:47
  111.2 1.1 collective-permute-done.49.refs_11_
  112.5 1.4 %shard_map.112 = (f32[128,256]{1,0:T(8,128)}, f32[5,128,256]{2,1,0:T(8,128)S(1)}, bf16[3,256,256]{2,1,0:T(8,128)(2,1)S(1)}, bf16[3,256,256]{2,1,0:T(8,128)(2,1)S...) custom-call(f32[128,256]{1,0:T(8,128)S(1)} %copy-done.1, ...), custom_call_target="tpu_custom_call" | custom-call | tf_op jit(solution)/shard_map/pallas_call | solution.py:238
  113.9 1.7 %shard_map.119 = (f32[128,256]{1,0:T(8,128)}, f32[128,256]{1,0:T(8,128)}, f32[1,128]{1,0:T(1,128)}, f32[3,32,256]{2,1,0:T(8,128)}) custom-call(f32[128,256]{1,0:T(8,128)S(1)} %copy-done, f32[1,128]{1,0:T(1,128)S(1)} %bitcast.11, f32[5,128,256]{2,1,0:T(8,128)S(1)} %get-tuple-element.49.kept, bf16[3,256,256]{2,1,0:T(8,128)(2,1)S(1)} %get-tuple-element.50.high, ...), custom_call_target="tpu_custom_call" | custom-call | tf_op jit(solution)/shard_map/pallas_call | solution.py:238
  (92 shorter events, 11.0 us)
Async XLA Ops:
  2.1 26.2 %collective-permute-start = (f32[384,256]{1,0:T(8,128)S(1)}, f32[384,256]{1,0:T(8,128)S(1)}, u32[]{:S(2)}, u32[]{:S(2)}) collective-permute-start(f32[384,256]{1,0:T(8,128)S(1)} %get-tuple-element.44), channel_id=1, source_target_pairs={{0,2},{1,3},{2,0},{3,1},{4,6},{5,7},{6,4},{7,5},{8,10},{9,11},{10,... | collective-permute-start | bytes 1179656 | tf_op jit(solution)/shard_map/ppermute | solution.py:624
  5.3 15.6 %collective-permute-start.18 = (f32[256,256]{1,0:T(8,128)S(1)}, f32[256,256]{1,0:T(8,128)S(1)}, u32[]{:S(2)}, u32[]{:S(2)}) collective-permute-start(f32[256,256]{1,0:T(8,128)S(1)} %get-tuple-element.65.refs_0_), channel_id=1, source_target_pairs={{0,2},{1,3},{2,0},{3,1},{4,6},{5,7},{6,4},{7,5},{8,10},{9,11},{10,... | collective-permute-start | bytes 786440 | tf_op jit(solution)/shard_map/ppermute | solution.py:624
  5.3 22.5 %collective-permute-start.1 = (f32[320,256]{1,0:T(8,128)S(1)}, f32[320,256]{1,0:T(8,128)S(1)}, u32[]{:S(2)}, u32[]{:S(2)}) collective-permute-start(f32[320,256]{1,0:T(8,128)S(1)} %get-tuple-element.45), channel_id=1, source_target_pairs={{0,4},{1,5},{2,0},{3,1},{4,6},{5,7},{6,2},{7,3},{8,12},{9,13},{10,... | collective-permute-start | bytes 983048 | tf_op jit(solution)/shard_map/ppermute | solution.py:624
  8.3 19.6 %collective-permute-start.2 = (f32[320,256]{1,0:T(8,128)S(1)}, f32[320,256]{1,0:T(8,128)S(1)}, u32[]{:S(2)}, u32[]{:S(2)}) collective-permute-start(f32[320,256]{1,0:T(8,128)S(1)} %get-tuple-element.46), channel_id=1, source_target_pairs={{0,1},{1,0},{2,4},{3,5},{4,2},{5,3},{6,7},{7,6},{8,9},{9,8},{10,12... | collective-permute-start | bytes 983048 | tf_op jit(solution)/shard_map/ppermute | solution.py:624
  8.3 24.3 %collective-permute-start.19 = (f32[256,256]{1,0:T(8,128)S(1)}, f32[256,256]{1,0:T(8,128)S(1)}, u32[]{:S(2)}, u32[]{:S(2)}) collective-permute-start(f32[256,256]{1,0:T(8,128)S(1)} %get-tuple-element.65.refs_0_), channel_id=1, source_target_pairs={{0,4},{1,5},{2,0},{3,1},{4,6},{5,7},{6,2},{7,3},{8,12},{9,13},{10,... | collective-permute-start | bytes 786440 | tf_op jit(solution)/shard_map/ppermute | solution.py:624
  20.8 13.5 %collective-permute-start.3 = (f32[384,256]{1,0:T(8,128)S(1)}, f32[384,256]{1,0:T(8,128)S(1)}, u32[]{:S(2)}, u32[]{:S(2)}) collective-permute-start(f32[384,256]{1,0:T(8,128)S(1)} %get-tuple-element.43.refs_0_), channel_id=1, source_target_pairs={{0,1},{1,0},{2,3},{3,2},{4,5},{5,4},{6,7},{7,6},{8,9},{9,8},{10,11... | collective-permute-start | bytes 1179656 | tf_op jit(solution)/shard_map/ppermute | solution.py:47
  27.9 6.8 %collective-permute-start.5 = (f32[320,256]{1,0:T(8,128)S(1)}, f32[320,256]{1,0:T(8,128)S(1)}, u32[]{:S(2)}, u32[]{:S(2)}) collective-permute-start(f32[320,256]{1,0:T(8,128)S(1)} %collective-permute-done.1.refs_2_), channel_id=1, source_target_pairs={{0,1},{1,0},{2,3},{3,2},{4,5},{5,4},{6,7},{7,6},{8,9},{9,8},{10,11... | collective-permute-start | bytes 983048 | tf_op jit(solution)/shard_map/ppermute | solution.py:47
  27.9 7.0 %collective-permute-start.6 = (f32[320,256]{1,0:T(8,128)S(1)}, f32[320,256]{1,0:T(8,128)S(1)}, u32[]{:S(2)}, u32[]{:S(2)}) collective-permute-start(f32[320,256]{1,0:T(8,128)S(1)} %collective-permute-done.2.refs_3_), channel_id=1, source_target_pairs={{0,1},{1,0},{2,3},{3,2},{4,5},{5,4},{6,7},{7,6},{8,9},{9,8},{10,11... | collective-permute-start | bytes 983048 | tf_op jit(solution)/shard_map/ppermute | solution.py:47
  28.4 6.8 %collective-permute-start.4 = (f32[384,256]{1,0:T(8,128)S(1)}, f32[384,256]{1,0:T(8,128)S(1)}, u32[]{:S(2)}, u32[]{:S(2)}) collective-permute-start(f32[384,256]{1,0:T(8,128)S(1)} %collective-permute-done.refs_1_), channel_id=1, source_target_pairs={{0,1},{1,0},{2,3},{3,2},{4,5},{5,4},{6,7},{7,6},{8,9},{9,8},{10,11... | collective-permute-start | bytes 1179656 | tf_op jit(solution)/shard_map/ppermute | solution.py:47
  34.2 6.7 %collective-permute-start.21 = (f32[256,256]{1,0:T(8,128)S(1)}, f32[256,256]{1,0:T(8,128)S(1)}, u32[]{:S(2)}, u32[]{:S(2)}) collective-permute-start(f32[256,256]{1,0:T(8,128)S(1)} %get-tuple-element.65.refs_0_), channel_id=1, source_target_pairs={{0,1},{1,0},{2,3},{3,2},{4,5},{5,4},{6,7},{7,6},{8,9},{9,8},{10,11... | collective-permute-start | bytes 786440 | tf_op jit(solution)/shard_map/ppermute | solution.py:47
  34.3 6.5 %collective-permute-start.22 = (f32[256,256]{1,0:T(8,128)S(1)}, f32[256,256]{1,0:T(8,128)S(1)}, u32[]{:S(2)}, u32[]{:S(2)}) collective-permute-start(f32[256,256]{1,0:T(8,128)S(1)} %collective-permute-done.18.refs_1_), channel_id=1, source_target_pairs={{0,1},{1,0},{2,3},{3,2},{4,5},{5,4},{6,7},{7,6},{8,9},{9,8},{10,11... | collective-permute-start | bytes 786440 | tf_op jit(solution)/shard_map/ppermute | solution.py:47
  34.7 6.2 %collective-permute-start.23 = (f32[256,256]{1,0:T(8,128)S(1)}, f32[256,256]{1,0:T(8,128)S(1)}, u32[]{:S(2)}, u32[]{:S(2)}) collective-permute-start(f32[256,256]{1,0:T(8,128)S(1)} %collective-permute-done.19.refs_2_), channel_id=1, source_target_pairs={{0,1},{1,0},{2,3},{3,2},{4,5},{5,4},{6,7},{7,6},{8,9},{9,8},{10,11... | collective-permute-start | bytes 786440 | tf_op jit(solution)/shard_map/ppermute | solution.py:47
  34.8 6.0 %collective-permute-start.24 = (f32[256,256]{1,0:T(8,128)S(1)}, f32[256,256]{1,0:T(8,128)S(1)}, u32[]{:S(2)}, u32[]{:S(2)}) collective-permute-start(f32[256,256]{1,0:T(8,128)S(1)} %collective-permute-done.20.refs_3_), channel_id=1, source_target_pairs={{0,1},{1,0},{2,3},{3,2},{4,5},{5,4},{6,7},{7,6},{8,9},{9,8},{10,11... | collective-permute-start | bytes 786440 | tf_op jit(solution)/shard_map/ppermute | solution.py:47
  39.2 6.5 %collective-permute-start.17 = (f32[2,64,256]{2,1,0:T(8,128)S(1)}, f32[2,64,256]{2,1,0:T(8,128)S(1)}, u32[]{:S(2)}, u32[]{:S(2)}) collective-permute-start(f32[2,64,256]{2,1,0:T(8,128)S(1)} %get-tuple-element.64), channel_id=1, source_target_pairs={{0,8},{8,16},{16,24},{24,0},{1,9},{9,17},{17,25},{25,1},{2,10},{10... | collective-permute-start | bytes 393224 | tf_op jit(solution)/shard_map/ppermute | solution.py:673
  45.7 8.0 %collective-permute-start.29 = (f32[3,64,256]{2,1,0:T(8,128)S(1)}, f32[3,64,256]{2,1,0:T(8,128)S(1)}, u32[]{:S(2)}, u32[]{:S(2)}) collective-permute-start(f32[3,64,256]{2,1,0:T(8,128)S(1)} %get-tuple-element.67), channel_id=1, source_target_pairs={{0,24},{8,0},{16,8},{24,16},{1,25},{9,1},{17,9},{25,17},{2,26},{10... | collective-permute-start | bytes 589832 | tf_op jit(solution)/shard_map/ppermute | solution.py:668
  47.4 4.6 %collective-permute-start.25 = (f32[8,256]{1,0:T(8,128)S(1)}, f32[8,256]{1,0:T(8,128)S(1)}, u32[]{:S(2)}, u32[]{:S(2)}) collective-permute-start(f32[8,256]{1,0:T(8,128)S(1)} %get-tuple-element.66), channel_id=1, source_target_pairs={{0,24},{8,0},{16,8},{24,16},{1,25},{9,1},{17,9},{25,17},{2,26},{10... | collective-permute-start | bytes 24584 | tf_op jit(solution)/shard_map/ppermute | solution.py:668
  53.7 9.0 %collective-permute-start.34 = (f32[3,64,256]{2,1,0:T(8,128)S(1)}, f32[3,64,256]{2,1,0:T(8,128)S(1)}, u32[]{:S(2)}, u32[]{:S(2)}) collective-permute-start(f32[3,64,256]{2,1,0:T(8,128)S(1)} %get-tuple-element.70), channel_id=1, source_target_pairs={{0,24},{8,0},{16,8},{24,16},{1,25},{9,1},{17,9},{25,17},{2,26},{10... | collective-permute-start | bytes 589832 | tf_op jit(solution)/shard_map/ppermute | solution.py:668
  56.4 28.6 %collective-permute-start.8 = (f32[192,256]{1,0:T(8,128)S(1)}, f32[192,256]{1,0:T(8,128)S(1)}, u32[]{:S(2)}, u32[]{:S(2)}) collective-permute-start(f32[192,256]{1,0:T(8,128)S(1)} %bitcast.5), channel_id=1, source_target_pairs={{0,1},{1,0},{2,4},{3,5},{4,2},{5,3},{6,7},{7,6},{8,9},{9,8},{10,12... | collective-permute-start | bytes 589832 | tf_op jit(solution)/shard_map/ppermute | solution.py:624
  56.4 4.7 %collective-permute-start.30 = (f32[8,256]{1,0:T(8,128)S(1)}, f32[8,256]{1,0:T(8,128)S(1)}, u32[]{:S(2)}, u32[]{:S(2)}) collective-permute-start(f32[8,256]{1,0:T(8,128)S(1)} %get-tuple-element.69), channel_id=1, source_target_pairs={{0,24},{8,0},{16,8},{24,16},{1,25},{9,1},{17,9},{25,17},{2,26},{10... | collective-permute-start | bytes 24584 | tf_op jit(solution)/shard_map/ppermute | solution.py:668
  62.8 28.4 %collective-permute-start.39 = (f32[3,64,256]{2,1,0:T(8,128)S(1)}, f32[3,64,256]{2,1,0:T(8,128)S(1)}, u32[]{:S(2)}, u32[]{:S(2)}) collective-permute-start(f32[3,64,256]{2,1,0:T(8,128)S(1)} %get-tuple-element.72), channel_id=1, source_target_pairs={{0,24},{8,0},{16,8},{24,16},{1,25},{9,1},{17,9},{25,17},{2,26},{10... | collective-permute-start | bytes 589832 | tf_op jit(solution)/shard_map/ppermute | solution.py:668
  66.2 31.3 %collective-permute-start.7 = (f32[192,256]{1,0:T(8,128)S(1)}, f32[192,256]{1,0:T(8,128)S(1)}, u32[]{:S(2)}, u32[]{:S(2)}) collective-permute-start(f32[192,256]{1,0:T(8,128)S(1)} %bitcast.6), channel_id=1, source_target_pairs={{0,2},{1,3},{2,0},{3,1},{4,6},{5,7},{6,4},{7,5},{8,10},{9,11},{10,... | collective-permute-start | bytes 589832 | tf_op jit(solution)/shard_map/ppermute | solution.py:624
  85.0 12.5 %collective-permute-start.9 = (f32[192,256]{1,0:T(8,128)S(1)}, f32[192,256]{1,0:T(8,128)S(1)}, u32[]{:S(2)}, u32[]{:S(2)}) collective-permute-start(f32[192,256]{1,0:T(8,128)S(1)} %collective-permute-done.8.refs_2_), channel_id=1, source_target_pairs={{0,2},{1,3},{2,0},{3,1},{4,6},{5,7},{6,4},{7,5},{8,10},{9,11},{10,... | collective-permute-start | bytes 589832 | tf_op jit(solution)/shard_map/ppermute | solution.py:624
  90.0 8.2 %collective-permute-start.10 = (f32[192,256]{1,0:T(8,128)S(1)}, f32[192,256]{1,0:T(8,128)S(1)}, u32[]{:S(2)}, u32[]{:S(2)}) collective-permute-start(f32[192,256]{1,0:T(8,128)S(1)} %bitcast.7), channel_id=1, source_target_pairs={{0,1},{1,0},{2,3},{3,2},{4,5},{5,4},{6,7},{7,6},{8,9},{9,8},{10,11... | collective-permute-start | bytes 589832 | tf_op jit(solution)/shard_map/ppermute | solution.py:47
  91.0 7.5 %collective-permute-start.12 = (f32[192,256]{1,0:T(8,128)S(1)}, f32[192,256]{1,0:T(8,128)S(1)}, u32[]{:S(2)}, u32[]{:S(2)}) collective-permute-start(f32[192,256]{1,0:T(8,128)S(1)} %collective-permute-done.8.refs_2_), channel_id=1, source_target_pairs={{0,1},{1,0},{2,3},{3,2},{4,5},{5,4},{6,7},{7,6},{8,9},{9,8},{10,11... | collective-permute-start | bytes 589832 | tf_op jit(solution)/shard_map/ppermute | solution.py:47
  91.3 13.3 %collective-permute-start.42 = (f32[224,256]{1,0:T(8,128)S(1)}, f32[224,256]{1,0:T(8,128)S(1)}, u32[]{:S(2)}, u32[]{:S(2)}) collective-permute-start(f32[224,256]{1,0:T(8,128)S(1)} %get-tuple-element.73), channel_id=1, source_target_pairs={{0,2},{1,3},{2,6},{3,7},{4,0},{5,1},{6,4},{7,5},{8,10},{9,11},{10,... | collective-permute-start | bytes 688136 | tf_op jit(solution)/shard_map/ppermute | solution.py:624
  98.2 10.3 %collective-permute-start.40 = (f32[192,256]{1,0:T(8,128)S(1)}, f32[192,256]{1,0:T(8,128)S(1)}, u32[]{:S(2)}, u32[]{:S(2)}) collective-permute-start(f32[192,256]{1,0:T(8,128)S(1)} %shard_map.117.refs_0_), channel_id=1, source_target_pairs={{0,2},{1,3},{2,0},{3,1},{4,6},{5,7},{6,4},{7,5},{8,10},{9,11},{10,... | collective-permute-start | bytes 589832 | tf_op jit(solution)/shard_map/ppermute | solution.py:624
  98.5 10.0 %collective-permute-start.41 = (f32[192,256]{1,0:T(8,128)S(1)}, f32[192,256]{1,0:T(8,128)S(1)}, u32[]{:S(2)}, u32[]{:S(2)}) collective-permute-start(f32[192,256]{1,0:T(8,128)S(1)} %shard_map.117.refs_0_), channel_id=1, source_target_pairs={{0,1},{1,0},{2,4},{3,5},{4,2},{5,3},{6,7},{7,6},{8,9},{9,8},{10,12... | collective-permute-start | bytes 589832 | tf_op jit(solution)/shard_map/ppermute | solution.py:624
  98.9 10.9 %collective-permute-start.43 = (f32[64,256]{1,0:T(8,128)S(1)}, f32[64,256]{1,0:T(8,128)S(1)}, u32[]{:S(2)}, u32[]{:S(2)}) collective-permute-start(f32[64,256]{1,0:T(8,128)S(1)} %get-tuple-element.75), channel_id=1, source_target_pairs={{0,2},{1,3},{2,0},{3,1},{4,6},{5,7},{6,4},{7,5},{8,10},{9,11},{10,... | collective-permute-start | bytes 196616 | tf_op jit(solution)/shard_map/ppermute | solution.py:624
  104.6 9.3 %collective-permute-start.48 = (f32[224,256]{1,0:T(8,128)S(1)}, f32[224,256]{1,0:T(8,128)S(1)}, u32[]{:S(2)}, u32[]{:S(2)}) collective-permute-start(f32[224,256]{1,0:T(8,128)S(1)} %collective-permute-done.42.refs_3_), channel_id=1, source_target_pairs={{0,1},{1,0},{2,3},{3,2},{4,5},{5,4},{6,7},{7,6},{8,9},{9,8},{10,11... | collective-permute-start | bytes 688136 | tf_op jit(solution)/shard_map/ppermute | solution.py:47
  104.6 9.3 %collective-permute-start.45 = (f32[192,256]{1,0:T(8,128)S(1)}, f32[192,256]{1,0:T(8,128)S(1)}, u32[]{:S(2)}, u32[]{:S(2)}) collective-permute-start(f32[192,256]{1,0:T(8,128)S(1)} %shard_map.117.refs_0_), channel_id=1, source_target_pairs={{0,1},{1,0},{2,3},{3,2},{4,5},{5,4},{6,7},{7,6},{8,9},{9,8},{10,11... | collective-permute-start | bytes 589832 | tf_op jit(solution)/shard_map/ppermute | solution.py:47
  108.5 5.4 %collective-permute-start.46 = (f32[192,256]{1,0:T(8,128)S(1)}, f32[192,256]{1,0:T(8,128)S(1)}, u32[]{:S(2)}, u32[]{:S(2)}) collective-permute-start(f32[192,256]{1,0:T(8,128)S(1)} %collective-permute-done.40.refs_1_), channel_id=1, source_target_pairs={{0,1},{1,0},{2,3},{3,2},{4,5},{5,4},{6,7},{7,6},{8,9},{9,8},{10,11... | collective-permute-start | bytes 589832 | tf_op jit(solution)/shard_map/ppermute | solution.py:47
  108.5 5.4 %collective-permute-start.47 = (f32[192,256]{1,0:T(8,128)S(1)}, f32[192,256]{1,0:T(8,128)S(1)}, u32[]{:S(2)}, u32[]{:S(2)}) collective-permute-start(f32[192,256]{1,0:T(8,128)S(1)} %collective-permute-done.41.refs_2_), channel_id=1, source_target_pairs={{0,1},{1,0},{2,3},{3,2},{4,5},{5,4},{6,7},{7,6},{8,9},{9,8},{10,11... | collective-permute-start | bytes 589832 | tf_op jit(solution)/shard_map/ppermute | solution.py:47
  (25 other events, 138.8 us)

commit v7 on v6

--- a/solution.py
+++ b/solution.py
@@ -272,7 +272,7 @@
 
 CHIPS = 4
 LOW, HIGH_CHIP = 1, 2
-CHUNK = 512
+CHUNK = 1024
 PACK_LIMIT = 61 * 1024 * 1024
 
 
@@ -285,15 +285,14 @@
     sources, outs = refs[:count], refs[count : count + CHIPS + 1]
     buffers, sems = refs[count + CHIPS + 1 : -1], refs[-1]
     copies = [pltpu.make_async_copy(a, b, sems.at[i]) for i, (a, b) in enumerate(zip(sources, buffers))]
-    for copy in copies:
-        copy.start()
-    for copy in copies:
-        copy.wait()
+    for index in (3, 4, 0, 1, 2, 5, 6):
+        copies[index].start()
     keys, values, rates, rows, final, queries, cot = buffers
     packs, ahead = outs[:CHIPS], outs[CHIPS]
     tokens = keys.shape[0]
     depth = rows.shape[1]
-    scaled = -column(rates[...], values.shape[1]) * values[...]
+    for copy in copies[3:5]:
+        copy.wait()
     sides = []
     for side in range(2):
         parts = []
@@ -306,6 +305,9 @@
                         lanes.append(source[m, :, start : start + depth])
             parts.append(jnp.concatenate(lanes, axis=1))
         sides.append(jnp.concatenate(parts))
+    for copy in copies[:3]:
+        copy.wait()
+    scaled = -column(rates[...], values.shape[1]) * values[...]
     for by, pack in enumerate(packs):
         pack[:tokens] = keys[...]
         pack[tokens : 2 * tokens] = scaled
@@ -314,6 +316,8 @@
         if by < 2:
             pack[2 * tokens + 2 * depth : 2 * tokens + 3 * depth] = rows[2]
             pack[2 * tokens + 3 * depth :] = final[2]
+    for copy in copies[5:]:
+        copy.wait()
     ahead[:tokens] = queries[...]
     ahead[tokens:] = cot[...]
 
@@ -635,7 +639,7 @@
 
 def exchanged(array):
     turned = [(2 * a + core, 2 * b + 1 - core) for a, b in enumerate(ACROSS) for core in range(2)]
-    return [array, over_chips(array, ACROSS), lax.ppermute(array, "tok", turned), core_swap(array)]
+    return [array, lax.ppermute(array, "tok", turned), over_chips(array, ACROSS), core_swap(array)]
 
 
 def both_cores(pieces):

time: 116 us -> 114 us (0.983)
  starting transfers between devices: 54.3 us -> 53.1 us
    ppermute x4, waiting for transfers between devices: 1.37 us -> 3.37 us  [exchanged(): lax.ppermute(array, 'tok', turned)]
    ppermute x18, waiting for transfers between devices: 34.4 us -> 32.4 us  [over_chips(): return lax.ppermute(array, 'tok', pairs)]
    ppermute x4, starting transfers between devices: 1.66 us -> 0.21 us  [exchanged(): lax.ppermute(array, 'tok', turned)]
where the time goes in v7:
time: 114 us
  waiting for transfers between devices  55.6 us (49%)
  starting transfers between devices  53.1 us (47%)
  Pallas kernels  4.67 us (4%)
    ppermute x18, starting transfers between devices, over_chips(): return lax.ppermute(array, 'tok', pairs)  36.1 us
    ppermute x18, waiting for transfers between devices, over_chips(): return lax.ppermute(array, 'tok', pairs)  32.4 us
    ppermute x6, starting transfers between devices, to_earlier(): lax.ppermute(array, 'block', [(i, (i - 1) % groups) for i in range(groups)])  10.8 us
    ppermute x6, waiting for transfers between devices, to_earlier(): lax.ppermute(array, 'block', [(i, (i - 1) % groups) for i in range(groups)])  10 us
    ppermute x23, waiting for transfers between devices, core_swap(): return lax.ppermute(array, 'tok', [(j, j ^ 1) for j in range(size)])  5.02 us
    ppermute x1, waiting for transfers between devices, to_later(): lax.ppermute(array, 'block', [(i, (i + 1) % groups) for i in range(groups)])  4.79 us
    pallas_call x10, Pallas kernels, kernel_call(): pl.pallas_call(body, in_specs=[pl.BlockSpec(memory_space=space) for _ in...  4.67 us
    ppermute x23, starting transfers between devices, core_swap(): return lax.ppermute(array, 'tok', [(j, j ^ 1) for j in range(size)])  4.34 us
  transfers between devices with their start and end apart: 52, of which 25 were waited for; matrix products, arithmetic and copies ran while one was open for 0% of the time, Pallas kernels for 1%

profile of v7, /device:TPU:0, one launch (start us, length us, event | category | flops | bytes accessed | tf_op | source)
XLA Modules:
  0.0 114.2 jit_solution(5382037835941564561)
XLA Ops:
  0.6 1.3 %shard_map.110 = (f32[384,256]{1,0:T(8,128)S(1)}, f32[384,256]{1,0:T(8,128)S(1)}, f32[320,256]{1,0:T(8,128)S(1)}, f32[320,256]{1,0:T(8,128)S(1)}, f32[256,256]{1,0:T(8,128)S(1)}) custom-call(f32[128,256]{1,0:T(8,128)} %keys.1, f32[128,256]{1,0:T(8,128)} %values.3, f32[1,128]{1,0:T(1,128)} %bitcast.9, f32[3,32,256]{2,1,0:T(8,128)} %bitcast.12, ...), custom_call_target="tpu_custom_call" | custom-call | tf_op jit(solution)/shard_map/pallas_call | solution.py:238
  1.9 3.1 %collective-permute-start = (f32[384,256]{1,0:T(8,128)S(1)}, f32[384,256]{1,0:T(8,128)S(1)}, u32[]{:S(2)}, u32[]{:S(2)}) collective-permute-start(f32[384,256]{1,0:T(8,128)S(1)} %get-tuple-element.44), channel_id=1, source_target_pairs={{0,2},{1,3},{2,0},{3,1},{4,6},{5,7},{6,4},{7,5},{8,10},{9,11},{10,... | collective-permute-start | bytes 1179656 | tf_op jit(solution)/shard_map/ppermute | solution.py:628
  5.1 3.0 %collective-permute-start.1 = (f32[320,256]{1,0:T(8,128)S(1)}, f32[320,256]{1,0:T(8,128)S(1)}, u32[]{:S(2)}, u32[]{:S(2)}) collective-permute-start(f32[320,256]{1,0:T(8,128)S(1)} %get-tuple-element.45), channel_id=1, source_target_pairs={{0,4},{1,5},{2,0},{3,1},{4,6},{5,7},{6,2},{7,3},{8,12},{9,13},{10,... | collective-permute-start | bytes 983048 | tf_op jit(solution)/shard_map/ppermute | solution.py:628
  8.1 1.6 %collective-permute-start.19 = (f32[256,256]{1,0:T(8,128)S(1)}, f32[256,256]{1,0:T(8,128)S(1)}, u32[]{:S(2)}, u32[]{:S(2)}) collective-permute-start(f32[256,256]{1,0:T(8,128)S(1)} %get-tuple-element.65.refs_0_), channel_id=1, source_target_pairs={{0,4},{1,5},{2,0},{3,1},{4,6},{5,7},{6,2},{7,3},{8,12},{9,13},{10,... | collective-permute-start | bytes 786440 | tf_op jit(solution)/shard_map/ppermute | solution.py:628
  9.7 11.0 %collective-permute-done.18.refs_1_ = f32[256,256]{1,0:T(8,128)S(1)} collective-permute-done((f32[256,256]{1,0:T(8,128)S(1)}, f32[256,256]{1,0:T(8,128)S(1)}, u32[]{:S(2)}, u32[]{:S(2)}) %collective-permute-start.18) | collective-permute-done | bytes 262176 | tf_op jit(solution)/shard_map/ppermute | solution.py:628
  20.6 7.0 %collective-permute-done.1.refs_2_ = f32[320,256]{1,0:T(8,128)S(1)} collective-permute-done((f32[320,256]{1,0:T(8,128)S(1)}, f32[320,256]{1,0:T(8,128)S(1)}, u32[]{:S(2)}, u32[]{:S(2)}) %collective-permute-start.1) | collective-permute-done | bytes 327712 | tf_op jit(solution)/shard_map/ppermute | solution.py:628
  28.2 4.2 %collective-permute-done.19.refs_2_ = f32[256,256]{1,0:T(8,128)S(1)} collective-permute-done((f32[256,256]{1,0:T(8,128)S(1)}, f32[256,256]{1,0:T(8,128)S(1)}, u32[]{:S(2)}, u32[]{:S(2)}) %collective-permute-start.19) | collective-permute-done | bytes 262176 | tf_op jit(solution)/shard_map/ppermute | solution.py:628
  32.4 1.5 %collective-permute-done.20.refs_3_ = f32[256,256]{1,0:T(8,128)S(1)} collective-permute-done((f32[256,256]{1,0:T(8,128)S(1)}, f32[256,256]{1,0:T(8,128)S(1)}, u32[]{:S(2)}, u32[]{:S(2)}) %collective-permute-start.20) | collective-permute-done | bytes 262176 | tf_op jit(solution)/shard_map/ppermute | solution.py:628
  35.2 1.4 %collective-permute-done.14.refs_4_ = f32[8,256]{1,0:T(8,128)S(1)} collective-permute-done((f32[8,256]{1,0:T(8,128)S(1)}, f32[8,256]{1,0:T(8,128)S(1)}, u32[]{:S(2)}, u32[]{:S(2)}) %collective-permute-start.14) | collective-permute-done | bytes 8224 | tf_op jit(solution)/shard_map/ppermute | solution.py:642
  36.8 1.0 collective-permute-done.15.refs_5_
  38.0 1.0 collective-permute-done.16.refs_6_
  39.0 1.7 %collective-permute-start.17 = (f32[2,64,256]{2,1,0:T(8,128)S(1)}, f32[2,64,256]{2,1,0:T(8,128)S(1)}, u32[]{:S(2)}, u32[]{:S(2)}) collective-permute-start(f32[2,64,256]{2,1,0:T(8,128)S(1)} %get-tuple-element.64), channel_id=1, source_target_pairs={{0,8},{8,16},{16,24},{24,0},{1,9},{9,17},{17,25},{25,1},{2,10},{10... | collective-permute-start | bytes 393224 | tf_op jit(solution)/shard_map/ppermute | solution.py:677
  40.7 4.8 %collective-permute-done.17.earlier.refs_18_ = f32[2,64,256]{2,1,0:T(8,128)S(1)} collective-permute-done((f32[2,64,256]{2,1,0:T(8,128)S(1)}, f32[2,64,256]{2,1,0:T(8,128)S(1)}, u32[]{:S(2)}, u32[]{:S(2)}) %collective-permute-start.17) | collective-permute-done | bytes 131104 | tf_op jit(solution)/shard_map/ppermute | solution.py:677
  45.5 1.8 %collective-permute-start.29 = (f32[3,64,256]{2,1,0:T(8,128)S(1)}, f32[3,64,256]{2,1,0:T(8,128)S(1)}, u32[]{:S(2)}, u32[]{:S(2)}) collective-permute-start(f32[3,64,256]{2,1,0:T(8,128)S(1)} %get-tuple-element.67), channel_id=1, source_target_pairs={{0,24},{8,0},{16,8},{24,16},{1,25},{9,1},{17,9},{25,17},{2,26},{10... | collective-permute-start | bytes 589832 | tf_op jit(solution)/shard_map/ppermute | solution.py:672
  47.2 1.4 %collective-permute-start.25 = (f32[8,256]{1,0:T(8,128)S(1)}, f32[8,256]{1,0:T(8,128)S(1)}, u32[]{:S(2)}, u32[]{:S(2)}) collective-permute-start(f32[8,256]{1,0:T(8,128)S(1)} %get-tuple-element.66), channel_id=1, source_target_pairs={{0,24},{8,0},{16,8},{24,16},{1,25},{9,1},{17,9},{25,17},{2,26},{10... | collective-permute-start | bytes 24584 | tf_op jit(solution)/shard_map/ppermute | solution.py:672
  48.7 3.1 %collective-permute-done.25.refs_7_ = f32[8,256]{1,0:T(8,128)S(1)} collective-permute-done((f32[8,256]{1,0:T(8,128)S(1)}, f32[8,256]{1,0:T(8,128)S(1)}, u32[]{:S(2)}, u32[]{:S(2)}) %collective-permute-start.25) | collective-permute-done | bytes 8224 | tf_op jit(solution)/shard_map/ppermute | solution.py:672
  53.5 2.7 %collective-permute-start.34 = (f32[3,64,256]{2,1,0:T(8,128)S(1)}, f32[3,64,256]{2,1,0:T(8,128)S(1)}, u32[]{:S(2)}, u32[]{:S(2)}) collective-permute-start(f32[3,64,256]{2,1,0:T(8,128)S(1)} %get-tuple-element.70), channel_id=1, source_target_pairs={{0,24},{8,0},{16,8},{24,16},{1,25},{9,1},{17,9},{25,17},{2,26},{10... | collective-permute-start | bytes 589832 | tf_op jit(solution)/shard_map/ppermute | solution.py:672
  56.7 4.1 %collective-permute-done.30.refs_7_.refs_11_ = f32[8,256]{1,0:T(8,128)S(1)} collective-permute-done((f32[8,256]{1,0:T(8,128)S(1)}, f32[8,256]{1,0:T(8,128)S(1)}, u32[]{:S(2)}, u32[]{:S(2)}) %collective-permute-start.30) | collective-permute-done | bytes 8224 | tf_op jit(solution)/shard_map/ppermute | solution.py:672
  62.6 3.4 %collective-permute-start.39 = (f32[3,64,256]{2,1,0:T(8,128)S(1)}, f32[3,64,256]{2,1,0:T(8,128)S(1)}, u32[]{:S(2)}, u32[]{:S(2)}) collective-permute-start(f32[3,64,256]{2,1,0:T(8,128)S(1)} %get-tuple-element.72), channel_id=1, source_target_pairs={{0,24},{8,0},{16,8},{24,16},{1,25},{9,1},{17,9},{25,17},{2,26},{10... | collective-permute-start | bytes 589832 | tf_op jit(solution)/shard_map/ppermute | solution.py:672
  66.0 18.9 %collective-permute-start.7 = (f32[192,256]{1,0:T(8,128)S(1)}, f32[192,256]{1,0:T(8,128)S(1)}, u32[]{:S(2)}, u32[]{:S(2)}) collective-permute-start(f32[192,256]{1,0:T(8,128)S(1)} %bitcast.6), channel_id=1, source_target_pairs={{0,2},{1,3},{2,0},{3,1},{4,6},{5,7},{6,4},{7,5},{8,10},{9,11},{10,... | collective-permute-start | bytes 589832 | tf_op jit(solution)/shard_map/ppermute | solution.py:628
  84.9 0.9 collective-permute-start.35
  85.8 2.7 %collective-permute-done.35.refs_15_ = f32[8,256]{1,0:T(8,128)S(1)} collective-permute-done((f32[8,256]{1,0:T(8,128)S(1)}, f32[8,256]{1,0:T(8,128)S(1)}, u32[]{:S(2)}, u32[]{:S(2)}) %collective-permute-start.35) | collective-permute-done | bytes 8224 | tf_op jit(solution)/shard_map/ppermute | solution.py:672
  89.1 0.7 collective-permute-done.36.refs_16_
  91.2 5.3 %collective-permute-start.42 = (f32[224,256]{1,0:T(8,128)S(1)}, f32[224,256]{1,0:T(8,128)S(1)}, u32[]{:S(2)}, u32[]{:S(2)}) collective-permute-start(f32[224,256]{1,0:T(8,128)S(1)} %get-tuple-element.73), channel_id=1, source_target_pairs={{0,2},{1,3},{2,6},{3,7},{4,0},{5,1},{6,4},{7,5},{8,10},{9,11},{10,... | collective-permute-start | bytes 688136 | tf_op jit(solution)/shard_map/ppermute | solution.py:628
  98.0 2.1 %collective-permute-start.43 = (f32[64,256]{1,0:T(8,128)S(1)}, f32[64,256]{1,0:T(8,128)S(1)}, u32[]{:S(2)}, u32[]{:S(2)}) collective-permute-start(f32[64,256]{1,0:T(8,128)S(1)} %get-tuple-element.75), channel_id=1, source_target_pairs={{0,2},{1,3},{2,0},{3,1},{4,6},{5,7},{6,4},{7,5},{8,10},{9,11},{10,... | collective-permute-start | bytes 196616 | tf_op jit(solution)/shard_map/ppermute | solution.py:628
  100.1 3.1 %collective-permute-done.42.refs_3_ = f32[224,256]{1,0:T(8,128)S(1)} collective-permute-done((f32[224,256]{1,0:T(8,128)S(1)}, f32[224,256]{1,0:T(8,128)S(1)}, u32[]{:S(2)}, u32[]{:S(2)}) %collective-permute-start.42) | collective-permute-done | bytes 229408 | tf_op jit(solution)/shard_map/ppermute | solution.py:628
  103.7 3.4 %collective-permute-done.40.refs_1_ = f32[192,256]{1,0:T(8,128)S(1)} collective-permute-done((f32[192,256]{1,0:T(8,128)S(1)}, f32[192,256]{1,0:T(8,128)S(1)}, u32[]{:S(2)}, u32[]{:S(2)}) %collective-permute-start.40) | collective-permute-done | bytes 196640 | tf_op jit(solution)/shard_map/ppermute | solution.py:628
  107.6 0.8 collective-permute-done.43.refs_5_
  108.4 1.2 %collective-permute-done.51.refs_13_ = f32[32,256]{1,0:T(8,128)S(1)} collective-permute-done((f32[32,256]{1,0:T(8,128)S(1)}, f32[32,256]{1,0:T(8,128)S(1)}, u32[]{:S(2)}, u32[]{:S(2)}) %collective-permute-start.51) | collective-permute-done | bytes 32800 | tf_op jit(solution)/shard_map/ppermute | solution.py:47
  109.8 1.1 collective-permute-done.49.refs_11_
  111.1 1.4 %shard_map.112 = (f32[128,256]{1,0:T(8,128)}, f32[5,128,256]{2,1,0:T(8,128)S(1)}, bf16[3,256,256]{2,1,0:T(8,128)(2,1)S(1)}, bf16[3,256,256]{2,1,0:T(8,128)(2,1)S...) custom-call(f32[128,256]{1,0:T(8,128)S(1)} %copy-done.1, ...), custom_call_target="tpu_custom_call" | custom-call | tf_op jit(solution)/shard_map/pallas_call | solution.py:238
  112.5 1.7 %shard_map.119 = (f32[128,256]{1,0:T(8,128)}, f32[128,256]{1,0:T(8,128)}, f32[1,128]{1,0:T(1,128)}, f32[3,32,256]{2,1,0:T(8,128)}) custom-call(f32[128,256]{1,0:T(8,128)S(1)} %copy-done, f32[1,128]{1,0:T(1,128)S(1)} %bitcast.11, f32[5,128,256]{2,1,0:T(8,128)S(1)} %get-tuple-element.49.kept, bf16[3,256,256]{2,1,0:T(8,128)(2,1)S(1)} %get-tuple-element.50.high, ...), custom_call_target="tpu_custom_call" | custom-call | tf_op jit(solution)/shard_map/pallas_call | solution.py:238
  (92 shorter events, 11.0 us)
Async XLA Ops:
  1.9 26.2 %collective-permute-start = (f32[384,256]{1,0:T(8,128)S(1)}, f32[384,256]{1,0:T(8,128)S(1)}, u32[]{:S(2)}, u32[]{:S(2)}) collective-permute-start(f32[384,256]{1,0:T(8,128)S(1)} %get-tuple-element.44), channel_id=1, source_target_pairs={{0,2},{1,3},{2,0},{3,1},{4,6},{5,7},{6,4},{7,5},{8,10},{9,11},{10,... | collective-permute-start | bytes 1179656 | tf_op jit(solution)/shard_map/ppermute | solution.py:628
  5.0 15.6 %collective-permute-start.18 = (f32[256,256]{1,0:T(8,128)S(1)}, f32[256,256]{1,0:T(8,128)S(1)}, u32[]{:S(2)}, u32[]{:S(2)}) collective-permute-start(f32[256,256]{1,0:T(8,128)S(1)} %get-tuple-element.65.refs_0_), channel_id=1, source_target_pairs={{0,2},{1,3},{2,0},{3,1},{4,6},{5,7},{6,4},{7,5},{8,10},{9,11},{10,... | collective-permute-start | bytes 786440 | tf_op jit(solution)/shard_map/ppermute | solution.py:628
  5.1 22.5 %collective-permute-start.1 = (f32[320,256]{1,0:T(8,128)S(1)}, f32[320,256]{1,0:T(8,128)S(1)}, u32[]{:S(2)}, u32[]{:S(2)}) collective-permute-start(f32[320,256]{1,0:T(8,128)S(1)} %get-tuple-element.45), channel_id=1, source_target_pairs={{0,4},{1,5},{2,0},{3,1},{4,6},{5,7},{6,2},{7,3},{8,12},{9,13},{10,... | collective-permute-start | bytes 983048 | tf_op jit(solution)/shard_map/ppermute | solution.py:628
  8.1 19.6 %collective-permute-start.2 = (f32[320,256]{1,0:T(8,128)S(1)}, f32[320,256]{1,0:T(8,128)S(1)}, u32[]{:S(2)}, u32[]{:S(2)}) collective-permute-start(f32[320,256]{1,0:T(8,128)S(1)} %get-tuple-element.46), channel_id=1, source_target_pairs={{0,1},{1,0},{2,4},{3,5},{4,2},{5,3},{6,7},{7,6},{8,9},{9,8},{10,12... | collective-permute-start | bytes 983048 | tf_op jit(solution)/shard_map/ppermute | solution.py:628
  8.1 24.3 %collective-permute-start.19 = (f32[256,256]{1,0:T(8,128)S(1)}, f32[256,256]{1,0:T(8,128)S(1)}, u32[]{:S(2)}, u32[]{:S(2)}) collective-permute-start(f32[256,256]{1,0:T(8,128)S(1)} %get-tuple-element.65.refs_0_), channel_id=1, source_target_pairs={{0,4},{1,5},{2,0},{3,1},{4,6},{5,7},{6,2},{7,3},{8,12},{9,13},{10,... | collective-permute-start | bytes 786440 | tf_op jit(solution)/shard_map/ppermute | solution.py:628
  20.6 13.5 %collective-permute-start.3 = (f32[384,256]{1,0:T(8,128)S(1)}, f32[384,256]{1,0:T(8,128)S(1)}, u32[]{:S(2)}, u32[]{:S(2)}) collective-permute-start(f32[384,256]{1,0:T(8,128)S(1)} %get-tuple-element.43.refs_0_), channel_id=1, source_target_pairs={{0,1},{1,0},{2,3},{3,2},{4,5},{5,4},{6,7},{7,6},{8,9},{9,8},{10,11... | collective-permute-start | bytes 1179656 | tf_op jit(solution)/shard_map/ppermute | solution.py:47
  27.7 6.8 %collective-permute-start.5 = (f32[320,256]{1,0:T(8,128)S(1)}, f32[320,256]{1,0:T(8,128)S(1)}, u32[]{:S(2)}, u32[]{:S(2)}) collective-permute-start(f32[320,256]{1,0:T(8,128)S(1)} %collective-permute-done.1.refs_2_), channel_id=1, source_target_pairs={{0,1},{1,0},{2,3},{3,2},{4,5},{5,4},{6,7},{7,6},{8,9},{9,8},{10,11... | collective-permute-start | bytes 983048 | tf_op jit(solution)/shard_map/ppermute | solution.py:47
  27.7 7.0 %collective-permute-start.6 = (f32[320,256]{1,0:T(8,128)S(1)}, f32[320,256]{1,0:T(8,128)S(1)}, u32[]{:S(2)}, u32[]{:S(2)}) collective-permute-start(f32[320,256]{1,0:T(8,128)S(1)} %collective-permute-done.2.refs_3_), channel_id=1, source_target_pairs={{0,1},{1,0},{2,3},{3,2},{4,5},{5,4},{6,7},{7,6},{8,9},{9,8},{10,11... | collective-permute-start | bytes 983048 | tf_op jit(solution)/shard_map/ppermute | solution.py:47
  28.2 6.8 %collective-permute-start.4 = (f32[384,256]{1,0:T(8,128)S(1)}, f32[384,256]{1,0:T(8,128)S(1)}, u32[]{:S(2)}, u32[]{:S(2)}) collective-permute-start(f32[384,256]{1,0:T(8,128)S(1)} %collective-permute-done.refs_1_), channel_id=1, source_target_pairs={{0,1},{1,0},{2,3},{3,2},{4,5},{5,4},{6,7},{7,6},{8,9},{9,8},{10,11... | collective-permute-start | bytes 1179656 | tf_op jit(solution)/shard_map/ppermute | solution.py:47
  34.0 6.7 %collective-permute-start.21 = (f32[256,256]{1,0:T(8,128)S(1)}, f32[256,256]{1,0:T(8,128)S(1)}, u32[]{:S(2)}, u32[]{:S(2)}) collective-permute-start(f32[256,256]{1,0:T(8,128)S(1)} %get-tuple-element.65.refs_0_), channel_id=1, source_target_pairs={{0,1},{1,0},{2,3},{3,2},{4,5},{5,4},{6,7},{7,6},{8,9},{9,8},{10,11... | collective-permute-start | bytes 786440 | tf_op jit(solution)/shard_map/ppermute | solution.py:47
  34.1 6.5 %collective-permute-start.22 = (f32[256,256]{1,0:T(8,128)S(1)}, f32[256,256]{1,0:T(8,128)S(1)}, u32[]{:S(2)}, u32[]{:S(2)}) collective-permute-start(f32[256,256]{1,0:T(8,128)S(1)} %collective-permute-done.18.refs_1_), channel_id=1, source_target_pairs={{0,1},{1,0},{2,3},{3,2},{4,5},{5,4},{6,7},{7,6},{8,9},{9,8},{10,11... | collective-permute-start | bytes 786440 | tf_op jit(solution)/shard_map/ppermute | solution.py:47
  34.5 6.2 %collective-permute-start.23 = (f32[256,256]{1,0:T(8,128)S(1)}, f32[256,256]{1,0:T(8,128)S(1)}, u32[]{:S(2)}, u32[]{:S(2)}) collective-permute-start(f32[256,256]{1,0:T(8,128)S(1)} %collective-permute-done.19.refs_2_), channel_id=1, source_target_pairs={{0,1},{1,0},{2,3},{3,2},{4,5},{5,4},{6,7},{7,6},{8,9},{9,8},{10,11... | collective-permute-start | bytes 786440 | tf_op jit(solution)/shard_map/ppermute | solution.py:47
  34.6 6.0 %collective-permute-start.24 = (f32[256,256]{1,0:T(8,128)S(1)}, f32[256,256]{1,0:T(8,128)S(1)}, u32[]{:S(2)}, u32[]{:S(2)}) collective-permute-start(f32[256,256]{1,0:T(8,128)S(1)} %collective-permute-done.20.refs_3_), channel_id=1, source_target_pairs={{0,1},{1,0},{2,3},{3,2},{4,5},{5,4},{6,7},{7,6},{8,9},{9,8},{10,11... | collective-permute-start | bytes 786440 | tf_op jit(solution)/shard_map/ppermute | solution.py:47
  39.0 6.5 %collective-permute-start.17 = (f32[2,64,256]{2,1,0:T(8,128)S(1)}, f32[2,64,256]{2,1,0:T(8,128)S(1)}, u32[]{:S(2)}, u32[]{:S(2)}) collective-permute-start(f32[2,64,256]{2,1,0:T(8,128)S(1)} %get-tuple-element.64), channel_id=1, source_target_pairs={{0,8},{8,16},{16,24},{24,0},{1,9},{9,17},{17,25},{25,1},{2,10},{10... | collective-permute-start | bytes 393224 | tf_op jit(solution)/shard_map/ppermute | solution.py:677
  45.5 8.0 %collective-permute-start.29 = (f32[3,64,256]{2,1,0:T(8,128)S(1)}, f32[3,64,256]{2,1,0:T(8,128)S(1)}, u32[]{:S(2)}, u32[]{:S(2)}) collective-permute-start(f32[3,64,256]{2,1,0:T(8,128)S(1)} %get-tuple-element.67), channel_id=1, source_target_pairs={{0,24},{8,0},{16,8},{24,16},{1,25},{9,1},{17,9},{25,17},{2,26},{10... | collective-permute-start | bytes 589832 | tf_op jit(solution)/shard_map/ppermute | solution.py:672
  47.2 4.6 %collective-permute-start.25 = (f32[8,256]{1,0:T(8,128)S(1)}, f32[8,256]{1,0:T(8,128)S(1)}, u32[]{:S(2)}, u32[]{:S(2)}) collective-permute-start(f32[8,256]{1,0:T(8,128)S(1)} %get-tuple-element.66), channel_id=1, source_target_pairs={{0,24},{8,0},{16,8},{24,16},{1,25},{9,1},{17,9},{25,17},{2,26},{10... | collective-permute-start | bytes 24584 | tf_op jit(solution)/shard_map/ppermute | solution.py:672
  53.5 9.0 %collective-permute-start.34 = (f32[3,64,256]{2,1,0:T(8,128)S(1)}, f32[3,64,256]{2,1,0:T(8,128)S(1)}, u32[]{:S(2)}, u32[]{:S(2)}) collective-permute-start(f32[3,64,256]{2,1,0:T(8,128)S(1)} %get-tuple-element.70), channel_id=1, source_target_pairs={{0,24},{8,0},{16,8},{24,16},{1,25},{9,1},{17,9},{25,17},{2,26},{10... | collective-permute-start | bytes 589832 | tf_op jit(solution)/shard_map/ppermute | solution.py:672
  56.2 28.7 %collective-permute-start.8 = (f32[192,256]{1,0:T(8,128)S(1)}, f32[192,256]{1,0:T(8,128)S(1)}, u32[]{:S(2)}, u32[]{:S(2)}) collective-permute-start(f32[192,256]{1,0:T(8,128)S(1)} %bitcast.5), channel_id=1, source_target_pairs={{0,1},{1,0},{2,4},{3,5},{4,2},{5,3},{6,7},{7,6},{8,9},{9,8},{10,12... | collective-permute-start | bytes 589832 | tf_op jit(solution)/shard_map/ppermute | solution.py:628
  56.2 4.7 %collective-permute-start.30 = (f32[8,256]{1,0:T(8,128)S(1)}, f32[8,256]{1,0:T(8,128)S(1)}, u32[]{:S(2)}, u32[]{:S(2)}) collective-permute-start(f32[8,256]{1,0:T(8,128)S(1)} %get-tuple-element.69), channel_id=1, source_target_pairs={{0,24},{8,0},{16,8},{24,16},{1,25},{9,1},{17,9},{25,17},{2,26},{10... | collective-permute-start | bytes 24584 | tf_op jit(solution)/shard_map/ppermute | solution.py:672
  62.6 28.5 %collective-permute-start.39 = (f32[3,64,256]{2,1,0:T(8,128)S(1)}, f32[3,64,256]{2,1,0:T(8,128)S(1)}, u32[]{:S(2)}, u32[]{:S(2)}) collective-permute-start(f32[3,64,256]{2,1,0:T(8,128)S(1)} %get-tuple-element.72), channel_id=1, source_target_pairs={{0,24},{8,0},{16,8},{24,16},{1,25},{9,1},{17,9},{25,17},{2,26},{10... | collective-permute-start | bytes 589832 | tf_op jit(solution)/shard_map/ppermute | solution.py:672
  66.0 30.5 %collective-permute-start.7 = (f32[192,256]{1,0:T(8,128)S(1)}, f32[192,256]{1,0:T(8,128)S(1)}, u32[]{:S(2)}, u32[]{:S(2)}) collective-permute-start(f32[192,256]{1,0:T(8,128)S(1)} %bitcast.6), channel_id=1, source_target_pairs={{0,2},{1,3},{2,0},{3,1},{4,6},{5,7},{6,4},{7,5},{8,10},{9,11},{10,... | collective-permute-start | bytes 589832 | tf_op jit(solution)/shard_map/ppermute | solution.py:628
  84.9 11.7 %collective-permute-start.9 = (f32[192,256]{1,0:T(8,128)S(1)}, f32[192,256]{1,0:T(8,128)S(1)}, u32[]{:S(2)}, u32[]{:S(2)}) collective-permute-start(f32[192,256]{1,0:T(8,128)S(1)} %collective-permute-done.8.refs_2_), channel_id=1, source_target_pairs={{0,2},{1,3},{2,0},{3,1},{4,6},{5,7},{6,4},{7,5},{8,10},{9,11},{10,... | collective-permute-start | bytes 589832 | tf_op jit(solution)/shard_map/ppermute | solution.py:628
  89.9 7.3 %collective-permute-start.10 = (f32[192,256]{1,0:T(8,128)S(1)}, f32[192,256]{1,0:T(8,128)S(1)}, u32[]{:S(2)}, u32[]{:S(2)}) collective-permute-start(f32[192,256]{1,0:T(8,128)S(1)} %bitcast.7), channel_id=1, source_target_pairs={{0,1},{1,0},{2,3},{3,2},{4,5},{5,4},{6,7},{7,6},{8,9},{9,8},{10,11... | collective-permute-start | bytes 589832 | tf_op jit(solution)/shard_map/ppermute | solution.py:47
  90.9 6.6 %collective-permute-start.12 = (f32[192,256]{1,0:T(8,128)S(1)}, f32[192,256]{1,0:T(8,128)S(1)}, u32[]{:S(2)}, u32[]{:S(2)}) collective-permute-start(f32[192,256]{1,0:T(8,128)S(1)} %collective-permute-done.8.refs_2_), channel_id=1, source_target_pairs={{0,1},{1,0},{2,3},{3,2},{4,5},{5,4},{6,7},{7,6},{8,9},{9,8},{10,11... | collective-permute-start | bytes 589832 | tf_op jit(solution)/shard_map/ppermute | solution.py:47
  91.2 12.0 %collective-permute-start.42 = (f32[224,256]{1,0:T(8,128)S(1)}, f32[224,256]{1,0:T(8,128)S(1)}, u32[]{:S(2)}, u32[]{:S(2)}) collective-permute-start(f32[224,256]{1,0:T(8,128)S(1)} %get-tuple-element.73), channel_id=1, source_target_pairs={{0,2},{1,3},{2,6},{3,7},{4,0},{5,1},{6,4},{7,5},{8,10},{9,11},{10,... | collective-permute-start | bytes 688136 | tf_op jit(solution)/shard_map/ppermute | solution.py:628
  97.2 9.8 %collective-permute-start.40 = (f32[192,256]{1,0:T(8,128)S(1)}, f32[192,256]{1,0:T(8,128)S(1)}, u32[]{:S(2)}, u32[]{:S(2)}) collective-permute-start(f32[192,256]{1,0:T(8,128)S(1)} %shard_map.117.refs_0_), channel_id=1, source_target_pairs={{0,2},{1,3},{2,0},{3,1},{4,6},{5,7},{6,4},{7,5},{8,10},{9,11},{10,... | collective-permute-start | bytes 589832 | tf_op jit(solution)/shard_map/ppermute | solution.py:628
  97.5 9.6 %collective-permute-start.41 = (f32[192,256]{1,0:T(8,128)S(1)}, f32[192,256]{1,0:T(8,128)S(1)}, u32[]{:S(2)}, u32[]{:S(2)}) collective-permute-start(f32[192,256]{1,0:T(8,128)S(1)} %shard_map.117.refs_0_), channel_id=1, source_target_pairs={{0,1},{1,0},{2,4},{3,5},{4,2},{5,3},{6,7},{7,6},{8,9},{9,8},{10,12... | collective-permute-start | bytes 589832 | tf_op jit(solution)/shard_map/ppermute | solution.py:628
  98.0 10.5 %collective-permute-start.43 = (f32[64,256]{1,0:T(8,128)S(1)}, f32[64,256]{1,0:T(8,128)S(1)}, u32[]{:S(2)}, u32[]{:S(2)}) collective-permute-start(f32[64,256]{1,0:T(8,128)S(1)} %get-tuple-element.75), channel_id=1, source_target_pairs={{0,2},{1,3},{2,0},{3,1},{4,6},{5,7},{6,4},{7,5},{8,10},{9,11},{10,... | collective-permute-start | bytes 196616 | tf_op jit(solution)/shard_map/ppermute | solution.py:628
  103.2 9.3 %collective-permute-start.48 = (f32[224,256]{1,0:T(8,128)S(1)}, f32[224,256]{1,0:T(8,128)S(1)}, u32[]{:S(2)}, u32[]{:S(2)}) collective-permute-start(f32[224,256]{1,0:T(8,128)S(1)} %collective-permute-done.42.refs_3_), channel_id=1, source_target_pairs={{0,1},{1,0},{2,3},{3,2},{4,5},{5,4},{6,7},{7,6},{8,9},{9,8},{10,11... | collective-permute-start | bytes 688136 | tf_op jit(solution)/shard_map/ppermute | solution.py:47
  103.2 9.3 %collective-permute-start.45 = (f32[192,256]{1,0:T(8,128)S(1)}, f32[192,256]{1,0:T(8,128)S(1)}, u32[]{:S(2)}, u32[]{:S(2)}) collective-permute-start(f32[192,256]{1,0:T(8,128)S(1)} %shard_map.117.refs_0_), channel_id=1, source_target_pairs={{0,1},{1,0},{2,3},{3,2},{4,5},{5,4},{6,7},{7,6},{8,9},{9,8},{10,11... | collective-permute-start | bytes 589832 | tf_op jit(solution)/shard_map/ppermute | solution.py:47
  107.1 5.4 %collective-permute-start.46 = (f32[192,256]{1,0:T(8,128)S(1)}, f32[192,256]{1,0:T(8,128)S(1)}, u32[]{:S(2)}, u32[]{:S(2)}) collective-permute-start(f32[192,256]{1,0:T(8,128)S(1)} %collective-permute-done.40.refs_1_), channel_id=1, source_target_pairs={{0,1},{1,0},{2,3},{3,2},{4,5},{5,4},{6,7},{7,6},{8,9},{9,8},{10,11... | collective-permute-start | bytes 589832 | tf_op jit(solution)/shard_map/ppermute | solution.py:47
  107.1 5.4 %collective-permute-start.47 = (f32[192,256]{1,0:T(8,128)S(1)}, f32[192,256]{1,0:T(8,128)S(1)}, u32[]{:S(2)}, u32[]{:S(2)}) collective-permute-start(f32[192,256]{1,0:T(8,128)S(1)} %collective-permute-done.41.refs_2_), channel_id=1, source_target_pairs={{0,1},{1,0},{2,3},{3,2},{4,5},{5,4},{6,7},{7,6},{8,9},{9,8},{10,11... | collective-permute-start | bytes 589832 | tf_op jit(solution)/shard_map/ppermute | solution.py:47
  (25 other events, 131.8 us)
